TPU v7x, 512 devices: a whole 4x4x16 slice. The times are simulated.
512 devices in a mesh: row: 32 (over y_hi, z), col: 16 (over y_lo, x, core).
Axes of the slice: x: 4, y: 4 (y_hi: 2, y_lo: 2; y = y_hi * 2 + y_lo), z: 16, core: 2. Of those that a mesh axis runs over, the one named last changes fastest.
Arguments:
- diag_block: float32 [512, 512], replicated, as said below
- panel: float32 [32768, 512], P('row', 'col'), may hold values from -2 to 2
- tiles: float32 [14336, 128, 128], P(('row', 'col')), may hold values from -6 to 6
- targets: int32 [14336, 2], P(('row', 'col')), may hold values from 0 to 255, as said below
Outputs:
- panel_factor: float32 [32768, 512], P('row', 'col')
- schur_tiles: float32 [14336, 128, 128], P(('row', 'col'))
Inputs may be any that keep to these rules, and one draw needn't show every extreme that they name: `diag_block`: symmetric positive definite. `targets`: slot s belongs to the device d = s // 28 at grid row d // 16 and grid column d % 16; its p satisfies p // 8 == d // 16 and its q satisfies (q // 8) % 16 == d % 16.
All inputs are finite; a program needn't handle non-finite values.
Results may differ from a plain program's by a relative error of at most 0.0003.
Values sent between devices are 32-bit elements; how exact they have to be, the bound alone decides.
No kernel may reach another device: no remote copies, remote signals or barrier semaphores. Data moves between devices by JAX's collectives and lax.ppermute only.
A program may use at most 128 MiB of HBM per device.

v0:
```python
import jax
import jax.numpy as jnp
from jax import lax
from jax.sharding import PartitionSpec as P


def from_root(value, axis, source):
    kept = jnp.where(lax.axis_index(axis) == source, value, 0).astype(value.dtype)
    return lax.psum(kept, axis)


def solve_rows(diag_factor, right_rows):
    return jax.scipy.linalg.solve_triangular(diag_factor, right_rows.T, lower=True).T


def on_device(diag_block, panel, tiles, targets):
    n_rows = lax.axis_size("row")
    n_cols = lax.axis_size("col")
    grid_col = lax.axis_index("col")
    width = diag_block.shape[0]
    local_rows = panel.shape[0]
    tile_rows = tiles.shape[1]
    local_blocks = local_rows // tile_rows
    groups = n_rows // n_cols
    diag_factor = jnp.linalg.cholesky(diag_block)
    whole = lax.all_gather(panel, "col", axis=1, tiled=True)
    factor = solve_rows(diag_factor, whole)
    panel_factor = lax.dynamic_slice_in_dim(
        factor, grid_col * (width // n_cols), width // n_cols, 1
    )
    received = []
    for group in range(groups):
        received.append(from_root(factor, "row", grid_col + group * n_cols))
    remote = jnp.stack(received)
    remote_blocks = remote.reshape(groups * local_blocks, tile_rows, width)
    own_blocks = factor.reshape(local_blocks, tile_rows, width)
    row_block = targets[:, 0]
    col_block = targets[:, 1]
    left = jnp.take(own_blocks, row_block % local_blocks, axis=0)
    remote_index = col_block // local_blocks // n_cols * local_blocks + col_block % local_blocks
    right = jnp.take(remote_blocks, remote_index, axis=0)
    update = jnp.einsum("skw,slw->skl", left, right, precision=lax.Precision.HIGHEST)
    keep = row_block >= col_block
    schur_tiles = tiles - jnp.where(keep[:, None, None], update, jnp.zeros_like(update))
    return (panel_factor, schur_tiles)


def solution(mesh):
    placed = (P(), P("row", "col"), P(("row", "col"), None, None), P(("row", "col"), None))
    return jax.shard_map(
        on_device,
        mesh=mesh,
        in_specs=placed,
        out_specs=(P("row", "col"), P(("row", "col"), None, None)),
        check_vma=False,
    )
```

profile of v0, /device:TPU:6, one launch (start us, length us, event | category | flops | bytes accessed | tf_op | source)
XLA Modules:
  0.0 509.1 jit_solution(1837923428524671871)
XLA Ops:
  7.2 0.7 all-gather.2.cloned.1.call-update
  8.0 1.6 copy.7
  9.8 11.7 %cholesky.104 = f32[128,128]{1,0:T(8,128)S(1)} custom-call(f32[128,128]{1,0:T(8,128)S(1)} %cholesky.266), custom_call_target="Cholesky" | custom-call | tf_op jit(solution)/shard_map/jit(cholesky)/cholesky | solution.py:25
  21.6 9.8 %custom-call.31 = f32[1,128,128]{1,2,0:T(8,128)S(1)} custom-call(f32[1,128,128]{2,1,0:T(8,128)S(1)} %get-tuple-element.39), custom_call_target="InvertDiagBlocksLowerTriangular" | custom-call | tf_op jit(solution)/shard_map/jit(cholesky)/cholesky | solution.py:25
  32.2 11.7 %cholesky.217 = f32[128,128]{1,0:T(8,128)S(1)} custom-call(f32[128,128]{1,0:T(8,128)S(1)} %cholesky.270), custom_call_target="Cholesky" | custom-call | tf_op jit(solution)/shard_map/jit(cholesky)/cholesky | solution.py:25
  43.9 10.0 %custom-call.32 = f32[1,128,128]{1,2,0:T(8,128)S(1)} custom-call(f32[1,128,128]{2,1,0:T(8,128)S(1)} %get-tuple-element.36), custom_call_target="InvertDiagBlocksLowerTriangular" | custom-call | tf_op jit(solution)/shard_map/jit(cholesky)/cholesky | solution.py:25
  54.5 11.7 %cholesky.238 = f32[128,128]{1,0:T(8,128)S(1)} custom-call(f32[128,128]{1,0:T(8,128)S(1)} %cholesky.275), custom_call_target="Cholesky" | custom-call | tf_op jit(solution)/shard_map/jit(cholesky)/cholesky | solution.py:25
  66.3 9.8 %custom-call.33 = f32[1,128,128]{1,2,0:T(8,128)S(1)} custom-call(f32[1,128,128]{2,1,0:T(8,128)S(1)} %get-tuple-element.33), custom_call_target="InvertDiagBlocksLowerTriangular" | custom-call | tf_op jit(solution)/shard_map/jit(cholesky)/cholesky | solution.py:25
  76.7 11.7 %cholesky.255 = f32[128,128]{1,0:T(8,128)S(1)} custom-call(f32[128,128]{1,0:T(8,128)S(1)} %convolution_subtract_fusion.4), custom_call_target="Cholesky" | custom-call | tf_op jit(solution)/shard_map/jit(cholesky)/cholesky | solution.py:25
  88.4 0.7 compare_reduce_fusion.2
  91.7 0.6 compare_reduce_fusion
  93.3 7.9 %while.1 = (s32[]{:T(128)}, f32[512,512]{1,0:T(8,128)S(1)}, s32[4,2]{0,1:T(2,128)S(1)}, f32[4,128,128]{2,1,0:T(8,128)S(1)}, s32[]{:T(128)}) while((s32[]{:T(128)}, f32[512,512]{1,0:T(8,128)S(1)}, s32[4,2]{0,1:T(2,128)S(1)}, f32[4,128,128]{2,1,0:T(8,128)S(1)}, s32[]{:T(128)}) %tuple.39), condition=%wide.while_cond, body=%wide.while_body.sunk | while | flops 2 | bytes 131189 | solution.py:13
  93.9 1.4 bitcast_dynamic-update-slice_fusion.2
  95.9 1.4 bitcast_dynamic-update-slice_fusion.2
  97.9 1.4 bitcast_dynamic-update-slice_fusion.2
  99.9 1.4 bitcast_dynamic-update-slice_fusion.2
  101.2 39.3 %custom-call.34 = f32[4,128,128]{1,2,0:T(8,128)S(1)} custom-call(f32[4,128,128]{2,1,0:T(8,128)S(1)} %get-tuple-element.9), custom_call_target="InvertDiagBlocksLowerTriangular" | custom-call | tf_op jit(solution)/shard_map/jit(_solve_triangular)/triangular_solve | solution.py:13
  140.6 1.8 fusion.23
  142.4 1.6 convolution_subtract_fusion.1
  144.7 0.7 convolution_subtract_fusion
  146.1 1.1 fusion.16
  147.8 2.6 select_bitcast_fusion.1
  150.4 0.7 copy-done.3
  151.2 2.6 fusion.47
  153.8 1.9 copy.10
  155.7 4.0 gather_fusion
  159.7 1.6 dynamic-slice_bitcast_fusion
  161.2 310.0 %all-reduce.4.cloned.1.call-done = (f32[1,1024,512]{1,2,0:T(8,128)}, f32[1,1024,512]{1,2,0:T(8,128)}) async-done(((f32[1,1024,512]{1,2,0:T(8,128)}, f32[1,1024,512]{1,2,0:T(8,128)}), (f32[1,1024,512]{1,2,0:T(8,128)}, f32[1,1024,512]{1,2,0:T(8,128)})) %all-reduce.4.cloned.1.call-update) | async-done | bytes 4194320 | tf_op jit(solution)/shard_map/psum | solution.py:9
  471.2 4.9 pad_maximum_fusion
  476.1 5.6 %copy.9 = f32[2,1024,512]{2,1,0:T(8,128)} copy(f32[2,1024,512]{1,2,0:T(8,128)} %pad_maximum_fusion) | data formatting | bytes 8388608 | tf_op jit(solution)/shard_map/stack | solution.py:34
  481.8 6.4 %gather_fusion.1 = f32[28,128,512]{2,1,0:T(8,128)} fusion(f32[16,128,512]{2,1,0:T(8,128)} %bitcast.70, s32[1024]{0:T(1024)S(1)} %pad_clamp_fusion), kind=kCustom, calls=%fused_computation.1 | custom fusion | bytes 14680176 | tf_op jit(solution)/shard_map/jit(_take)/gather | solution.py:41
  488.1 13.7 %select_subtract_fusion = f32[28,128,128]{2,1,0:T(8,128)} fusion(f32[28,128,128]{2,1,0:T(8,128)S(1)} %copy-done.2, f32[28,128,512]{2,1,0:T(8,128)} %gather_fusion.1, pred[28]{0:T(512)(128)(4,1)S(1)} %get-tuple-element.42, f32[28,128,512]{2,1,0:T(8,128)} %gather_fusion, pred[28]{0:T(512)(128)(4,1)S(1)} %get-tuple-element.20, ...), kind=kOutput, calls=%fused_computation.14 | convolution fusion | flops 2823159808 | bytes 18350164 | tf_op jit(solution)/shard_map/skw,slw->skl/dot_general | solution.py:42
  (45 shorter events, 7.8 us)
Async XLA Ops:
  7.2 2.4 copy-start
  7.2 133.4 %all-gather.2.cloned.1.call-start = ((), (), s32[]{:S(2)}) async-start(), calls=%async_computation | async-start | bytes 2228224 | tf_op jit(solution)/shard_map/all_gather | solution.py:26
  7.9 463.3 %all-reduce.4.cloned.1.call-start = ((), (), s32[]{:S(2)}) async-start(), calls=%async_computation.1 | async-start | bytes 8388608 | tf_op jit(solution)/shard_map/psum | solution.py:9
  140.6 4.1 copy-start.1
  150.4 0.7 copy-start.3
  481.8 6.4 %copy-start.2 = (f32[28,128,128]{2,1,0:T(8,128)S(1)}, f32[28,128,128]{2,1,0:T(8,128)}, u32[]{:S(2)}) copy-start(f32[28,128,128]{2,1,0:T(8,128)} %param.6) | copy-start | bytes 5505028
Sparse Core Ops, SparseCore 0:
  10.1 45.1 all-gather.1
  150.6 320.6 all-reduce.3
where the time goes:
time: 518 us; the launch traced here: 509 us
  waiting for transfers between devices  311 us (60%)
  other arithmetic  129 us (25%)
  local copies, waits for them, and re-layouts  29.7 us (6%)
  matrix products  22.7 us (4%)
  between operations  17.4 us (3%)
    psum x1, waiting for transfers between devices, from_root(): return lax.psum(kept, axis)  310 us
    another operation x14, other arithmetic, on_device(): diag_factor = jnp.linalg.cholesky(diag_block)  78.5 us
    another operation x3, other arithmetic, solve_rows(): jax.scipy.linalg.solve_triangular(diag_factor, right_rows.T, lower=True)  39.7 us
    dot_general x1, matrix products, on_device(): jnp.einsum('skw,slw->skl', left, right, precision=lax.Precision.HIGHEST)  13.7 us
  transfers between devices with their start and end apart: 2, of which 1 were waited for; matrix products, arithmetic and copies ran while one was open for 27% of the time, Pallas kernels for 0%

commit v1 on v0

v1 whole, which is shorter than its diff:
```python
import jax
import jax.numpy as jnp
from jax import lax
from jax.experimental import pallas as pl
from jax.experimental.pallas import tpu as pltpu
from jax.sharding import PartitionSpec as P

W, B, G = 512, 128, 8
HI = lax.Precision.HIGHEST

def splat(col, k):
    return jnp.broadcast_to(col[k:k + 1, :], (G, B))

def factor_block(groups):
    n = len(groups)
    lane = lax.broadcasted_iota(jnp.int32, (G, B), 1)
    sub = lax.broadcasted_iota(jnp.int32, (G, B), 0)
    out = []
    for g in range(n):
        base = g * G
        rows = groups[g]
        cols = [jnp.broadcast_to(rows[:, base + m:base + m + 1], (G, B)) for m in range(G)]
        a = {(k, m): splat(cols[m], k) for m in range(G) for k in range(m, G)}
        inv = {}
        low = {}
        for m in range(G):
            r = lax.rsqrt(a[m, m])
            inv[m, m] = r
            for k in range(m + 1, G):
                low[k, m] = a[k, m] * r
            for j in range(m + 1, G):
                for k in range(j, G):
                    a[k, j] = a[k, j] - low[k, m] * low[j, m]
            for j in range(m):
                total = low[m, j] * inv[j, j]
                for k in range(j + 1, m):
                    total = total + low[m, k] * inv[k, j]
                inv[m, j] = -total * r
        inside = (lane >= base) & (lane < base + G)
        unit = jnp.where(lane - base == sub, 1.0, 0.0).astype(jnp.float32)
        rows = jnp.where(inside, unit, rows)
        spread = [splat(rows, m) for m in range(G)]
        done = None
        for m in range(G):
            column = inv[m, m]
            for k in range(m + 1, G):
                column = jnp.where(sub == k, inv[k, m], column)
            column = jnp.where(sub < m, 0.0, column)
            term = column * spread[m]
            done = term if done is None else done + term
        out.append(jnp.where(lane < base + G, done, 0.0))
        if g + 1 == n:
            break
        spread_done = [splat(done, m) for m in range(G)]
        solved = []
        for j in range(G):
            total = None
            for m in range(j, G):
                term = inv[m, j] * spread_done[m]
                total = term if total is None else total + term
            solved.append(total)
        for h in range(g + 1, n):
            old = groups[h]
            new = jnp.where(inside, 0.0, old)
            for m in range(G):
                c = jnp.broadcast_to(old[:, base + m:base + m + 1], (G, B))
                new = new - c * solved[m]
            groups[h] = new
    return out

def chol_inverse_kernel(a_ref, o_ref, t_ref, d_ref):
    t_ref[...] = a_ref[...]
    row = lax.broadcasted_iota(jnp.int32, (W, B), 0)
    eye = jnp.where(lax.broadcasted_iota(jnp.int32, (B, B), 0) == lax.broadcasted_iota(jnp.int32, (B, B), 1), 1.0, 0.0).astype(jnp.float32)
    lane_w = lax.broadcasted_iota(jnp.int32, (B, W), 1)

    def step(b, carry):
        here = pl.ds(pl.multiple_of(b * B, B), B)
        panel = t_ref[:, here]
        block = t_ref[here, here]
        groups = [block[g * G:(g + 1) * G, :] for g in range(B // G)]
        inv = factor_block(groups)
        for g in range(B // G):
            d_ref[g * G:(g + 1) * G, :] = inv[g]
        inverse = d_ref[...]
        t_ref[here, here] = eye
        done = jnp.dot(inverse, t_ref[here, :], precision=HI, preferred_element_type=jnp.float32)
        coef = lax.dot_general(panel, inverse, (((1,), (1,)), ((), ())), precision=HI, preferred_element_type=jnp.float32)
        coef = jnp.where(row >= (b + 1) * B, coef, 0.0)
        t_ref[:, here] = jnp.where(row >= b * B, 0.0, panel)
        t_ref[...] = t_ref[...] - jnp.dot(coef, done, precision=HI, preferred_element_type=jnp.float32)
        t_ref[here, :] = jnp.where(lane_w < (b + 1) * B, done, 0.0)
        return carry

    lax.fori_loop(0, W // B, step, 0)
    o_ref[...] = t_ref[...]

def chol_inverse(a):
    return pl.pallas_call(
        chol_inverse_kernel,
        out_shape=jax.ShapeDtypeStruct((W, W), jnp.float32),
        in_specs=[pl.BlockSpec(memory_space=pltpu.VMEM)],
        out_specs=pl.BlockSpec(memory_space=pltpu.VMEM),
        scratch_shapes=[pltpu.VMEM((W, W), jnp.float32), pltpu.VMEM((B, B), jnp.float32)],
        name="factor_inverse",
    )(a)


BF, F32 = jnp.bfloat16, jnp.float32


def halves(value):
    high = value.astype(BF)
    return high, (value - high.astype(F32)).astype(BF)


def product(left_high, left_low, right_high, right_low):
    return (
        jnp.dot(left_high, right_high, preferred_element_type=F32)
        + jnp.dot(left_high, right_low, preferred_element_type=F32)
        + jnp.dot(left_low, right_high, preferred_element_type=F32)
    )


def split_factor(inverse_ref, high_ref, low_ref):
    high, low = halves(inverse_ref[...])
    high_ref[...] = high
    low_ref[...] = low


def own_kernel(inverse_ref, panel_ref, left_ref, slice_ref, lh, ll, ph, pq, xt):
    split_factor(inverse_ref, lh, ll)
    high, low = halves(panel_ref[...])
    ph[...] = high
    pq[...] = low
    rows = panel_ref.shape[1]
    for top in range(0, W, 2 * B):
        depth = top + 2 * B
        for first in range(0, rows, 2 * B):
            cut = slice(first, first + 2 * B)
            xt[top:depth, cut] = product(
                lh[top:depth, :depth], ll[top:depth, :depth], ph[:depth, cut], pq[:depth, cut]
            )
    mine = slice_ref.shape[0]
    start = pl.multiple_of(lax.axis_index("col") * mine, mine)
    slice_ref[...] = xt[pl.ds(start, mine), :]
    for block in range(rows // B):
        for part in range(W // B):
            turned = xt[part * B:(part + 1) * B, block * B:(block + 1) * B].T
            high, low = halves(turned)
            left_ref[block, :B, part * B:(part + 1) * B] = high
            left_ref[block, B:, part * B:(part + 1) * B] = low


def tile_step(targets_ref, left_ref, right, tiles_ref, out_ref, side, blocks, groups):
    def one(slot, carry):
        p = targets_ref[0, slot]
        q = targets_ref[1, slot]
        group = lax.rem(lax.div(lax.div(q, blocks), lax.axis_size("col")), groups)
        which = jnp.where(group == side, 0, 1) * blocks + lax.rem(q, blocks)
        four = jnp.dot(left_ref[lax.rem(p, blocks)], right[which], preferred_element_type=F32)
        update = four[:B, :B] + (four[:B, B:] + four[B:, :B])
        tile = tiles_ref[slot]
        out_ref[slot] = jnp.where(p >= q, tile - update, tile)
        return carry

    lax.fori_loop(0, out_ref.shape[0], one, 0)


def tiles_kernel(targets_ref, inverse_ref, left_ref, far_ref, tiles_ref, out_ref, lh, ll, ph, pq, right):
    split_factor(inverse_ref, lh, ll)
    blocks = left_ref.shape[0]
    size = far_ref.shape[2]
    side = lax.div(lax.axis_index("row"), lax.axis_size("col"))
    for slot in range(2):
        for k in range(W // size):
            high, low = halves(far_ref[k, slot])
            ph[k * size:(k + 1) * size, :] = high
            pq[k * size:(k + 1) * size, :] = low

        def columns(step, carry):
            cut = pl.ds(pl.multiple_of(step * 2 * B, 2 * B), 2 * B)
            for top in range(0, W, 2 * B):
                depth = top + 2 * B
                both = product(lh[top:depth, :depth], ll[top:depth, :depth], ph[:depth, cut], pq[:depth, cut])
                high, low = halves(both)
                for part in range(2):
                    at = slot * blocks + step * 2 + part
                    right[at, top:depth, :B] = high[:, part * B:(part + 1) * B]
                    right[at, top:depth, B:] = low[:, part * B:(part + 1) * B]
            return carry

        lax.fori_loop(0, blocks // 2, columns, 0)
    tile_step(targets_ref, left_ref, right, tiles_ref, out_ref, side, blocks, 2)


def vmem(count):
    return [pl.BlockSpec(memory_space=pltpu.VMEM)] * count


def on_device(diag_block, panel, tiles, targets):
    n_rows, n_cols = lax.axis_size("row"), lax.axis_size("col")
    size, rows = panel.shape[1], panel.shape[0]
    blocks = rows // B
    mine = panel.T
    own = lax.all_gather(mine, "col", axis=0, tiled=True)
    at = lambda r, c: r * n_cols + c
    first, second = [], []
    for r in range(n_rows):
        for c in range(n_cols):
            if r < n_cols:
                first.append((at(r, c), at(c, r)))
                second.append((at(r, c), at(c + n_cols, r)))
            else:
                first.append((at(r, c), at(c + n_cols, r - n_cols)))
    near = lax.ppermute(mine, ("row", "col"), first)
    other = lax.ppermute(mine, ("row", "col"), second)
    lines = [[side * n_cols + z for z in range(n_cols)] for side in range(n_rows // n_cols)]
    far = lax.all_gather(jnp.stack([near, other]), "row", axis=0, axis_index_groups=lines)
    inverse = chol_inverse(diag_block)
    factor = [pltpu.VMEM((W, W), BF)] * 2
    piece = [pltpu.VMEM((W, rows), BF)] * 2
    left, panel_slice = pl.pallas_call(
        own_kernel,
        out_shape=(
            jax.ShapeDtypeStruct((blocks, 2 * B, W), BF),
            jax.ShapeDtypeStruct((size, rows), F32),
        ),
        in_specs=vmem(2),
        out_specs=tuple(vmem(2)),
        scratch_shapes=[*factor, *piece, pltpu.VMEM((W, rows), F32)],
        name="own_rows",
    )(inverse, own)
    schur = pl.pallas_call(
        tiles_kernel,
        out_shape=jax.ShapeDtypeStruct(tiles.shape, F32),
        in_specs=[pl.BlockSpec(memory_space=pltpu.SMEM), *vmem(4)],
        out_specs=vmem(1)[0],
        scratch_shapes=[*factor, *piece, pltpu.VMEM((2 * blocks, W, 2 * B), BF)],
        name="schur_tiles",
    )(targets.T, inverse, left, far, tiles)
    return panel_slice.T, schur


def solution(mesh):
    placed = (P(), P("row", "col"), P(("row", "col"), None, None), P(("row", "col"), None))
    return jax.shard_map(
        on_device,
        mesh=mesh,
        in_specs=placed,
        out_specs=(P("row", "col"), P(("row", "col"), None, None)),
        check_vma=False,
    )
```

time: 518 us -> 171 us (0.33); the launches traced: 509 us -> 171 us
  waiting for transfers between devices: 311 us -> 89.1 us
  other arithmetic: 129 us -> 0.72 us
  Pallas kernels: 0 us -> 50.7 us
  local copies, waits for them, and re-layouts: 29.7 us -> 0 us
  matrix products: 22.7 us -> 0 us
  starting transfers between devices: 0.08 us -> 16.4 us
    psum x1 -> x0, waiting for transfers between devices: 310 us -> none  [from_root(): return lax.psum(kept, axis)]
    another operation x19 -> x1, other arithmetic: 126 us -> 0.72 us  [on_device(): jnp.stack([near, other])]
    all_gather x1 -> x2, waiting for transfers between devices: 0.02 us -> 69.6 us  [the longest x1 69.6 us: on_device(): lax.all_gather(jnp.stack([near, other]), 'row', axis=0, axis_index_groups...]
    pallas_call x0 -> x3, Pallas kernels: none -> 50.7 us  [the longest x1 29.5 us: chol_inverse(): pl.pallas_call(chol_inverse_kernel, out_shape=jax.ShapeDtypeStruct((W, W)...]
    ppermute x0 -> x2, waiting for transfers between devices: none -> 18.8 us  [the longest x1 14.5 us: on_device(): near = lax.ppermute(mine, ('row', 'col'), first)]
    ppermute x0 -> x2, starting transfers between devices: none -> 16.3 us  [the longest x1 14.4 us: on_device(): other = lax.ppermute(mine, ('row', 'col'), second)]
    dot_general x1 -> x0, matrix products: 13.7 us -> none  [on_device(): jnp.einsum('skw,slw->skl', left, right, precision=lax.Precision.HIGHEST)]
    another operation x18 -> x0, local copies, waits for them, and re-layouts: 13.6 us -> none
  transfers between devices with their start and end apart: 2 -> 4, of which waited for: 1 -> 3; matrix products, arithmetic and copies ran while one was open for 27% -> 0% of each run, Pallas kernels for 0% -> 20%
where the time goes in v1:
time: 171 us
  waiting for transfers between devices  89.1 us (52%)
  Pallas kernels  50.7 us (30%)
  starting transfers between devices  16.4 us (10%)
  between operations  14.1 us (8%)
    all_gather x1, waiting for transfers between devices, on_device(): lax.all_gather(jnp.stack([near, other]), 'row', axis=0, axis_index_groups...  69.6 us
    pallas_call x1, Pallas kernels, chol_inverse(): pl.pallas_call(chol_inverse_kernel, out_shape=jax.ShapeDtypeStruct((W, W)...  29.5 us
    pallas_call x1, Pallas kernels, on_device(): pl.pallas_call(tiles_kernel, out_shape=jax.ShapeDtypeStruct(tiles.shape,...  16.3 us
    ppermute x1, waiting for transfers between devices, on_device(): near = lax.ppermute(mine, ('row', 'col'), first)  14.5 us
    ppermute x1, starting transfers between devices, on_device(): other = lax.ppermute(mine, ('row', 'col'), second)  14.4 us
    pallas_call x1, Pallas kernels, on_device(): pl.pallas_call(own_kernel, out_shape=(jax.ShapeDtypeStruct((blocks, 2 * B...  4.89 us
    ppermute x1, waiting for transfers between devices, on_device(): other = lax.ppermute(mine, ('row', 'col'), second)  4.3 us
  transfers between devices with their start and end apart: 4, of which 3 were waited for; matrix products, arithmetic and copies ran while one was open for 0% of the time, Pallas kernels for 20%

profile of v1, /device:TPU:6, one launch (start us, length us, event | category | flops | bytes accessed | tf_op | source)
XLA Modules:
  0.0 171.0 jit_solution(15983775804961246831)
XLA Ops:
  7.2 0.0 all-gather.4.cloned.1.call-start
  7.2 0.7 all-gather.4.cloned.1.call-update
  7.9 0.0 all-gather.6.cloned.1.call-start
  7.9 14.4 %collective-permute-start.1 = (f32[32,1024]{1,0:T(8,128)}, f32[32,1024]{1,0:T(8,128)S(1)}, u32[]{:S(2)}, u32[]{:S(2)}) collective-permute-start(f32[32,1024]{1,0:T(8,128)} %bitcast.8), channel_id=1, source_target_pairs={{0,256},{1,272},{2,288},{3,304},{4,320},{5,336},{6,352},{7,368},{8... | collective-permute-start | bytes 393224 | tf_op jit(solution)/shard_map/ppermute | solution.py:217
  22.3 1.9 %collective-permute-start = (f32[32,1024]{1,0:T(8,128)}, f32[32,1024]{1,0:T(8,128)S(1)}, u32[]{:S(2)}, u32[]{:S(2)}) collective-permute-start(f32[32,1024]{1,0:T(8,128)} %bitcast.9), channel_id=1, source_target_pairs={{0,0},{1,16},{2,32},{3,48},{4,64},{5,80},{6,96},{7,112},{8,128},{9... | collective-permute-start | bytes 393224 | tf_op jit(solution)/shard_map/ppermute | solution.py:216
  24.2 4.3 %collective-permute-done.1 = f32[32,1024]{1,0:T(8,128)S(1)} collective-permute-done((f32[32,1024]{1,0:T(8,128)}, f32[32,1024]{1,0:T(8,128)S(1)}, u32[]{:S(2)}, u32[]{:S(2)}) %collective-permute-start.1) | collective-permute-done | bytes 131104 | tf_op jit(solution)/shard_map/ppermute | solution.py:217
  28.6 14.5 %collective-permute-done = f32[32,1024]{1,0:T(8,128)S(1)} collective-permute-done((f32[32,1024]{1,0:T(8,128)}, f32[32,1024]{1,0:T(8,128)S(1)}, u32[]{:S(2)}, u32[]{:S(2)}) %collective-permute-start) | collective-permute-done | bytes 131104 | tf_op jit(solution)/shard_map/ppermute | solution.py:216
  43.0 0.7 pad_maximum_fusion
  43.7 0.0 all-gather.6.cloned.1.call-update
  43.8 29.5 %factor_inverse.1.inverse_ref = f32[512,512]{1,0:T(8,128)} custom-call(f32[512,512]{1,0:T(8,128)} %a_ref.1), custom_call_target="tpu_custom_call" | custom-call | tf_op jit(solution)/shard_map/factor_inverse/pallas_call | solution.py:99
  73.3 0.0 all-gather.4.cloned.1.call-done.panel_ref
  73.3 4.9 %own_rows.1 = (bf16[8,256,512]{2,1,0:T(8,128)(2,1)}, f32[32,1024]{1,0:T(8,128)}) custom-call(f32[512,512]{1,0:T(8,128)} %factor_inverse.1.inverse_ref, f32[512,1024]{1,0:T(8,128)} %all-gather.4.cloned.1.call-done.panel_ref), custom_call_target="tpu_custom_call" | custom-call | tf_op jit(solution)/shard_map/own_rows/pallas_call | solution.py:223
  78.2 69.6 %all-gather.6.cloned.1.call-done = f32[32,32,1024]{2,1,0:T(8,128)} async-done(((f32[2,32,1024]{2,1,0:T(8,128)}), f32[32,32,1024]{2,1,0:T(8,128)}) %all-gather.6.cloned.1.call-update) | async-done | bytes 4194320 | tf_op jit(solution)/shard_map/all_gather | solution.py:219
  147.8 16.3 %schur_tiles.1 = f32[28,128,128]{2,1,0:T(8,128)} custom-call(s32[2,28]{1,0:T(2,128)} %bitcast.12, f32[512,512]{1,0:T(8,128)} %factor_inverse.1.inverse_ref, bf16[8,256,512]{2,1,0:T(8,128)(2,1)} %get-tuple-element.5.left_ref, f32[16,2,32,1024]{3,2,1,0:T(8,128)} %bitcast.6, f32[28,128,128]{2,1,0:T(8,128)} %tiles_ref.1), custom_call_target="tpu_custom_call" | custom-call | tf_op jit(solution)/shard_map/schur_tiles/pallas_call | solution.py:234
Async XLA Ops:
  7.2 66.1 %all-gather.4.cloned.1.call-start = ((), (), s32[]{:S(2)}) async-start(), calls=%async_computation | async-start | bytes 2228224 | tf_op jit(solution)/shard_map/all_gather | solution.py:206
  7.9 139.9 %all-gather.6.cloned.1.call-start = ((), (), s32[]{:S(2)}) async-start(), calls=%async_computation.1 | async-start | bytes 4456448 | tf_op jit(solution)/shard_map/all_gather | solution.py:219
  7.9 20.6 %collective-permute-start.1 = (f32[32,1024]{1,0:T(8,128)}, f32[32,1024]{1,0:T(8,128)S(1)}, u32[]{:S(2)}, u32[]{:S(2)}) collective-permute-start(f32[32,1024]{1,0:T(8,128)} %bitcast.8), channel_id=1, source_target_pairs={{0,256},{1,272},{2,288},{3,304},{4,320},{5,336},{6,352},{7,368},{8... | collective-permute-start | bytes 393224 | tf_op jit(solution)/shard_map/ppermute | solution.py:217
  22.3 20.7 %collective-permute-start = (f32[32,1024]{1,0:T(8,128)}, f32[32,1024]{1,0:T(8,128)S(1)}, u32[]{:S(2)}, u32[]{:S(2)}) collective-permute-start(f32[32,1024]{1,0:T(8,128)} %bitcast.9), channel_id=1, source_target_pairs={{0,0},{1,16},{2,32},{3,48},{4,64},{5,80},{6,96},{7,112},{8,128},{9... | collective-permute-start | bytes 393224 | tf_op jit(solution)/shard_map/ppermute | solution.py:216
Sparse Core Ops, SparseCore 0:
  10.1 52.6 all-gather.3
  65.5 82.2 all-gather.5

commit v2 on v1

--- a/solution.py
+++ b/solution.py
@@ -5,7 +5,7 @@
 from jax.experimental.pallas import tpu as pltpu
 from jax.sharding import PartitionSpec as P
 
-W, B, G = 512, 128, 8
+W, B, G, UNROLL = 512, 128, 8, 4
 HI = lax.Precision.HIGHEST
 
 def splat(col, k):
@@ -128,11 +128,17 @@
     low_ref[...] = low
 
 
-def own_kernel(inverse_ref, panel_ref, left_ref, slice_ref, lh, ll, ph, pq, xt):
+def own_kernel(inverse_ref, panel_ref, partner_ref, left_ref, slice_ref, lh, ll, ph, pq, xh, xl, xt):
     split_factor(inverse_ref, lh, ll)
-    high, low = halves(panel_ref[...])
-    ph[...] = high
-    pq[...] = low
+    size = slice_ref.shape[0]
+    col = lax.axis_index("col")
+    for j, flip in enumerate(gathered_order(W // size)):
+        to = pl.ds(pl.multiple_of(jnp.bitwise_xor(col, flip) * size, size), size)
+        at = j * size % (W // 2)
+        source = panel_ref if j * size < W // 2 else partner_ref
+        high, low = halves(source[at:at + size, :])
+        ph[to, :] = high
+        pq[to, :] = low
     rows = panel_ref.shape[1]
     for top in range(0, W, 2 * B):
         depth = top + 2 * B
@@ -141,104 +147,141 @@
             xt[top:depth, cut] = product(
                 lh[top:depth, :depth], ll[top:depth, :depth], ph[:depth, cut], pq[:depth, cut]
             )
-    mine = slice_ref.shape[0]
-    start = pl.multiple_of(lax.axis_index("col") * mine, mine)
-    slice_ref[...] = xt[pl.ds(start, mine), :]
-    for block in range(rows // B):
-        for part in range(W // B):
-            turned = xt[part * B:(part + 1) * B, block * B:(block + 1) * B].T
-            high, low = halves(turned)
-            left_ref[block, :B, part * B:(part + 1) * B] = high
-            left_ref[block, B:, part * B:(part + 1) * B] = low
-
-
-def tile_step(targets_ref, left_ref, right, tiles_ref, out_ref, side, blocks, groups):
+    slice_ref[...] = xt[pl.ds(pl.multiple_of(col * size, size), size), :]
+    for first in range(0, rows, B):
+        for part in range(0, W, B):
+            high, low = halves(xt[part:part + B, first:first + B].T)
+            xh[first:first + B, part:part + B] = high
+            xl[first:first + B, part:part + B] = low
+    for first in range(0, rows, 2 * B):
+        cut = slice(first, first + 2 * B)
+        for top in range(0, W, 2 * B):
+            across = slice(top, top + 2 * B)
+            high, low = halves(product(xh[cut, top:], xl[cut, top:], lh[top:, across], ll[top:, across]))
+            for part in range(2):
+                left_ref[first // B + part, :B, across] = high[part * B:(part + 1) * B]
+                left_ref[first // B + part, B:, across] = low[part * B:(part + 1) * B]
+
+
+def tiles_kernel(targets_ref, left_hbm, far_hbm, tiles_hbm, out_hbm, left, far, tiles, out, right, in_sem, far_sem, out_sem):
+    blocks, size, planes = left.shape[0], far.shape[2], far.shape[0]
+    count = out.shape[0]
+    col, row = lax.axis_index("col"), lax.axis_index("row")
+    n_cols = lax.axis_size("col")
+    side = lax.div(row, n_cols)
+    far_copies = [pltpu.make_async_copy(far_hbm.at[z], far.at[z], far_sem.at[z]) for z in range(planes)]
+    left_copy = pltpu.make_async_copy(left_hbm, left, in_sem.at[0])
+    tiles_copy = pltpu.make_async_copy(tiles_hbm, tiles, in_sem.at[1])
+    for copy in far_copies:
+        copy.start()
+    left_copy.start()
+    tiles_copy.start()
+    for z in range(planes):
+        far_copies[z].wait()
+        apart = lax.rem(z - col + n_cols, n_cols)
+        k = jnp.where(apart < planes // 2, 2 * apart, 2 * planes - 1 - 2 * apart)
+        to = pl.ds(pl.multiple_of(k * size, size), size)
+        for slot in range(2):
+            high, low = halves(far[z, slot])
+            for block in range(blocks):
+                right[slot * blocks + block, to, :B] = high[:, block * B:(block + 1) * B]
+                right[slot * blocks + block, to, B:] = low[:, block * B:(block + 1) * B]
+    left_copy.wait()
+    tiles_copy.wait()
+
     def one(slot, carry):
         p = targets_ref[0, slot]
         q = targets_ref[1, slot]
-        group = lax.rem(lax.div(lax.div(q, blocks), lax.axis_size("col")), groups)
+        group = lax.rem(lax.div(lax.div(q, blocks), n_cols), 2)
         which = jnp.where(group == side, 0, 1) * blocks + lax.rem(q, blocks)
-        four = jnp.dot(left_ref[lax.rem(p, blocks)], right[which], preferred_element_type=F32)
+        four = jnp.dot(left[lax.rem(p, blocks)], right[which], preferred_element_type=F32)
         update = four[:B, :B] + (four[:B, B:] + four[B:, :B])
-        tile = tiles_ref[slot]
-        out_ref[slot] = jnp.where(p >= q, tile - update, tile)
+        tile = tiles[slot]
+        out[slot] = jnp.where(p >= q, tile - update, tile)
+        pltpu.make_async_copy(out.at[slot], out_hbm.at[slot], out_sem.at[slot]).start()
         return carry
 
-    lax.fori_loop(0, out_ref.shape[0], one, 0)
-
-
-def tiles_kernel(targets_ref, inverse_ref, left_ref, far_ref, tiles_ref, out_ref, lh, ll, ph, pq, right):
-    split_factor(inverse_ref, lh, ll)
-    blocks = left_ref.shape[0]
-    size = far_ref.shape[2]
-    side = lax.div(lax.axis_index("row"), lax.axis_size("col"))
-    for slot in range(2):
-        for k in range(W // size):
-            high, low = halves(far_ref[k, slot])
-            ph[k * size:(k + 1) * size, :] = high
-            pq[k * size:(k + 1) * size, :] = low
-
-        def columns(step, carry):
-            cut = pl.ds(pl.multiple_of(step * 2 * B, 2 * B), 2 * B)
-            for top in range(0, W, 2 * B):
-                depth = top + 2 * B
-                both = product(lh[top:depth, :depth], ll[top:depth, :depth], ph[:depth, cut], pq[:depth, cut])
-                high, low = halves(both)
-                for part in range(2):
-                    at = slot * blocks + step * 2 + part
-                    right[at, top:depth, :B] = high[:, part * B:(part + 1) * B]
-                    right[at, top:depth, B:] = low[:, part * B:(part + 1) * B]
-            return carry
-
-        lax.fori_loop(0, blocks // 2, columns, 0)
-    tile_step(targets_ref, left_ref, right, tiles_ref, out_ref, side, blocks, 2)
+    lax.fori_loop(0, count, one, 0, unroll=UNROLL)
+
+    def drain(slot, carry):
+        pltpu.make_async_copy(out.at[slot], out_hbm.at[slot], out_sem.at[slot]).wait()
+        return carry
+
+    lax.fori_loop(0, count, drain, 0)
 
 
 def vmem(count):
     return [pl.BlockSpec(memory_space=pltpu.VMEM)] * count
+
+
+def gathered_order(n_cols):
+    order = [0]
+    for flip in (n_cols // 4, n_cols // 8, n_cols // 2, 1):
+        order += [entry ^ flip for entry in order]
+    return order
 
 
 def on_device(diag_block, panel, tiles, targets):
     n_rows, n_cols = lax.axis_size("row"), lax.axis_size("col")
     size, rows = panel.shape[1], panel.shape[0]
-    blocks = rows // B
+    blocks, count = rows // B, tiles.shape[0]
     mine = panel.T
-    own = lax.all_gather(mine, "col", axis=0, tiled=True)
-    at = lambda r, c: r * n_cols + c
-    first, second = [], []
-    for r in range(n_rows):
-        for c in range(n_cols):
-            if r < n_cols:
-                first.append((at(r, c), at(c, r)))
-                second.append((at(r, c), at(c + n_cols, r)))
-            else:
-                first.append((at(r, c), at(c + n_cols, r - n_cols)))
-    near = lax.ppermute(mine, ("row", "col"), first)
-    other = lax.ppermute(mine, ("row", "col"), second)
-    lines = [[side * n_cols + z for z in range(n_cols)] for side in range(n_rows // n_cols)]
+
+    def at(r, c):
+        return r * n_cols + c
+
+    def shifted(r, c):
+        step = c // 2 if c % 2 == 0 else n_cols - 1 - c // 2
+        return r // n_cols * n_cols + (r + step) % n_cols
+
+    turn = [(at(r, c), at(shifted(r, c), r % n_cols)) for r in range(n_rows) for c in range(n_cols)]
+    lift = [(at(r, c), at(r + n_cols, c)) for r in range(n_cols) for c in range(n_cols)]
+    near = lax.ppermute(mine, ("row", "col"), turn)
+    other = lax.ppermute(near, ("row", "col"), lift)
+    lines = [[part * n_cols + z for z in range(n_cols)] for part in range(n_rows // n_cols)]
     far = lax.all_gather(jnp.stack([near, other]), "row", axis=0, axis_index_groups=lines)
-    inverse = chol_inverse(diag_block)
-    factor = [pltpu.VMEM((W, W), BF)] * 2
-    piece = [pltpu.VMEM((W, rows), BF)] * 2
+
+    own, diag, _ = lax.optimization_barrier((mine, diag_block, other))
+    for flip in (n_cols // 4, n_cols // 8, n_cols // 2, 1):
+        pairs = [(c, c ^ flip) for c in range(n_cols)]
+        received = lax.ppermute(own, "col", pairs)
+        if flip != 1:
+            own = jnp.concatenate([own, received])
+    inverse = chol_inverse(diag)
+    any_space = pl.BlockSpec(memory_space=pl.ANY)
     left, panel_slice = pl.pallas_call(
         own_kernel,
         out_shape=(
             jax.ShapeDtypeStruct((blocks, 2 * B, W), BF),
             jax.ShapeDtypeStruct((size, rows), F32),
         ),
-        in_specs=vmem(2),
+        in_specs=vmem(3),
         out_specs=tuple(vmem(2)),
-        scratch_shapes=[*factor, *piece, pltpu.VMEM((W, rows), F32)],
+        scratch_shapes=[
+            *[pltpu.VMEM((W, W), BF)] * 2,
+            *[pltpu.VMEM((W, rows), BF)] * 2,
+            *[pltpu.VMEM((rows, W), BF)] * 2,
+            pltpu.VMEM((W, rows), F32),
+        ],
         name="own_rows",
-    )(inverse, own)
+    )(inverse, own, received)
     schur = pl.pallas_call(
         tiles_kernel,
         out_shape=jax.ShapeDtypeStruct(tiles.shape, F32),
-        in_specs=[pl.BlockSpec(memory_space=pltpu.SMEM), *vmem(4)],
-        out_specs=vmem(1)[0],
-        scratch_shapes=[*factor, *piece, pltpu.VMEM((2 * blocks, W, 2 * B), BF)],
+        in_specs=[pl.BlockSpec(memory_space=pltpu.SMEM), *[any_space] * 3],
+        out_specs=any_space,
+        scratch_shapes=[
+            pltpu.VMEM(left.shape, BF),
+            pltpu.VMEM(far.shape, F32),
+            pltpu.VMEM(tiles.shape, F32),
+            pltpu.VMEM(tiles.shape, F32),
+            pltpu.VMEM((2 * blocks, W, 2 * B), BF),
+            pltpu.SemaphoreType.DMA((2,)),
+            pltpu.SemaphoreType.DMA((far.shape[0],)),
+            pltpu.SemaphoreType.DMA((count,)),
+        ],
         name="schur_tiles",
-    )(targets.T, inverse, left, far, tiles)
+    )(targets.T, left, far, tiles)
     return panel_slice.T, schur
 
 

time: 171 us -> 144 us (0.84)
  waiting for transfers between devices: 89.1 us -> 58.8 us
  Pallas kernels: 50.7 us -> 43.9 us
  starting transfers between devices: 16.4 us -> 22.7 us
  other arithmetic: 0.72 us -> 2.62 us
    all_gather x1, waiting for transfers between devices: 69.6 us -> 18.5 us  [on_device(): lax.all_gather(jnp.stack([near, other]), 'row', axis=0, axis_index_groups...]
    ppermute x2 -> x6, waiting for transfers between devices: 18.8 us -> 40.3 us  [the longest x4 27.7 us: on_device(): received = lax.ppermute(own, 'col', pairs)]
    pallas_call x1, Pallas kernels: 16.3 us -> 8.35 us  [on_device(): pl.pallas_call(tiles_kernel, out_shape=jax.ShapeDtypeStruct(tiles.shape,...]
    ppermute x2 -> x6, starting transfers between devices: 16.3 us -> 22.6 us  [the longest x4 11.4 us: on_device(): received = lax.ppermute(own, 'col', pairs)]
    concatenate x0 -> x2, other arithmetic: none -> 1.87 us  [on_device(): own = jnp.concatenate([own, received])]
  transfers between devices with their start and end apart: 4 -> 7, of which waited for: 3 -> 6; matrix products, arithmetic and copies ran while one was open for 0% -> 1% of each run, Pallas kernels for 20% -> 25%
where the time goes in v2:
time: 144 us; the launch traced here: 143 us
  waiting for transfers between devices  58.8 us (41%)
  Pallas kernels  43.9 us (30%)
  starting transfers between devices  22.7 us (16%)
  between operations  14.2 us (10%)
  other arithmetic  2.62 us (2%)
    pallas_call x1, Pallas kernels, chol_inverse(): pl.pallas_call(chol_inverse_kernel, out_shape=jax.ShapeDtypeStruct((W, W)...  29.4 us
    ppermute x4, waiting for transfers between devices, on_device(): received = lax.ppermute(own, 'col', pairs)  27.7 us
    all_gather x1, waiting for transfers between devices, on_device(): lax.all_gather(jnp.stack([near, other]), 'row', axis=0, axis_index_groups...  18.5 us
    ppermute x4, starting transfers between devices, on_device(): received = lax.ppermute(own, 'col', pairs)  11.4 us
    ppermute x1, waiting for transfers between devices, on_device(): near = lax.ppermute(mine, ('row', 'col'), turn)  10.1 us
    pallas_call x1, Pallas kernels, on_device(): pl.pallas_call(tiles_kernel, out_shape=jax.ShapeDtypeStruct(tiles.shape,...  8.35 us
    ppermute x1, starting transfers between devices, on_device(): near = lax.ppermute(mine, ('row', 'col'), turn)  6.45 us
    pallas_call x1, Pallas kernels, on_device(): pl.pallas_call(own_kernel, out_shape=(jax.ShapeDtypeStruct((blocks, 2 * B...  6.12 us
  transfers between devices with their start and end apart: 7, of which 6 were waited for; matrix products, arithmetic and copies ran while one was open for 1% of the time, Pallas kernels for 25%

profile of v2, /device:TPU:6, one launch (start us, length us, event | category | flops | bytes accessed | tf_op | source)
XLA Modules:
  0.0 143.3 jit_solution(12792471522059454896)
XLA Ops:
  7.2 0.0 copy-start.1
  7.2 0.0 all-gather.3.cloned.1.call-start
  7.2 6.5 %collective-permute-start = (f32[32,1024]{1,0:T(8,128)}, f32[32,1024]{1,0:T(8,128)S(1)}, u32[]{:S(2)}, u32[]{:S(2)}) collective-permute-start(f32[32,1024]{1,0:T(8,128)} %bitcast.7), channel_id=1, source_target_pairs={{0,0},{1,240},{2,16},{3,224},{4,32},{5,208},{6,48},{7,192},{8,64},... | collective-permute-start | bytes 393224 | tf_op jit(solution)/shard_map/ppermute | solution.py:239
  13.7 10.1 %collective-permute-done = f32[32,1024]{1,0:T(8,128)S(1)} collective-permute-done((f32[32,1024]{1,0:T(8,128)}, f32[32,1024]{1,0:T(8,128)S(1)}, u32[]{:S(2)}, u32[]{:S(2)}) %collective-permute-start) | collective-permute-done | bytes 131104 | tf_op jit(solution)/shard_map/ppermute | solution.py:239
  23.8 4.8 %collective-permute-start.1 = (f32[32,1024]{1,0:T(8,128)S(1)}, f32[32,1024]{1,0:T(8,128)S(1)}, u32[]{:S(2)}, u32[]{:S(2)}) collective-permute-start(f32[32,1024]{1,0:T(8,128)S(1)} %collective-permute-done), channel_id=1, source_target_pairs={{0,256},{1,257},{2,258},{3,259},{4,260},{5,261},{6,262},{7,263},{8... | collective-permute-start | bytes 393224 | tf_op jit(solution)/shard_map/ppermute | solution.py:240
  28.6 2.5 %collective-permute-done.1 = f32[32,1024]{1,0:T(8,128)S(1)} collective-permute-done((f32[32,1024]{1,0:T(8,128)S(1)}, f32[32,1024]{1,0:T(8,128)S(1)}, u32[]{:S(2)}, u32[]{:S(2)}) %collective-permute-start.1) | collective-permute-done | bytes 131104 | tf_op jit(solution)/shard_map/ppermute | solution.py:240
  31.1 0.7 pad_maximum_fusion.2
  31.9 0.0 all-gather.3.cloned.1.call-update
  31.9 1.9 %collective-permute-start.2 = (f32[32,1024]{1,0:T(8,128)}, f32[32,1024]{1,0:T(8,128)S(1)}, u32[]{:S(2)}, u32[]{:S(2)}) collective-permute-start(f32[32,1024]{1,0:T(8,128)} %bitcast.8), channel_id=1, source_target_pairs={{0,4},{1,5},{2,6},{3,7},{4,0},{5,1},{6,2},{7,3},{8,12},{9,13},{10,... | collective-permute-start | bytes 393224 | tf_op jit(solution)/shard_map/ppermute | solution.py:247
  33.8 7.0 %collective-permute-done.2 = f32[32,1024]{1,0:T(8,128)S(1)} collective-permute-done((f32[32,1024]{1,0:T(8,128)}, f32[32,1024]{1,0:T(8,128)S(1)}, u32[]{:S(2)}, u32[]{:S(2)}) %collective-permute-start.2) | collective-permute-done | bytes 131104 | tf_op jit(solution)/shard_map/ppermute | solution.py:247
  40.9 0.9 pad_maximum_fusion.1
  41.8 1.9 %collective-permute-start.3 = (f32[64,1024]{1,0:T(8,128)S(1)}, f32[64,1024]{1,0:T(8,128)S(1)}, u32[]{:S(2)}, u32[]{:S(2)}) collective-permute-start(f32[64,1024]{1,0:T(8,128)S(1)} %pad_maximum_fusion.1), channel_id=1, source_target_pairs={{0,2},{1,3},{2,0},{3,1},{4,6},{5,7},{6,4},{7,5},{8,10},{9,11},{10,... | collective-permute-start | bytes 786440 | tf_op jit(solution)/shard_map/ppermute | solution.py:247
  43.7 9.0 %collective-permute-done.3 = f32[64,1024]{1,0:T(8,128)S(1)} collective-permute-done((f32[64,1024]{1,0:T(8,128)S(1)}, f32[64,1024]{1,0:T(8,128)S(1)}, u32[]{:S(2)}, u32[]{:S(2)}) %collective-permute-start.3) | collective-permute-done | bytes 262176 | tf_op jit(solution)/shard_map/ppermute | solution.py:247
  52.7 0.9 pad_maximum_fusion
  53.7 4.4 %collective-permute-start.4 = (f32[128,1024]{1,0:T(8,128)S(1)}, f32[128,1024]{1,0:T(8,128)S(1)}, u32[]{:S(2)}, u32[]{:S(2)}) collective-permute-start(f32[128,1024]{1,0:T(8,128)S(1)} %pad_maximum_fusion), channel_id=1, source_target_pairs={{0,8},{1,9},{2,10},{3,11},{4,12},{5,13},{6,14},{7,15},{8,0},{9,1},... | collective-permute-start | bytes 1572872 | tf_op jit(solution)/shard_map/ppermute | solution.py:247
  58.1 0.0 copy-done.1
  58.2 11.7 %collective-permute-done.4 = f32[128,1024]{1,0:T(8,128)S(1)} collective-permute-done((f32[128,1024]{1,0:T(8,128)S(1)}, f32[128,1024]{1,0:T(8,128)S(1)}, u32[]{:S(2)}, u32[]{:S(2)}) %collective-permute-start.4) | collective-permute-done | bytes 524320 | tf_op jit(solution)/shard_map/ppermute | solution.py:247
  69.9 0.0 copy-start
  69.9 3.2 %collective-permute-start.5 = (f32[256,1024]{1,0:T(8,128)S(1)}, f32[256,1024]{1,0:T(8,128)S(1)}, u32[]{:S(2)}, u32[]{:S(2)}) collective-permute-start(f32[256,1024]{1,0:T(8,128)S(1)} %constant_dynamic-update-slice_fusion.panel_ref), channel_id=1, source_target_pairs={{0,1},{1,0},{2,3},{3,2},{4,5},{5,4},{6,7},{7,6},{8,9},{9,8},{10,11... | collective-permute-start | bytes 3145736 | tf_op jit(solution)/shard_map/ppermute | solution.py:247
  73.0 29.4 %factor_inverse.1.inverse_ref = f32[512,512]{1,0:T(8,128)} custom-call(f32[512,512]{1,0:T(8,128)} %a_ref), custom_call_target="tpu_custom_call" | custom-call | tf_op jit(solution)/shard_map/factor_inverse/pallas_call | solution.py:99
  102.5 0.0 collective-permute-done.5.partner_ref
  102.5 0.0 copy-done
  102.5 0.0 copy-start.2
  102.5 1.0 copy-done.2
  103.5 6.1 %own_rows.1 = (bf16[8,256,512]{2,1,0:T(8,128)(2,1)}, f32[32,1024]{1,0:T(8,128)}) custom-call(f32[512,512]{1,0:T(8,128)} %factor_inverse.1.inverse_ref, f32[256,1024]{1,0:T(8,128)} %copy-done, f32[256,1024]{1,0:T(8,128)} %copy-done.2), custom_call_target="tpu_custom_call" | custom-call | tf_op jit(solution)/shard_map/own_rows/pallas_call | solution.py:252
  109.6 18.5 %all-gather.3.cloned.1.call-done = f32[32,32,1024]{2,1,0:T(8,128)} async-done(((f32[2,32,1024]{2,1,0:T(8,128)}), f32[32,32,1024]{2,1,0:T(8,128)}) %all-gather.3.cloned.1.call-update) | async-done | bytes 4194320 | tf_op jit(solution)/shard_map/all_gather | solution.py:242
  128.1 8.4 %schur_tiles.1 = f32[28,128,128]{2,1,0:T(8,128)} custom-call(s32[2,28]{1,0:T(2,128)} %bitcast.14, bf16[8,256,512]{2,1,0:T(8,128)(2,1)} %get-tuple-element.9.left_hbm, f32[16,2,32,1024]{3,2,1,0:T(8,128)} %bitcast.6, f32[28,128,128]{2,1,0:T(8,128)} %tiles_hbm.1), custom_call_target="tpu_custom_call" | custom-call | tf_op jit(solution)/shard_map/schur_tiles/pallas_call | solution.py:268
  (4 shorter events, 0.1 us)
Async XLA Ops:
  7.2 50.9 %copy-start.1 = (f32[1024,32]{0,1:T(8,128)S(1)}, f32[1024,32]{0,1:T(8,128)}, u32[]{:S(2)}) copy-start(f32[1024,32]{0,1:T(8,128)} %param.5) | copy-start | bytes 393220
  7.2 120.9 %all-gather.3.cloned.1.call-start = ((), (), s32[]{:S(2)}) async-start(), calls=%async_computation | async-start | bytes 4456448 | tf_op jit(solution)/shard_map/all_gather | solution.py:242
  7.2 16.6 %collective-permute-start = (f32[32,1024]{1,0:T(8,128)}, f32[32,1024]{1,0:T(8,128)S(1)}, u32[]{:S(2)}, u32[]{:S(2)}) collective-permute-start(f32[32,1024]{1,0:T(8,128)} %bitcast.7), channel_id=1, source_target_pairs={{0,0},{1,240},{2,16},{3,224},{4,32},{5,208},{6,48},{7,192},{8,64},... | collective-permute-start | bytes 393224 | tf_op jit(solution)/shard_map/ppermute | solution.py:239
  23.8 7.3 %collective-permute-start.1 = (f32[32,1024]{1,0:T(8,128)S(1)}, f32[32,1024]{1,0:T(8,128)S(1)}, u32[]{:S(2)}, u32[]{:S(2)}) collective-permute-start(f32[32,1024]{1,0:T(8,128)S(1)} %collective-permute-done), channel_id=1, source_target_pairs={{0,256},{1,257},{2,258},{3,259},{4,260},{5,261},{6,262},{7,263},{8... | collective-permute-start | bytes 393224 | tf_op jit(solution)/shard_map/ppermute | solution.py:240
  31.9 9.0 %collective-permute-start.2 = (f32[32,1024]{1,0:T(8,128)}, f32[32,1024]{1,0:T(8,128)S(1)}, u32[]{:S(2)}, u32[]{:S(2)}) collective-permute-start(f32[32,1024]{1,0:T(8,128)} %bitcast.8), channel_id=1, source_target_pairs={{0,4},{1,5},{2,6},{3,7},{4,0},{5,1},{6,2},{7,3},{8,12},{9,13},{10,... | collective-permute-start | bytes 393224 | tf_op jit(solution)/shard_map/ppermute | solution.py:247
  41.8 10.9 %collective-permute-start.3 = (f32[64,1024]{1,0:T(8,128)S(1)}, f32[64,1024]{1,0:T(8,128)S(1)}, u32[]{:S(2)}, u32[]{:S(2)}) collective-permute-start(f32[64,1024]{1,0:T(8,128)S(1)} %pad_maximum_fusion.1), channel_id=1, source_target_pairs={{0,2},{1,3},{2,0},{3,1},{4,6},{5,7},{6,4},{7,5},{8,10},{9,11},{10,... | collective-permute-start | bytes 786440 | tf_op jit(solution)/shard_map/ppermute | solution.py:247
  53.7 16.1 %collective-permute-start.4 = (f32[128,1024]{1,0:T(8,128)S(1)}, f32[128,1024]{1,0:T(8,128)S(1)}, u32[]{:S(2)}, u32[]{:S(2)}) collective-permute-start(f32[128,1024]{1,0:T(8,128)S(1)} %pad_maximum_fusion), channel_id=1, source_target_pairs={{0,8},{1,9},{2,10},{3,11},{4,12},{5,13},{6,14},{7,15},{8,0},{9,1},... | collective-permute-start | bytes 1572872 | tf_op jit(solution)/shard_map/ppermute | solution.py:247
  69.9 32.6 %copy-start = (f32[256,1024]{1,0:T(8,128)}, f32[256,1024]{1,0:T(8,128)S(1)}, u32[]{:S(2)}) copy-start(f32[256,1024]{1,0:T(8,128)S(1)} %constant_dynamic-update-slice_fusion.panel_ref) | copy-start | bytes 3145732
  69.9 32.6 %collective-permute-start.5 = (f32[256,1024]{1,0:T(8,128)S(1)}, f32[256,1024]{1,0:T(8,128)S(1)}, u32[]{:S(2)}, u32[]{:S(2)}) collective-permute-start(f32[256,1024]{1,0:T(8,128)S(1)} %constant_dynamic-update-slice_fusion.panel_ref), channel_id=1, source_target_pairs={{0,1},{1,0},{2,3},{3,2},{4,5},{5,4},{6,7},{7,6},{8,9},{9,8},{10,11... | collective-permute-start | bytes 3145736 | tf_op jit(solution)/shard_map/ppermute | solution.py:247
  102.5 1.0 copy-start.2
Sparse Core Ops, SparseCore 0:
  32.0 96.0 all-gather.2

commit v3 on v2

--- a/solution.py
+++ b/solution.py
@@ -1,3 +1,5 @@
+import functools
+
 import jax
 import jax.numpy as jnp
 from jax import lax
@@ -68,41 +70,41 @@
             groups[h] = new
     return out
 
-def chol_inverse_kernel(a_ref, o_ref, t_ref, d_ref):
-    t_ref[...] = a_ref[...]
-    row = lax.broadcasted_iota(jnp.int32, (W, B), 0)
-    eye = jnp.where(lax.broadcasted_iota(jnp.int32, (B, B), 0) == lax.broadcasted_iota(jnp.int32, (B, B), 1), 1.0, 0.0).astype(jnp.float32)
-    lane_w = lax.broadcasted_iota(jnp.int32, (B, W), 1)
-
-    def step(b, carry):
-        here = pl.ds(pl.multiple_of(b * B, B), B)
-        panel = t_ref[:, here]
-        block = t_ref[here, here]
-        groups = [block[g * G:(g + 1) * G, :] for g in range(B // G)]
-        inv = factor_block(groups)
-        for g in range(B // G):
-            d_ref[g * G:(g + 1) * G, :] = inv[g]
-        inverse = d_ref[...]
-        t_ref[here, here] = eye
-        done = jnp.dot(inverse, t_ref[here, :], precision=HI, preferred_element_type=jnp.float32)
-        coef = lax.dot_general(panel, inverse, (((1,), (1,)), ((), ())), precision=HI, preferred_element_type=jnp.float32)
-        coef = jnp.where(row >= (b + 1) * B, coef, 0.0)
-        t_ref[:, here] = jnp.where(row >= b * B, 0.0, panel)
-        t_ref[...] = t_ref[...] - jnp.dot(coef, done, precision=HI, preferred_element_type=jnp.float32)
-        t_ref[here, :] = jnp.where(lane_w < (b + 1) * B, done, 0.0)
-        return carry
-
-    lax.fori_loop(0, W // B, step, 0)
-    o_ref[...] = t_ref[...]
-
-def chol_inverse(a):
+def dot(left, right):
+    return jnp.dot(left, right, precision=HI, preferred_element_type=jnp.float32)
+
+
+def factor_step_kernel(b, a_ref, o_ref, d_ref):
+    start, end = b * B, (b + 1) * B
+    block = a_ref[start:end, start:end]
+    for g, rows in enumerate(factor_block([block[g * G:(g + 1) * G, :] for g in range(B // G)])):
+        d_ref[g * G:(g + 1) * G, :] = rows
+    inverse = d_ref[...]
+    if b > 0:
+        o_ref[:start, :] = a_ref[:start, :]
+        before = dot(inverse, a_ref[start:end, :start])
+        o_ref[start:end, :start] = before
+    o_ref[start:end, start:end] = inverse
+    if end < W:
+        o_ref[start:end, end:] = jnp.zeros((B, W - end), jnp.float32)
+        behind = dot(inverse, a_ref[start:end, end:])
+        coef = lax.dot_general(
+            a_ref[end:, start:end], inverse, (((1,), (1,)), ((), ())), precision=HI, preferred_element_type=jnp.float32
+        )
+        if b > 0:
+            o_ref[end:, :start] = a_ref[end:, :start] - dot(coef, before)
+        o_ref[end:, start:end] = -dot(coef, inverse)
+        o_ref[end:, end:] = a_ref[end:, end:] - dot(coef, behind)
+
+
+def factor_step(b, a):
     return pl.pallas_call(
-        chol_inverse_kernel,
+        functools.partial(factor_step_kernel, b),
         out_shape=jax.ShapeDtypeStruct((W, W), jnp.float32),
         in_specs=[pl.BlockSpec(memory_space=pltpu.VMEM)],
         out_specs=pl.BlockSpec(memory_space=pltpu.VMEM),
-        scratch_shapes=[pltpu.VMEM((W, W), jnp.float32), pltpu.VMEM((B, B), jnp.float32)],
-        name="factor_inverse",
+        scratch_shapes=[pltpu.VMEM((B, B), jnp.float32)],
+        name="factor_step",
     )(a)
 
 
@@ -163,26 +165,28 @@
                 left_ref[first // B + part, B:, across] = low[part * B:(part + 1) * B]
 
 
-def tiles_kernel(targets_ref, left_hbm, far_hbm, tiles_hbm, out_hbm, left, far, tiles, out, right, in_sem, far_sem, out_sem):
-    blocks, size, planes = left.shape[0], far.shape[2], far.shape[0]
+def tiles_kernel(reach, targets_ref, left_hbm, tiles_hbm, *refs):
+    pieces, (out_hbm, left, far, tiles, out, right, in_sem, far_sem, out_sem) = refs[:len(reach)], refs[len(reach):]
+    blocks, size = left.shape[0], far.shape[2]
     count = out.shape[0]
     col, row = lax.axis_index("col"), lax.axis_index("row")
     n_cols = lax.axis_size("col")
     side = lax.div(row, n_cols)
-    far_copies = [pltpu.make_async_copy(far_hbm.at[z], far.at[z], far_sem.at[z]) for z in range(planes)]
+    far_copies = [pltpu.make_async_copy(piece, far.at[i], far_sem.at[i]) for i, piece in enumerate(pieces)]
     left_copy = pltpu.make_async_copy(left_hbm, left, in_sem.at[0])
     tiles_copy = pltpu.make_async_copy(tiles_hbm, tiles, in_sem.at[1])
     for copy in far_copies:
         copy.start()
     left_copy.start()
     tiles_copy.start()
-    for z in range(planes):
-        far_copies[z].wait()
-        apart = lax.rem(z - col + n_cols, n_cols)
-        k = jnp.where(apart < planes // 2, 2 * apart, 2 * planes - 1 - 2 * apart)
-        to = pl.ds(pl.multiple_of(k * size, size), size)
-        for slot in range(2):
-            high, low = halves(far[z, slot])
+    for i, away in enumerate(reach):
+        far_copies[i].wait()
+        for part in range(far.shape[1]):
+            twin, slot = part % 2, part // 2
+            apart = lax.rem(row + away - col - twin * (n_cols // 2) + 4 * n_cols, n_cols)
+            k = jnp.where(apart < n_cols // 2, 2 * apart, 2 * n_cols - 1 - 2 * apart)
+            to = pl.ds(pl.multiple_of(k * size, size), size)
+            high, low = halves(far[i, part])
             for block in range(blocks):
                 right[slot * blocks + block, to, :B] = high[:, block * B:(block + 1) * B]
                 right[slot * blocks + block, to, B:] = low[:, block * B:(block + 1) * B]
@@ -226,30 +230,84 @@
     size, rows = panel.shape[1], panel.shape[0]
     blocks, count = rows // B, tiles.shape[0]
     mine = panel.T
+    half = n_cols // 2
+    together = lax.optimization_barrier
 
     def at(r, c):
         return r * n_cols + c
 
-    def shifted(r, c):
-        step = c // 2 if c % 2 == 0 else n_cols - 1 - c // 2
+    def moved(r, step):
         return r // n_cols * n_cols + (r + step) % n_cols
 
-    turn = [(at(r, c), at(shifted(r, c), r % n_cols)) for r in range(n_rows) for c in range(n_cols)]
-    lift = [(at(r, c), at(r + n_cols, c)) for r in range(n_cols) for c in range(n_cols)]
-    near = lax.ppermute(mine, ("row", "col"), turn)
+    def spread(c):
+        return c // 2 if c % 2 == 0 else n_cols - 1 - c // 2
+
+    everyone = [(r, c) for r in range(n_rows) for c in range(n_cols)]
+    turn = [(at(r, c), at(moved(r, spread(c)), r % n_cols)) for r, c in everyone]
+    twin = [(at(r, c), at(moved(r, spread(c) + half), r % n_cols)) for r, c in everyone]
+    lift = [(at(r, c), at(r + n_cols, c)) for r, c in everyone if r < n_cols]
+    up = [(r, moved(r, 1)) for r in range(n_rows)]
+    down = [(r, moved(r, -1)) for r in range(n_rows)]
+    flips = [[(c, c ^ flip) for c in range(n_cols)] for flip in (n_cols // 4, n_cols // 8, n_cols // 2, 1)]
+
+    first = lax.ppermute(mine, ("row", "col"), turn)
+    second = lax.ppermute(mine, ("row", "col"), twin)
+    work = factor_step(0, diag_block)
+    first, second, work, own = together((first, second, work, mine))
+
+    near = jnp.stack([first, second])
     other = lax.ppermute(near, ("row", "col"), lift)
-    lines = [[part * n_cols + z for z in range(n_cols)] for part in range(n_rows // n_cols)]
-    far = lax.all_gather(jnp.stack([near, other]), "row", axis=0, axis_index_groups=lines)
-
-    own, diag, _ = lax.optimization_barrier((mine, diag_block, other))
-    for flip in (n_cols // 4, n_cols // 8, n_cols // 2, 1):
-        pairs = [(c, c ^ flip) for c in range(n_cols)]
-        received = lax.ppermute(own, "col", pairs)
-        if flip != 1:
+    received = lax.ppermute(own, "col", flips[0])
+    work = factor_step(1, work)
+    near, other, received, work = together((near, other, received, work))
+
+    base = jnp.concatenate([near, other])
+    own = jnp.concatenate([own, received])
+    upward, downward, pieces, reach = base, base, [base], [0]
+    for step in range(1, half // 2 + 1):
+        upward = lax.ppermute(upward, "row", up)
+        pieces.append(upward)
+        reach.append(-step)
+        if step < half // 2:
+            downward = lax.ppermute(downward, "row", down)
+            pieces.append(downward)
+            reach.append(step)
+        if step < len(flips):
+            received = lax.ppermute(own, "col", flips[step])
+        if step + 1 < W // B:
+            work = factor_step(step + 1, work)
+        upward, downward, received, work, own = together((upward, downward, received, work, own))
+        pieces[-1 if step == half // 2 else -2] = upward
+        if step < half // 2:
+            pieces[-1] = downward
+        if step + 1 < len(flips):
             own = jnp.concatenate([own, received])
-    inverse = chol_inverse(diag)
+        if step + 1 == len(flips):
+            left, panel_slice = own_rows(work, own, received, size, blocks)
     any_space = pl.BlockSpec(memory_space=pl.ANY)
-    left, panel_slice = pl.pallas_call(
+    schur = pl.pallas_call(
+        functools.partial(tiles_kernel, tuple(reach)),
+        out_shape=jax.ShapeDtypeStruct(tiles.shape, F32),
+        in_specs=[pl.BlockSpec(memory_space=pltpu.SMEM), *[any_space] * (2 + len(pieces))],
+        out_specs=any_space,
+        scratch_shapes=[
+            pltpu.VMEM(left.shape, BF),
+            pltpu.VMEM((len(pieces), *base.shape), F32),
+            pltpu.VMEM(tiles.shape, F32),
+            pltpu.VMEM(tiles.shape, F32),
+            pltpu.VMEM((2 * blocks, W, 2 * B), BF),
+            pltpu.SemaphoreType.DMA((2,)),
+            pltpu.SemaphoreType.DMA((len(pieces),)),
+            pltpu.SemaphoreType.DMA((count,)),
+        ],
+        name="schur_tiles",
+    )(targets.T, left, tiles, *pieces)
+    return panel_slice.T, schur
+
+
+def own_rows(inverse, own, received, size, blocks):
+    rows = own.shape[1]
+    return pl.pallas_call(
         own_kernel,
         out_shape=(
             jax.ShapeDtypeStruct((blocks, 2 * B, W), BF),
@@ -265,24 +323,6 @@
         ],
         name="own_rows",
     )(inverse, own, received)
-    schur = pl.pallas_call(
-        tiles_kernel,
-        out_shape=jax.ShapeDtypeStruct(tiles.shape, F32),
-        in_specs=[pl.BlockSpec(memory_space=pltpu.SMEM), *[any_space] * 3],
-        out_specs=any_space,
-        scratch_shapes=[
-            pltpu.VMEM(left.shape, BF),
-            pltpu.VMEM(far.shape, F32),
-            pltpu.VMEM(tiles.shape, F32),
-            pltpu.VMEM(tiles.shape, F32),
-            pltpu.VMEM((2 * blocks, W, 2 * B), BF),
-            pltpu.SemaphoreType.DMA((2,)),
-            pltpu.SemaphoreType.DMA((far.shape[0],)),
-            pltpu.SemaphoreType.DMA((count,)),
-        ],
-        name="schur_tiles",
-    )(targets.T, left, far, tiles)
-    return panel_slice.T, schur
 
 
 def solution(mesh):

time: 144 us -> 139 us (0.965)
  starting transfers between devices: 22.7 us -> 63.2 us
  waiting for transfers between devices: 58.8 us -> 26.7 us
  between operations: 14.2 us -> 1.08 us
  Pallas kernels: 43.9 us -> 46.7 us
  other arithmetic: 2.62 us -> 0.02 us
    ppermute x5 -> x13, starting transfers between devices: 17.8 us -> 58.3 us  [the longest x3 14.5 us: on_device(): downward = lax.ppermute(downward, 'row', down)]
    all_gather x1 -> x0, waiting for transfers between devices: 18.5 us -> none  [on_device(): lax.all_gather(jnp.stack([near, other]), 'row', axis=0, axis_index_groups...]
    ppermute x5 -> x13, waiting for transfers between devices: 37.8 us -> 26.7 us  [the longest x4 21.1 us: on_device(): upward = lax.ppermute(upward, 'row', up)]
    pallas_call x3 -> x6, Pallas kernels: 43.9 us -> 46.7 us  [the longest x4 32.3 us: factor_step(): pl.pallas_call(functools.partial(factor_step_kernel, b), out_shape=jax.Sh...]
    ppermute x1, waiting for transfers between devices: 2.5 us -> 0.01 us  [on_device(): other = lax.ppermute(near, ('row', 'col'), lift)]
    concatenate x2 -> x0, other arithmetic: 1.87 us -> none  [on_device(): own = jnp.concatenate([own, received])]
  transfers between devices with their start and end apart: 7 -> 14, of which waited for: 6 -> 5; matrix products, arithmetic and copies ran while one was open for 1% -> 0% of each run, Pallas kernels for 25% -> 28%
where the time goes in v3:
time: 139 us
  starting transfers between devices  63.2 us (45%)
  Pallas kernels  46.7 us (34%)
  waiting for transfers between devices  26.7 us (19%)
    pallas_call x4, Pallas kernels, factor_step(): pl.pallas_call(functools.partial(factor_step_kernel, b), out_shape=jax.Sh...  32.3 us
    ppermute x4, waiting for transfers between devices, on_device(): upward = lax.ppermute(upward, 'row', up)  21.1 us
    ppermute x3, starting transfers between devices, on_device(): downward = lax.ppermute(downward, 'row', down)  14.5 us
    ppermute x1, starting transfers between devices, on_device(): second = lax.ppermute(mine, ('row', 'col'), twin)  14.4 us
    ppermute x3, starting transfers between devices, on_device(): received = lax.ppermute(own, 'col', flips[step])  13.9 us
    pallas_call x1, Pallas kernels, on_device(): pl.pallas_call(functools.partial(tiles_kernel, tuple(reach)), out_shape=j...  8.27 us
    ppermute x4, starting transfers between devices, on_device(): upward = lax.ppermute(upward, 'row', up)  7.89 us
    pallas_call x1, Pallas kernels, own_rows(): pl.pallas_call(own_kernel, out_shape=(jax.ShapeDtypeStruct((blocks, 2 * B...  6.13 us
  transfers between devices with their start and end apart: 14, of which 5 were waited for; matrix products, arithmetic and copies ran while one was open for 0% of the time, Pallas kernels for 28%

profile of v3, /device:TPU:6, one launch (start us, length us, event | category | flops | bytes accessed | tf_op | source)
XLA Modules:
  0.0 138.7 jit_solution(17132047163590761692)
XLA Ops:
  0.6 14.4 %collective-permute-start.1 = (f32[32,1024]{1,0:T(8,128)}, f32[32,1024]{1,0:T(8,128)S(1)}, u32[]{:S(2)}, u32[]{:S(2)}) collective-permute-start(f32[32,1024]{1,0:T(8,128)} %bitcast.5), channel_id=1, source_target_pairs={{0,128},{1,112},{2,144},{3,96},{4,160},{5,80},{6,176},{7,64},{8,19... | collective-permute-start | bytes 393224 | tf_op jit(solution)/shard_map/ppermute | solution.py:254
  15.1 5.5 %collective-permute-start = (f32[32,1024]{1,0:T(8,128)}, f32[32,1024]{1,0:T(8,128)S(1)}, u32[]{:S(2)}, u32[]{:S(2)}) collective-permute-start(f32[32,1024]{1,0:T(8,128)} %bitcast.6), channel_id=1, source_target_pairs={{0,0},{1,240},{2,16},{3,224},{4,32},{5,208},{6,48},{7,192},{8,64},... | collective-permute-start | bytes 393224 | tf_op jit(solution)/shard_map/ppermute | solution.py:253
  20.6 8.6 %factor_step.4.a_ref = f32[512,512]{1,0:T(8,128)} custom-call(f32[512,512]{1,0:T(8,128)} %a_ref.1), custom_call_target="tpu_custom_call" | custom-call | tf_op jit(solution)/shard_map/factor_step/pallas_call | solution.py:101
  29.2 0.0 collective-permute-done.1
  29.2 4.0 %collective-permute-done = f32[32,1024]{1,0:T(8,128)S(1)} collective-permute-done((f32[32,1024]{1,0:T(8,128)}, f32[32,1024]{1,0:T(8,128)S(1)}, u32[]{:S(2)}, u32[]{:S(2)}) %collective-permute-start) | collective-permute-done | bytes 131104 | tf_op jit(solution)/shard_map/ppermute | solution.py:253
  33.2 4.9 %collective-permute-start.2 = (f32[2,32,1024]{2,1,0:T(8,128)S(1)}, f32[2,32,1024]{2,1,0:T(8,128)S(1)}, u32[]{:S(2)}, u32[]{:S(2)}) collective-permute-start(f32[2,32,1024]{2,1,0:T(8,128)S(1)} %pad_maximum_fusion), channel_id=1, source_target_pairs={{0,256},{1,257},{2,258},{3,259},{4,260},{5,261},{6,262},{7,263},{8... | collective-permute-start | bytes 786440 | tf_op jit(solution)/shard_map/ppermute | solution.py:259
  38.2 1.9 %collective-permute-start.3 = (f32[32,1024]{1,0:T(8,128)S(1)}, f32[32,1024]{1,0:T(8,128)S(1)}, u32[]{:S(2)}, u32[]{:S(2)}) collective-permute-start(f32[32,1024]{1,0:T(8,128)S(1)} %bitcast.7), channel_id=1, source_target_pairs={{0,4},{1,5},{2,6},{3,7},{4,0},{5,1},{6,2},{7,3},{8,12},{9,13},{10,... | collective-permute-start | bytes 393224 | tf_op jit(solution)/shard_map/ppermute | solution.py:260
  40.1 8.3 %factor_step.5.a_ref = f32[512,512]{1,0:T(8,128)} custom-call(f32[512,512]{1,0:T(8,128)} %factor_step.4.a_ref), custom_call_target="tpu_custom_call" | custom-call | tf_op jit(solution)/shard_map/factor_step/pallas_call | solution.py:101
  48.4 0.0 collective-permute-done.3
  48.4 4.3 %collective-permute-start.5 = (f32[4,32,1024]{2,1,0:T(8,128)S(1)}, f32[4,32,1024]{2,1,0:T(8,128)S(1)}, u32[]{:S(2)}, u32[]{:S(2)}) collective-permute-start(f32[4,32,1024]{2,1,0:T(8,128)S(1)} %constant_dynamic-update-slice_fusion.refs_0_), channel_id=1, source_target_pairs={{0,240},{16,0},{32,16},{48,32},{64,48},{80,64},{96,80},{112,96},{1... | collective-permute-start | bytes 1572872 | tf_op jit(solution)/shard_map/ppermute | solution.py:272
  52.7 1.9 %collective-permute-start.4 = (f32[4,32,1024]{2,1,0:T(8,128)S(1)}, f32[4,32,1024]{2,1,0:T(8,128)S(1)}, u32[]{:S(2)}, u32[]{:S(2)}) collective-permute-start(f32[4,32,1024]{2,1,0:T(8,128)S(1)} %constant_dynamic-update-slice_fusion.refs_0_), channel_id=1, source_target_pairs={{0,16},{16,32},{32,48},{48,64},{64,80},{80,96},{96,112},{112,128},... | collective-permute-start | bytes 1572872 | tf_op jit(solution)/shard_map/ppermute | solution.py:268
  54.7 3.3 %collective-permute-start.6 = (f32[64,1024]{1,0:T(8,128)S(1)}, f32[64,1024]{1,0:T(8,128)S(1)}, u32[]{:S(2)}, u32[]{:S(2)}) collective-permute-start(f32[64,1024]{1,0:T(8,128)S(1)} %constant_dynamic-update-slice_fusion.2), channel_id=1, source_target_pairs={{0,2},{1,3},{2,0},{3,1},{4,6},{5,7},{6,4},{7,5},{8,10},{9,11},{10,... | collective-permute-start | bytes 786440 | tf_op jit(solution)/shard_map/ppermute | solution.py:276
  58.0 8.1 %factor_step.6.a_ref = f32[512,512]{1,0:T(8,128)} custom-call(f32[512,512]{1,0:T(8,128)} %factor_step.5.a_ref), custom_call_target="tpu_custom_call" | custom-call | tf_op jit(solution)/shard_map/factor_step/pallas_call | solution.py:101
  66.1 2.0 %collective-permute-done.4.refs_1_ = f32[4,32,1024]{2,1,0:T(8,128)S(1)} collective-permute-done((f32[4,32,1024]{2,1,0:T(8,128)S(1)}, f32[4,32,1024]{2,1,0:T(8,128)S(1)}, u32[]{:S(2)}, u32[]{:S(2)}) %collective-permute-start.4) | collective-permute-done | bytes 524320 | tf_op jit(solution)/shard_map/ppermute | solution.py:268
  68.2 8.6 %collective-permute-start.9 = (f32[128,1024]{1,0:T(8,128)S(1)}, f32[128,1024]{1,0:T(8,128)S(1)}, u32[]{:S(2)}, u32[]{:S(2)}) collective-permute-start(f32[128,1024]{1,0:T(8,128)S(1)} %constant_dynamic-update-slice_fusion.4), channel_id=1, source_target_pairs={{0,8},{1,9},{2,10},{3,11},{4,12},{5,13},{6,14},{7,15},{8,0},{9,1},... | collective-permute-start | bytes 1572872 | tf_op jit(solution)/shard_map/ppermute | solution.py:276
  76.8 1.9 %collective-permute-start.7 = (f32[4,32,1024]{2,1,0:T(8,128)S(1)}, f32[4,32,1024]{2,1,0:T(8,128)S(1)}, u32[]{:S(2)}, u32[]{:S(2)}) collective-permute-start(f32[4,32,1024]{2,1,0:T(8,128)S(1)} %collective-permute-done.4.refs_1_), channel_id=1, source_target_pairs={{0,16},{16,32},{32,48},{48,64},{64,80},{80,96},{96,112},{112,128},... | collective-permute-start | bytes 1572872 | tf_op jit(solution)/shard_map/ppermute | solution.py:268
  78.7 5.1 %collective-permute-start.8 = (f32[4,32,1024]{2,1,0:T(8,128)S(1)}, f32[4,32,1024]{2,1,0:T(8,128)}, u32[]{:S(2)}, u32[]{:S(2)}) collective-permute-start(f32[4,32,1024]{2,1,0:T(8,128)S(1)} %collective-permute-done.5.refs_2_), channel_id=1, source_target_pairs={{0,240},{16,0},{32,16},{48,32},{64,48},{80,64},{96,80},{112,96},{1... | collective-permute-start | bytes 1572872 | tf_op jit(solution)/shard_map/ppermute | solution.py:272
  83.9 7.4 %factor_step.7.inverse_ref = f32[512,512]{1,0:T(8,128)} custom-call(f32[512,512]{1,0:T(8,128)} %factor_step.6.a_ref), custom_call_target="tpu_custom_call" | custom-call | tf_op jit(solution)/shard_map/factor_step/pallas_call | solution.py:101
  91.2 0.0 collective-permute-done.9
  91.2 0.0 collective-permute-done.7.refs_3_
  91.3 0.8 copy-done.5
  92.1 0.0 collective-permute-done.8.refs_4_
  92.2 0.0 copy-start
  92.2 2.1 %collective-permute-start.12 = (f32[256,1024]{1,0:T(8,128)S(1)}, f32[256,1024]{1,0:T(8,128)S(1)}, u32[]{:S(2)}, u32[]{:S(2)}) collective-permute-start(f32[256,1024]{1,0:T(8,128)S(1)} %constant_dynamic-update-slice_fusion.6.panel_ref), channel_id=1, source_target_pairs={{0,1},{1,0},{2,3},{3,2},{4,5},{5,4},{6,7},{7,6},{8,9},{9,8},{10,11... | collective-permute-start | bytes 3145736 | tf_op jit(solution)/shard_map/ppermute | solution.py:276
  94.3 1.9 %collective-permute-start.10 = (f32[4,32,1024]{2,1,0:T(8,128)S(1)}, f32[4,32,1024]{2,1,0:T(8,128)S(1)}, u32[]{:S(2)}, u32[]{:S(2)}) collective-permute-start(f32[4,32,1024]{2,1,0:T(8,128)S(1)} %copy-done.6), channel_id=1, source_target_pairs={{0,16},{16,32},{32,48},{48,64},{64,80},{80,96},{96,112},{112,128},... | collective-permute-start | bytes 1572872 | tf_op jit(solution)/shard_map/ppermute | solution.py:268
  96.2 5.1 %collective-permute-start.11 = (f32[4,32,1024]{2,1,0:T(8,128)}, f32[4,32,1024]{2,1,0:T(8,128)S(1)}, u32[]{:S(2)}, u32[]{:S(2)}) collective-permute-start(f32[4,32,1024]{2,1,0:T(8,128)} %collective-permute-done.8.refs_4_), channel_id=1, source_target_pairs={{0,240},{16,0},{32,16},{48,32},{64,48},{80,64},{96,80},{112,96},{1... | collective-permute-start | bytes 1572872 | tf_op jit(solution)/shard_map/ppermute | solution.py:272
  101.3 10.4 %collective-permute-done.10.refs_5_ = f32[4,32,1024]{2,1,0:T(8,128)S(1)} collective-permute-done((f32[4,32,1024]{2,1,0:T(8,128)S(1)}, f32[4,32,1024]{2,1,0:T(8,128)S(1)}, u32[]{:S(2)}, u32[]{:S(2)}) %collective-permute-start.10) | collective-permute-done | bytes 524320 | tf_op jit(solution)/shard_map/ppermute | solution.py:268
  111.7 1.5 %collective-permute-done.11.refs_6_ = f32[4,32,1024]{2,1,0:T(8,128)S(1)} collective-permute-done((f32[4,32,1024]{2,1,0:T(8,128)}, f32[4,32,1024]{2,1,0:T(8,128)S(1)}, u32[]{:S(2)}, u32[]{:S(2)}) %collective-permute-start.11) | collective-permute-done | bytes 524320 | tf_op jit(solution)/shard_map/ppermute | solution.py:272
  113.2 2.1 %collective-permute-start.13 = (f32[4,32,1024]{2,1,0:T(8,128)S(1)}, f32[4,32,1024]{2,1,0:T(8,128)}, u32[]{:S(2)}, u32[]{:S(2)}) collective-permute-start(f32[4,32,1024]{2,1,0:T(8,128)S(1)} %collective-permute-done.10.refs_5_), channel_id=1, source_target_pairs={{0,16},{16,32},{32,48},{48,64},{64,80},{80,96},{96,112},{112,128},... | collective-permute-start | bytes 1572872 | tf_op jit(solution)/shard_map/ppermute | solution.py:268
  115.4 6.1 %own_rows.1 = (bf16[8,256,512]{2,1,0:T(8,128)(2,1)}, f32[32,1024]{1,0:T(8,128)}) custom-call(f32[512,512]{1,0:T(8,128)} %factor_step.7.inverse_ref, f32[256,1024]{1,0:T(8,128)} %copy-done, f32[256,1024]{1,0:T(8,128)} %copy-done.2), custom_call_target="tpu_custom_call" | custom-call | tf_op jit(solution)/shard_map/own_rows/pallas_call | solution.py:310
  121.5 8.7 %collective-permute-done.13.refs_7_ = f32[4,32,1024]{2,1,0:T(8,128)} collective-permute-done((f32[4,32,1024]{2,1,0:T(8,128)S(1)}, f32[4,32,1024]{2,1,0:T(8,128)}, u32[]{:S(2)}, u32[]{:S(2)}) %collective-permute-start.13) | collective-permute-done | bytes 524320 | tf_op jit(solution)/shard_map/ppermute | solution.py:268
  130.2 8.3 %schur_tiles.1 = f32[28,128,128]{2,1,0:T(8,128)} custom-call(s32[2,28]{1,0:T(2,128)} %bitcast.11, bf16[8,256,512]{2,1,0:T(8,128)(2,1)} %get-tuple-element.50.left_hbm, f32[28,128,128]{2,1,0:T(8,128)} %tiles_hbm.1, f32[4,32,1024]{2,1,0:T(8,128)} %copy-done.1, f32[4,32,1024]{2,1,0:T(8,128)} %copy-done.4, f32[4,32,1024]{2,1,0:T(8,128)} %copy-done.3, ...), custom_call_target="tpu_custom_call" | custom-call | tf_op jit(solution)/shard_map/schur_tiles/pallas_call | solution.py:288
  (31 shorter events, 0.2 us)
Async XLA Ops:
  0.6 37.5 %copy-start.9 = (f32[1024,32]{0,1:T(8,128)S(1)}, f32[1024,32]{0,1:T(8,128)}, u32[]{:S(2)}) copy-start(f32[1024,32]{0,1:T(8,128)} %param.5) | copy-start | bytes 393220
  0.6 28.6 %collective-permute-start.1 = (f32[32,1024]{1,0:T(8,128)}, f32[32,1024]{1,0:T(8,128)S(1)}, u32[]{:S(2)}, u32[]{:S(2)}) collective-permute-start(f32[32,1024]{1,0:T(8,128)} %bitcast.5), channel_id=1, source_target_pairs={{0,128},{1,112},{2,144},{3,96},{4,160},{5,80},{6,176},{7,64},{8,19... | collective-permute-start | bytes 393224 | tf_op jit(solution)/shard_map/ppermute | solution.py:254
  15.1 18.1 %collective-permute-start = (f32[32,1024]{1,0:T(8,128)}, f32[32,1024]{1,0:T(8,128)S(1)}, u32[]{:S(2)}, u32[]{:S(2)}) collective-permute-start(f32[32,1024]{1,0:T(8,128)} %bitcast.6), channel_id=1, source_target_pairs={{0,0},{1,240},{2,16},{3,224},{4,32},{5,208},{6,48},{7,192},{8,64},... | collective-permute-start | bytes 393224 | tf_op jit(solution)/shard_map/ppermute | solution.py:253
  33.2 15.1 %collective-permute-start.2 = (f32[2,32,1024]{2,1,0:T(8,128)S(1)}, f32[2,32,1024]{2,1,0:T(8,128)S(1)}, u32[]{:S(2)}, u32[]{:S(2)}) collective-permute-start(f32[2,32,1024]{2,1,0:T(8,128)S(1)} %pad_maximum_fusion), channel_id=1, source_target_pairs={{0,256},{1,257},{2,258},{3,259},{4,260},{5,261},{6,262},{7,263},{8... | collective-permute-start | bytes 786440 | tf_op jit(solution)/shard_map/ppermute | solution.py:259
  38.2 10.2 %collective-permute-start.3 = (f32[32,1024]{1,0:T(8,128)S(1)}, f32[32,1024]{1,0:T(8,128)S(1)}, u32[]{:S(2)}, u32[]{:S(2)}) collective-permute-start(f32[32,1024]{1,0:T(8,128)S(1)} %bitcast.7), channel_id=1, source_target_pairs={{0,4},{1,5},{2,6},{3,7},{4,0},{5,1},{6,2},{7,3},{8,12},{9,13},{10,... | collective-permute-start | bytes 393224 | tf_op jit(solution)/shard_map/ppermute | solution.py:260
  48.4 19.8 %copy-start.1 = (f32[4,32,1024]{2,1,0:T(8,128)}, f32[4,32,1024]{2,1,0:T(8,128)S(1)}, u32[]{:S(2)}) copy-start(f32[4,32,1024]{2,1,0:T(8,128)S(1)} %constant_dynamic-update-slice_fusion.refs_0_) | copy-start | bytes 1572868
  48.4 17.7 %collective-permute-start.5 = (f32[4,32,1024]{2,1,0:T(8,128)S(1)}, f32[4,32,1024]{2,1,0:T(8,128)S(1)}, u32[]{:S(2)}, u32[]{:S(2)}) collective-permute-start(f32[4,32,1024]{2,1,0:T(8,128)S(1)} %constant_dynamic-update-slice_fusion.refs_0_), channel_id=1, source_target_pairs={{0,240},{16,0},{32,16},{48,32},{64,48},{80,64},{96,80},{112,96},{1... | collective-permute-start | bytes 1572872 | tf_op jit(solution)/shard_map/ppermute | solution.py:272
  52.7 15.4 %collective-permute-start.4 = (f32[4,32,1024]{2,1,0:T(8,128)S(1)}, f32[4,32,1024]{2,1,0:T(8,128)S(1)}, u32[]{:S(2)}, u32[]{:S(2)}) collective-permute-start(f32[4,32,1024]{2,1,0:T(8,128)S(1)} %constant_dynamic-update-slice_fusion.refs_0_), channel_id=1, source_target_pairs={{0,16},{16,32},{32,48},{48,64},{64,80},{80,96},{96,112},{112,128},... | collective-permute-start | bytes 1572872 | tf_op jit(solution)/shard_map/ppermute | solution.py:268
  54.7 11.4 %collective-permute-start.6 = (f32[64,1024]{1,0:T(8,128)S(1)}, f32[64,1024]{1,0:T(8,128)S(1)}, u32[]{:S(2)}, u32[]{:S(2)}) collective-permute-start(f32[64,1024]{1,0:T(8,128)S(1)} %constant_dynamic-update-slice_fusion.2), channel_id=1, source_target_pairs={{0,2},{1,3},{2,0},{3,1},{4,6},{5,7},{6,4},{7,5},{8,10},{9,11},{10,... | collective-permute-start | bytes 786440 | tf_op jit(solution)/shard_map/ppermute | solution.py:276
  66.1 26.0 %copy-start.3 = (f32[4,32,1024]{2,1,0:T(8,128)}, f32[4,32,1024]{2,1,0:T(8,128)S(1)}, u32[]{:S(2)}) copy-start(f32[4,32,1024]{2,1,0:T(8,128)S(1)} %collective-permute-done.5.refs_2_) | copy-start | bytes 1572868
  68.2 24.0 %copy-start.4 = (f32[4,32,1024]{2,1,0:T(8,128)}, f32[4,32,1024]{2,1,0:T(8,128)S(1)}, u32[]{:S(2)}) copy-start(f32[4,32,1024]{2,1,0:T(8,128)S(1)} %collective-permute-done.4.refs_1_) | copy-start | bytes 1572868
  68.2 23.0 %collective-permute-start.9 = (f32[128,1024]{1,0:T(8,128)S(1)}, f32[128,1024]{1,0:T(8,128)S(1)}, u32[]{:S(2)}, u32[]{:S(2)}) collective-permute-start(f32[128,1024]{1,0:T(8,128)S(1)} %constant_dynamic-update-slice_fusion.4), channel_id=1, source_target_pairs={{0,8},{1,9},{2,10},{3,11},{4,12},{5,13},{6,14},{7,15},{8,0},{9,1},... | collective-permute-start | bytes 1572872 | tf_op jit(solution)/shard_map/ppermute | solution.py:276
  76.8 14.4 %collective-permute-start.7 = (f32[4,32,1024]{2,1,0:T(8,128)S(1)}, f32[4,32,1024]{2,1,0:T(8,128)S(1)}, u32[]{:S(2)}, u32[]{:S(2)}) collective-permute-start(f32[4,32,1024]{2,1,0:T(8,128)S(1)} %collective-permute-done.4.refs_1_), channel_id=1, source_target_pairs={{0,16},{16,32},{32,48},{48,64},{64,80},{80,96},{96,112},{112,128},... | collective-permute-start | bytes 1572872 | tf_op jit(solution)/shard_map/ppermute | solution.py:268
  78.7 13.3 %collective-permute-start.8 = (f32[4,32,1024]{2,1,0:T(8,128)S(1)}, f32[4,32,1024]{2,1,0:T(8,128)}, u32[]{:S(2)}, u32[]{:S(2)}) collective-permute-start(f32[4,32,1024]{2,1,0:T(8,128)S(1)} %collective-permute-done.5.refs_2_), channel_id=1, source_target_pairs={{0,240},{16,0},{32,16},{48,32},{64,48},{80,64},{96,80},{112,96},{1... | collective-permute-start | bytes 1572872 | tf_op jit(solution)/shard_map/ppermute | solution.py:272
  91.2 0.8 copy-start.5
  92.1 2.2 %copy-start.6 = (f32[4,32,1024]{2,1,0:T(8,128)S(1)}, f32[4,32,1024]{2,1,0:T(8,128)}, u32[]{:S(2)}) copy-start(f32[4,32,1024]{2,1,0:T(8,128)} %copy-done.5) | copy-start | bytes 1572868
  92.2 23.2 %copy-start = (f32[256,1024]{1,0:T(8,128)}, f32[256,1024]{1,0:T(8,128)S(1)}, u32[]{:S(2)}) copy-start(f32[256,1024]{1,0:T(8,128)S(1)} %constant_dynamic-update-slice_fusion.6.panel_ref) | copy-start | bytes 3145732
  92.2 21.0 %collective-permute-start.12 = (f32[256,1024]{1,0:T(8,128)S(1)}, f32[256,1024]{1,0:T(8,128)S(1)}, u32[]{:S(2)}, u32[]{:S(2)}) collective-permute-start(f32[256,1024]{1,0:T(8,128)S(1)} %constant_dynamic-update-slice_fusion.6.panel_ref), channel_id=1, source_target_pairs={{0,1},{1,0},{2,3},{3,2},{4,5},{5,4},{6,7},{7,6},{8,9},{9,8},{10,11... | collective-permute-start | bytes 3145736 | tf_op jit(solution)/shard_map/ppermute | solution.py:276
  94.3 17.4 %collective-permute-start.10 = (f32[4,32,1024]{2,1,0:T(8,128)S(1)}, f32[4,32,1024]{2,1,0:T(8,128)S(1)}, u32[]{:S(2)}, u32[]{:S(2)}) collective-permute-start(f32[4,32,1024]{2,1,0:T(8,128)S(1)} %copy-done.6), channel_id=1, source_target_pairs={{0,16},{16,32},{32,48},{48,64},{64,80},{80,96},{96,112},{112,128},... | collective-permute-start | bytes 1572872 | tf_op jit(solution)/shard_map/ppermute | solution.py:268
  96.2 17.0 %collective-permute-start.11 = (f32[4,32,1024]{2,1,0:T(8,128)}, f32[4,32,1024]{2,1,0:T(8,128)S(1)}, u32[]{:S(2)}, u32[]{:S(2)}) collective-permute-start(f32[4,32,1024]{2,1,0:T(8,128)} %collective-permute-done.8.refs_4_), channel_id=1, source_target_pairs={{0,240},{16,0},{32,16},{48,32},{64,48},{80,64},{96,80},{112,96},{1... | collective-permute-start | bytes 1572872 | tf_op jit(solution)/shard_map/ppermute | solution.py:272
  111.7 18.5 %copy-start.7 = (f32[4,32,1024]{2,1,0:T(8,128)}, f32[4,32,1024]{2,1,0:T(8,128)S(1)}, u32[]{:S(2)}) copy-start(f32[4,32,1024]{2,1,0:T(8,128)S(1)} %collective-permute-done.10.refs_5_) | copy-start | bytes 1572868
  113.2 17.0 %copy-start.8 = (f32[4,32,1024]{2,1,0:T(8,128)}, f32[4,32,1024]{2,1,0:T(8,128)S(1)}, u32[]{:S(2)}) copy-start(f32[4,32,1024]{2,1,0:T(8,128)S(1)} %collective-permute-done.11.refs_6_) | copy-start | bytes 1572868
  113.2 2.2 %copy-start.2 = (f32[256,1024]{1,0:T(8,128)}, f32[256,1024]{1,0:T(8,128)S(1)}, u32[]{:S(2)}) copy-start(f32[256,1024]{1,0:T(8,128)S(1)} %collective-permute-done.12.partner_ref) | copy-start | bytes 3145732
  113.2 17.0 %collective-permute-start.13 = (f32[4,32,1024]{2,1,0:T(8,128)S(1)}, f32[4,32,1024]{2,1,0:T(8,128)}, u32[]{:S(2)}, u32[]{:S(2)}) collective-permute-start(f32[4,32,1024]{2,1,0:T(8,128)S(1)} %collective-permute-done.10.refs_5_), channel_id=1, source_target_pairs={{0,16},{16,32},{32,48},{48,64},{64,80},{80,96},{96,112},{112,128},... | collective-permute-start | bytes 1572872 | tf_op jit(solution)/shard_map/ppermute | solution.py:268

commit v4 on v3

--- a/solution.py
+++ b/solution.py
@@ -10,8 +10,10 @@
 W, B, G, UNROLL = 512, 128, 8, 4
 HI = lax.Precision.HIGHEST
 
+
 def splat(col, k):
     return jnp.broadcast_to(col[k:k + 1, :], (G, B))
+
 
 def factor_block(groups):
     n = len(groups)
@@ -70,6 +72,7 @@
             groups[h] = new
     return out
 
+
 def dot(left, right):
     return jnp.dot(left, right, precision=HI, preferred_element_type=jnp.float32)
 
@@ -258,32 +261,30 @@
     near = jnp.stack([first, second])
     other = lax.ppermute(near, ("row", "col"), lift)
     received = lax.ppermute(own, "col", flips[0])
-    work = factor_step(1, work)
-    near, other, received, work = together((near, other, received, work))
+    near, other, work = together((near, other, work))
 
     base = jnp.concatenate([near, other])
-    own = jnp.concatenate([own, received])
     upward, downward, pieces, reach = base, base, [base], [0]
     for step in range(1, half // 2 + 1):
+        both = step < half // 2
         upward = lax.ppermute(upward, "row", up)
+        if both:
+            downward = lax.ppermute(downward, "row", down)
+        if step < W // B:
+            work = factor_step(step, work)
+            received, work = together((received, work))
+            own = jnp.concatenate([own, received])
+            received = lax.ppermute(own, "col", flips[step])
+            if step + 1 == W // B:
+                left, panel_slice = own_rows(work, own, received, size, blocks)
+            upward, downward, work = together((upward, downward, work))
+        else:
+            upward, left, panel_slice = together((upward, left, panel_slice))
         pieces.append(upward)
         reach.append(-step)
-        if step < half // 2:
-            downward = lax.ppermute(downward, "row", down)
+        if both:
             pieces.append(downward)
             reach.append(step)
-        if step < len(flips):
-            received = lax.ppermute(own, "col", flips[step])
-        if step + 1 < W // B:
-            work = factor_step(step + 1, work)
-        upward, downward, received, work, own = together((upward, downward, received, work, own))
-        pieces[-1 if step == half // 2 else -2] = upward
-        if step < half // 2:
-            pieces[-1] = downward
-        if step + 1 < len(flips):
-            own = jnp.concatenate([own, received])
-        if step + 1 == len(flips):
-            left, panel_slice = own_rows(work, own, received, size, blocks)
     any_space = pl.BlockSpec(memory_space=pl.ANY)
     schur = pl.pallas_call(
         functools.partial(tiles_kernel, tuple(reach)),

time: 139 us -> 151 us (1.086); the launches traced: 139 us -> 149 us
  waiting for transfers between devices: 26.7 us -> 32 us
  starting transfers between devices: 63.2 us -> 66.4 us
    ppermute x3, starting transfers between devices: 14.5 us -> 23.3 us  [on_device(): downward = lax.ppermute(downward, 'row', down)]
    ppermute x3, starting transfers between devices: 13.9 us -> 7.38 us  [on_device(): received = lax.ppermute(own, 'col', flips[step])]
    ppermute x3, waiting for transfers between devices: 1.5 us -> 8 us  [on_device(): downward = lax.ppermute(downward, 'row', down)]
    ppermute x1, waiting for transfers between devices: 0.01 us -> 5.42 us  [on_device(): other = lax.ppermute(near, ('row', 'col'), lift)]
    ppermute x1, waiting for transfers between devices: 4.02 us -> 0.01 us  [on_device(): first = lax.ppermute(mine, ('row', 'col'), turn)]
    ppermute x1, starting transfers between devices: 14.4 us -> 11.7 us  [on_device(): second = lax.ppermute(mine, ('row', 'col'), twin)]
    ppermute x4, waiting for transfers between devices: 21.1 us -> 18.5 us  [on_device(): upward = lax.ppermute(upward, 'row', up)]
    ppermute x4, starting transfers between devices: 7.89 us -> 9.58 us  [on_device(): upward = lax.ppermute(upward, 'row', up)]
  transfers between devices with their start and end apart: 14 -> 14, of which waited for: 5 -> 6; matrix products, arithmetic and copies ran while one was open for 0% -> 1% of each run, Pallas kernels for 28% -> 26%
where the time goes in v4:
time: 151 us; the launch traced here: 149 us
  starting transfers between devices  66.4 us (44%)
  Pallas kernels  47.1 us (31%)
  waiting for transfers between devices  32 us (21%)
    pallas_call x4, Pallas kernels, factor_step(): pl.pallas_call(functools.partial(factor_step_kernel, b), out_shape=jax.Sh...  32.7 us
    ppermute x3, starting transfers between devices, on_device(): downward = lax.ppermute(downward, 'row', down)  23.3 us
    ppermute x4, waiting for transfers between devices, on_device(): upward = lax.ppermute(upward, 'row', up)  18.5 us
    ppermute x1, starting transfers between devices, on_device(): second = lax.ppermute(mine, ('row', 'col'), twin)  11.7 us
    ppermute x4, starting transfers between devices, on_device(): upward = lax.ppermute(upward, 'row', up)  9.58 us
    pallas_call x1, Pallas kernels, on_device(): pl.pallas_call(functools.partial(tiles_kernel, tuple(reach)), out_shape=j...  8.28 us
    ppermute x3, waiting for transfers between devices, on_device(): downward = lax.ppermute(downward, 'row', down)  8 us
    ppermute x3, starting transfers between devices, on_device(): received = lax.ppermute(own, 'col', flips[step])  7.38 us
  transfers between devices with their start and end apart: 14, of which 6 were waited for; matrix products, arithmetic and copies ran while one was open for 1% of the time, Pallas kernels for 26%

profile of v4, /device:TPU:6, one launch (start us, length us, event | category | flops | bytes accessed | tf_op | source)
XLA Modules:
  0.0 148.6 jit_solution(6141992922798944170)
XLA Ops:
  0.6 6.6 %collective-permute-start = (f32[32,1024]{1,0:T(8,128)}, f32[32,1024]{1,0:T(8,128)S(1)}, u32[]{:S(2)}, u32[]{:S(2)}) collective-permute-start(f32[32,1024]{1,0:T(8,128)} %bitcast.5), channel_id=1, source_target_pairs={{0,0},{1,240},{2,16},{3,224},{4,32},{5,208},{6,48},{7,192},{8,64},... | collective-permute-start | bytes 393224 | tf_op jit(solution)/shard_map/ppermute | solution.py:256
  7.2 11.7 %collective-permute-start.1 = (f32[32,1024]{1,0:T(8,128)}, f32[32,1024]{1,0:T(8,128)S(1)}, u32[]{:S(2)}, u32[]{:S(2)}) collective-permute-start(f32[32,1024]{1,0:T(8,128)} %bitcast.6), channel_id=1, source_target_pairs={{0,128},{1,112},{2,144},{3,96},{4,160},{5,80},{6,176},{7,64},{8,19... | collective-permute-start | bytes 393224 | tf_op jit(solution)/shard_map/ppermute | solution.py:257
  18.9 8.6 %factor_step.4.a_ref = f32[512,512]{1,0:T(8,128)} custom-call(f32[512,512]{1,0:T(8,128)} %a_ref.1), custom_call_target="tpu_custom_call" | custom-call | tf_op jit(solution)/shard_map/factor_step/pallas_call | solution.py:104
  27.5 0.0 collective-permute-done
  27.5 0.0 collective-permute-done.1
  27.5 4.8 %collective-permute-start.2 = (f32[2,32,1024]{2,1,0:T(8,128)S(1)}, f32[2,32,1024]{2,1,0:T(8,128)S(1)}, u32[]{:S(2)}, u32[]{:S(2)}) collective-permute-start(f32[2,32,1024]{2,1,0:T(8,128)S(1)} %pad_maximum_fusion.1), channel_id=1, source_target_pairs={{0,256},{1,257},{2,258},{3,259},{4,260},{5,261},{6,262},{7,263},{8... | collective-permute-start | bytes 786440 | tf_op jit(solution)/shard_map/ppermute | solution.py:262
  32.4 5.4 %collective-permute-done.2 = f32[2,32,1024]{2,1,0:T(8,128)S(1)} collective-permute-done((f32[2,32,1024]{2,1,0:T(8,128)S(1)}, f32[2,32,1024]{2,1,0:T(8,128)S(1)}, u32[]{:S(2)}, u32[]{:S(2)}) %collective-permute-start.2) | collective-permute-done | bytes 262176 | tf_op jit(solution)/shard_map/ppermute | solution.py:262
  37.8 3.6 %collective-permute-start.3 = (f32[4,32,1024]{2,1,0:T(8,128)S(1)}, f32[4,32,1024]{2,1,0:T(8,128)S(1)}, u32[]{:S(2)}, u32[]{:S(2)}) collective-permute-start(f32[4,32,1024]{2,1,0:T(8,128)S(1)} %constant_dynamic-update-slice_fusion.refs_0_), channel_id=1, source_target_pairs={{0,16},{16,32},{32,48},{48,64},{64,80},{80,96},{96,112},{112,128},... | collective-permute-start | bytes 1572872 | tf_op jit(solution)/shard_map/ppermute | solution.py:270
  41.5 5.8 %collective-permute-start.4 = (f32[4,32,1024]{2,1,0:T(8,128)S(1)}, f32[4,32,1024]{2,1,0:T(8,128)S(1)}, u32[]{:S(2)}, u32[]{:S(2)}) collective-permute-start(f32[4,32,1024]{2,1,0:T(8,128)S(1)} %constant_dynamic-update-slice_fusion.refs_0_), channel_id=1, source_target_pairs={{0,240},{16,0},{32,16},{48,32},{64,48},{80,64},{96,80},{112,96},{1... | collective-permute-start | bytes 1572872 | tf_op jit(solution)/shard_map/ppermute | solution.py:272
  47.3 3.1 %collective-permute-start.5 = (f32[32,1024]{1,0:T(8,128)S(1)}, f32[32,1024]{1,0:T(8,128)S(1)}, u32[]{:S(2)}, u32[]{:S(2)}) collective-permute-start(f32[32,1024]{1,0:T(8,128)S(1)} %bitcast.7), channel_id=1, source_target_pairs={{0,4},{1,5},{2,6},{3,7},{4,0},{5,1},{6,2},{7,3},{8,12},{9,13},{10,... | collective-permute-start | bytes 393224 | tf_op jit(solution)/shard_map/ppermute | solution.py:263
  50.4 8.3 %factor_step.5.a_ref = f32[512,512]{1,0:T(8,128)} custom-call(f32[512,512]{1,0:T(8,128)} %factor_step.4.a_ref), custom_call_target="tpu_custom_call" | custom-call | tf_op jit(solution)/shard_map/factor_step/pallas_call | solution.py:104
  58.7 3.6 %collective-permute-start.8 = (f32[64,1024]{1,0:T(8,128)S(1)}, f32[64,1024]{1,0:T(8,128)S(1)}, u32[]{:S(2)}, u32[]{:S(2)}) collective-permute-start(f32[64,1024]{1,0:T(8,128)S(1)} %pad_maximum_fusion.2), channel_id=1, source_target_pairs={{0,2},{1,3},{2,0},{3,1},{4,6},{5,7},{6,4},{7,5},{8,10},{9,11},{10,... | collective-permute-start | bytes 786440 | tf_op jit(solution)/shard_map/ppermute | solution.py:277
  62.2 0.0 collective-permute-done.3.refs_1_
  62.3 8.5 %factor_step.6.a_ref = f32[512,512]{1,0:T(8,128)} custom-call(f32[512,512]{1,0:T(8,128)} %factor_step.5.a_ref), custom_call_target="tpu_custom_call" | custom-call | tf_op jit(solution)/shard_map/factor_step/pallas_call | solution.py:104
  70.8 1.9 %collective-permute-start.6 = (f32[4,32,1024]{2,1,0:T(8,128)S(1)}, f32[4,32,1024]{2,1,0:T(8,128)}, u32[]{:S(2)}, u32[]{:S(2)}) collective-permute-start(f32[4,32,1024]{2,1,0:T(8,128)S(1)} %collective-permute-done.3.refs_1_), channel_id=1, source_target_pairs={{0,16},{16,32},{32,48},{48,64},{64,80},{80,96},{96,112},{112,128},... | collective-permute-start | bytes 1572872 | tf_op jit(solution)/shard_map/ppermute | solution.py:270
  72.7 11.8 %collective-permute-start.7 = (f32[4,32,1024]{2,1,0:T(8,128)S(1)}, f32[4,32,1024]{2,1,0:T(8,128)}, u32[]{:S(2)}, u32[]{:S(2)}) collective-permute-start(f32[4,32,1024]{2,1,0:T(8,128)S(1)} %collective-permute-done.4.refs_2_), channel_id=1, source_target_pairs={{0,240},{16,0},{32,16},{48,32},{64,48},{80,64},{96,80},{112,96},{1... | collective-permute-start | bytes 1572872 | tf_op jit(solution)/shard_map/ppermute | solution.py:272
  84.5 0.8 pad_maximum_fusion
  85.3 1.9 %collective-permute-start.11 = (f32[128,1024]{1,0:T(8,128)}, f32[128,1024]{1,0:T(8,128)S(1)}, u32[]{:S(2)}, u32[]{:S(2)}) collective-permute-start(f32[128,1024]{1,0:T(8,128)} %pad_maximum_fusion), channel_id=1, source_target_pairs={{0,8},{1,9},{2,10},{3,11},{4,12},{5,13},{6,14},{7,15},{8,0},{9,1},... | collective-permute-start | bytes 1572872 | tf_op jit(solution)/shard_map/ppermute | solution.py:277
  87.3 7.5 %collective-permute-done.6.refs_3_ = f32[4,32,1024]{2,1,0:T(8,128)} collective-permute-done((f32[4,32,1024]{2,1,0:T(8,128)S(1)}, f32[4,32,1024]{2,1,0:T(8,128)}, u32[]{:S(2)}, u32[]{:S(2)}) %collective-permute-start.6) | collective-permute-done | bytes 524320 | tf_op jit(solution)/shard_map/ppermute | solution.py:270
  94.8 1.1 collective-permute-done.7.refs_4_
  95.9 7.4 %factor_step.7.inverse_ref = f32[512,512]{1,0:T(8,128)} custom-call(f32[512,512]{1,0:T(8,128)} %factor_step.6.a_ref), custom_call_target="tpu_custom_call" | custom-call | tf_op jit(solution)/shard_map/factor_step/pallas_call | solution.py:104
  103.2 5.7 %collective-permute-start.10 = (f32[4,32,1024]{2,1,0:T(8,128)}, f32[4,32,1024]{2,1,0:T(8,128)S(1)}, u32[]{:S(2)}, u32[]{:S(2)}) collective-permute-start(f32[4,32,1024]{2,1,0:T(8,128)} %collective-permute-done.7.refs_4_), channel_id=1, source_target_pairs={{0,240},{16,0},{32,16},{48,32},{64,48},{80,64},{96,80},{112,96},{1... | collective-permute-start | bytes 1572872 | tf_op jit(solution)/shard_map/ppermute | solution.py:272
  108.9 1.9 %collective-permute-start.9 = (f32[4,32,1024]{2,1,0:T(8,128)}, f32[4,32,1024]{2,1,0:T(8,128)S(1)}, u32[]{:S(2)}, u32[]{:S(2)}) collective-permute-start(f32[4,32,1024]{2,1,0:T(8,128)} %collective-permute-done.6.refs_3_), channel_id=1, source_target_pairs={{0,16},{16,32},{32,48},{48,64},{64,80},{80,96},{96,112},{112,128},... | collective-permute-start | bytes 1572872 | tf_op jit(solution)/shard_map/ppermute | solution.py:270
  110.9 0.0 copy-start
  110.9 1.9 %collective-permute-start.13 = (f32[256,1024]{1,0:T(8,128)S(1)}, f32[256,1024]{1,0:T(8,128)S(1)}, u32[]{:S(2)}, u32[]{:S(2)}) collective-permute-start(f32[256,1024]{1,0:T(8,128)S(1)} %constant_dynamic-update-slice_fusion.2.panel_ref), channel_id=1, source_target_pairs={{0,1},{1,0},{2,3},{3,2},{4,5},{5,4},{6,7},{7,6},{8,9},{9,8},{10,11... | collective-permute-start | bytes 3145736 | tf_op jit(solution)/shard_map/ppermute | solution.py:277
  112.8 6.9 %collective-permute-done.10.refs_6_ = f32[4,32,1024]{2,1,0:T(8,128)S(1)} collective-permute-done((f32[4,32,1024]{2,1,0:T(8,128)}, f32[4,32,1024]{2,1,0:T(8,128)S(1)}, u32[]{:S(2)}, u32[]{:S(2)}) %collective-permute-start.10) | collective-permute-done | bytes 524320 | tf_op jit(solution)/shard_map/ppermute | solution.py:272
  119.8 5.2 %collective-permute-done.9.refs_5_ = f32[4,32,1024]{2,1,0:T(8,128)S(1)} collective-permute-done((f32[4,32,1024]{2,1,0:T(8,128)}, f32[4,32,1024]{2,1,0:T(8,128)S(1)}, u32[]{:S(2)}, u32[]{:S(2)}) %collective-permute-start.9) | collective-permute-done | bytes 524320 | tf_op jit(solution)/shard_map/ppermute | solution.py:270
  125.0 2.1 %collective-permute-start.12 = (f32[4,32,1024]{2,1,0:T(8,128)S(1)}, f32[4,32,1024]{2,1,0:T(8,128)}, u32[]{:S(2)}, u32[]{:S(2)}) collective-permute-start(f32[4,32,1024]{2,1,0:T(8,128)S(1)} %collective-permute-done.9.refs_5_), channel_id=1, source_target_pairs={{0,16},{16,32},{32,48},{48,64},{64,80},{80,96},{96,112},{112,128},... | collective-permute-start | bytes 1572872 | tf_op jit(solution)/shard_map/ppermute | solution.py:270
  127.2 1.0 copy-done.3
  128.1 6.1 %own_rows.1 = (bf16[8,256,512]{2,1,0:T(8,128)(2,1)}, f32[32,1024]{1,0:T(8,128)}) custom-call(f32[512,512]{1,0:T(8,128)} %factor_step.7.inverse_ref, f32[256,1024]{1,0:T(8,128)} %copy-done, f32[256,1024]{1,0:T(8,128)} %copy-done.3), custom_call_target="tpu_custom_call" | custom-call | tf_op jit(solution)/shard_map/own_rows/pallas_call | solution.py:311
  134.2 5.8 %collective-permute-done.12.refs_7_ = f32[4,32,1024]{2,1,0:T(8,128)} collective-permute-done((f32[4,32,1024]{2,1,0:T(8,128)S(1)}, f32[4,32,1024]{2,1,0:T(8,128)}, u32[]{:S(2)}, u32[]{:S(2)}) %collective-permute-start.12) | collective-permute-done | bytes 524320 | tf_op jit(solution)/shard_map/ppermute | solution.py:270
  140.1 8.3 %schur_tiles.1 = f32[28,128,128]{2,1,0:T(8,128)} custom-call(s32[2,28]{1,0:T(2,128)} %bitcast.13, bf16[8,256,512]{2,1,0:T(8,128)(2,1)} %get-tuple-element.51.left_hbm, f32[28,128,128]{2,1,0:T(8,128)} %tiles_hbm.1, f32[4,32,1024]{2,1,0:T(8,128)} %copy-done.1, f32[4,32,1024]{2,1,0:T(8,128)} %copy-done.4, f32[4,32,1024]{2,1,0:T(8,128)} %copy-done.5, ...), custom_call_target="tpu_custom_call" | custom-call | tf_op jit(solution)/shard_map/schur_tiles/pallas_call | solution.py:289
  (27 shorter events, 0.2 us)
Async XLA Ops:
  0.6 46.6 %copy-start.2 = (f32[1024,32]{0,1:T(8,128)S(1)}, f32[1024,32]{0,1:T(8,128)}, u32[]{:S(2)}) copy-start(f32[1024,32]{0,1:T(8,128)} %param.5) | copy-start | bytes 393220
  0.6 26.9 %collective-permute-start = (f32[32,1024]{1,0:T(8,128)}, f32[32,1024]{1,0:T(8,128)S(1)}, u32[]{:S(2)}, u32[]{:S(2)}) collective-permute-start(f32[32,1024]{1,0:T(8,128)} %bitcast.5), channel_id=1, source_target_pairs={{0,0},{1,240},{2,16},{3,224},{4,32},{5,208},{6,48},{7,192},{8,64},... | collective-permute-start | bytes 393224 | tf_op jit(solution)/shard_map/ppermute | solution.py:256
  7.2 20.3 %collective-permute-start.1 = (f32[32,1024]{1,0:T(8,128)}, f32[32,1024]{1,0:T(8,128)S(1)}, u32[]{:S(2)}, u32[]{:S(2)}) collective-permute-start(f32[32,1024]{1,0:T(8,128)} %bitcast.6), channel_id=1, source_target_pairs={{0,128},{1,112},{2,144},{3,96},{4,160},{5,80},{6,176},{7,64},{8,19... | collective-permute-start | bytes 393224 | tf_op jit(solution)/shard_map/ppermute | solution.py:257
  27.5 10.2 %collective-permute-start.2 = (f32[2,32,1024]{2,1,0:T(8,128)S(1)}, f32[2,32,1024]{2,1,0:T(8,128)S(1)}, u32[]{:S(2)}, u32[]{:S(2)}) collective-permute-start(f32[2,32,1024]{2,1,0:T(8,128)S(1)} %pad_maximum_fusion.1), channel_id=1, source_target_pairs={{0,256},{1,257},{2,258},{3,259},{4,260},{5,261},{6,262},{7,263},{8... | collective-permute-start | bytes 786440 | tf_op jit(solution)/shard_map/ppermute | solution.py:262
  37.8 32.9 %copy-start.1 = (f32[4,32,1024]{2,1,0:T(8,128)}, f32[4,32,1024]{2,1,0:T(8,128)S(1)}, u32[]{:S(2)}) copy-start(f32[4,32,1024]{2,1,0:T(8,128)S(1)} %constant_dynamic-update-slice_fusion.refs_0_) | copy-start | bytes 1572868
  37.8 24.4 %collective-permute-start.3 = (f32[4,32,1024]{2,1,0:T(8,128)S(1)}, f32[4,32,1024]{2,1,0:T(8,128)S(1)}, u32[]{:S(2)}, u32[]{:S(2)}) collective-permute-start(f32[4,32,1024]{2,1,0:T(8,128)S(1)} %constant_dynamic-update-slice_fusion.refs_0_), channel_id=1, source_target_pairs={{0,16},{16,32},{32,48},{48,64},{64,80},{80,96},{96,112},{112,128},... | collective-permute-start | bytes 1572872 | tf_op jit(solution)/shard_map/ppermute | solution.py:270
  41.5 20.8 %collective-permute-start.4 = (f32[4,32,1024]{2,1,0:T(8,128)S(1)}, f32[4,32,1024]{2,1,0:T(8,128)S(1)}, u32[]{:S(2)}, u32[]{:S(2)}) collective-permute-start(f32[4,32,1024]{2,1,0:T(8,128)S(1)} %constant_dynamic-update-slice_fusion.refs_0_), channel_id=1, source_target_pairs={{0,240},{16,0},{32,16},{48,32},{64,48},{80,64},{96,80},{112,96},{1... | collective-permute-start | bytes 1572872 | tf_op jit(solution)/shard_map/ppermute | solution.py:272
  47.3 11.4 %collective-permute-start.5 = (f32[32,1024]{1,0:T(8,128)S(1)}, f32[32,1024]{1,0:T(8,128)S(1)}, u32[]{:S(2)}, u32[]{:S(2)}) collective-permute-start(f32[32,1024]{1,0:T(8,128)S(1)} %bitcast.7), channel_id=1, source_target_pairs={{0,4},{1,5},{2,6},{3,7},{4,0},{5,1},{6,2},{7,3},{8,12},{9,13},{10,... | collective-permute-start | bytes 393224 | tf_op jit(solution)/shard_map/ppermute | solution.py:263
  58.7 12.1 %collective-permute-start.8 = (f32[64,1024]{1,0:T(8,128)S(1)}, f32[64,1024]{1,0:T(8,128)S(1)}, u32[]{:S(2)}, u32[]{:S(2)}) collective-permute-start(f32[64,1024]{1,0:T(8,128)S(1)} %pad_maximum_fusion.2), channel_id=1, source_target_pairs={{0,2},{1,3},{2,0},{3,1},{4,6},{5,7},{6,4},{7,5},{8,10},{9,11},{10,... | collective-permute-start | bytes 786440 | tf_op jit(solution)/shard_map/ppermute | solution.py:277
  62.2 25.0 %copy-start.4 = (f32[4,32,1024]{2,1,0:T(8,128)}, f32[4,32,1024]{2,1,0:T(8,128)S(1)}, u32[]{:S(2)}) copy-start(f32[4,32,1024]{2,1,0:T(8,128)S(1)} %collective-permute-done.3.refs_1_) | copy-start | bytes 1572868
  62.3 25.0 %copy-start.5 = (f32[4,32,1024]{2,1,0:T(8,128)}, f32[4,32,1024]{2,1,0:T(8,128)S(1)}, u32[]{:S(2)}) copy-start(f32[4,32,1024]{2,1,0:T(8,128)S(1)} %collective-permute-done.4.refs_2_) | copy-start | bytes 1572868
  70.8 24.0 %collective-permute-start.6 = (f32[4,32,1024]{2,1,0:T(8,128)S(1)}, f32[4,32,1024]{2,1,0:T(8,128)}, u32[]{:S(2)}, u32[]{:S(2)}) collective-permute-start(f32[4,32,1024]{2,1,0:T(8,128)S(1)} %collective-permute-done.3.refs_1_), channel_id=1, source_target_pairs={{0,16},{16,32},{32,48},{48,64},{64,80},{80,96},{96,112},{112,128},... | collective-permute-start | bytes 1572872 | tf_op jit(solution)/shard_map/ppermute | solution.py:270
  72.7 23.2 %collective-permute-start.7 = (f32[4,32,1024]{2,1,0:T(8,128)S(1)}, f32[4,32,1024]{2,1,0:T(8,128)}, u32[]{:S(2)}, u32[]{:S(2)}) collective-permute-start(f32[4,32,1024]{2,1,0:T(8,128)S(1)} %collective-permute-done.4.refs_2_), channel_id=1, source_target_pairs={{0,240},{16,0},{32,16},{48,32},{64,48},{80,64},{96,80},{112,96},{1... | collective-permute-start | bytes 1572872 | tf_op jit(solution)/shard_map/ppermute | solution.py:272
  85.3 17.9 %collective-permute-start.11 = (f32[128,1024]{1,0:T(8,128)}, f32[128,1024]{1,0:T(8,128)S(1)}, u32[]{:S(2)}, u32[]{:S(2)}) collective-permute-start(f32[128,1024]{1,0:T(8,128)} %pad_maximum_fusion), channel_id=1, source_target_pairs={{0,8},{1,9},{2,10},{3,11},{4,12},{5,13},{6,14},{7,15},{8,0},{9,1},... | collective-permute-start | bytes 1572872 | tf_op jit(solution)/shard_map/ppermute | solution.py:277
  103.2 16.5 %collective-permute-start.10 = (f32[4,32,1024]{2,1,0:T(8,128)}, f32[4,32,1024]{2,1,0:T(8,128)S(1)}, u32[]{:S(2)}, u32[]{:S(2)}) collective-permute-start(f32[4,32,1024]{2,1,0:T(8,128)} %collective-permute-done.7.refs_4_), channel_id=1, source_target_pairs={{0,240},{16,0},{32,16},{48,32},{64,48},{80,64},{96,80},{112,96},{1... | collective-permute-start | bytes 1572872 | tf_op jit(solution)/shard_map/ppermute | solution.py:272
  108.9 16.1 %collective-permute-start.9 = (f32[4,32,1024]{2,1,0:T(8,128)}, f32[4,32,1024]{2,1,0:T(8,128)S(1)}, u32[]{:S(2)}, u32[]{:S(2)}) collective-permute-start(f32[4,32,1024]{2,1,0:T(8,128)} %collective-permute-done.6.refs_3_), channel_id=1, source_target_pairs={{0,16},{16,32},{32,48},{48,64},{64,80},{80,96},{96,112},{112,128},... | collective-permute-start | bytes 1572872 | tf_op jit(solution)/shard_map/ppermute | solution.py:270
  110.9 16.2 %copy-start = (f32[256,1024]{1,0:T(8,128)}, f32[256,1024]{1,0:T(8,128)S(1)}, u32[]{:S(2)}) copy-start(f32[256,1024]{1,0:T(8,128)S(1)} %constant_dynamic-update-slice_fusion.2.panel_ref) | copy-start | bytes 3145732
  110.9 16.2 %collective-permute-start.13 = (f32[256,1024]{1,0:T(8,128)S(1)}, f32[256,1024]{1,0:T(8,128)S(1)}, u32[]{:S(2)}, u32[]{:S(2)}) collective-permute-start(f32[256,1024]{1,0:T(8,128)S(1)} %constant_dynamic-update-slice_fusion.2.panel_ref), channel_id=1, source_target_pairs={{0,1},{1,0},{2,3},{3,2},{4,5},{5,4},{6,7},{7,6},{8,9},{9,8},{10,11... | collective-permute-start | bytes 3145736 | tf_op jit(solution)/shard_map/ppermute | solution.py:277
  119.8 20.3 %copy-start.6 = (f32[4,32,1024]{2,1,0:T(8,128)}, f32[4,32,1024]{2,1,0:T(8,128)S(1)}, u32[]{:S(2)}) copy-start(f32[4,32,1024]{2,1,0:T(8,128)S(1)} %collective-permute-done.10.refs_6_) | copy-start | bytes 1572868
  125.0 15.1 %copy-start.7 = (f32[4,32,1024]{2,1,0:T(8,128)}, f32[4,32,1024]{2,1,0:T(8,128)S(1)}, u32[]{:S(2)}) copy-start(f32[4,32,1024]{2,1,0:T(8,128)S(1)} %collective-permute-done.9.refs_5_) | copy-start | bytes 1572868
  125.0 15.1 %collective-permute-start.12 = (f32[4,32,1024]{2,1,0:T(8,128)S(1)}, f32[4,32,1024]{2,1,0:T(8,128)}, u32[]{:S(2)}, u32[]{:S(2)}) collective-permute-start(f32[4,32,1024]{2,1,0:T(8,128)S(1)} %collective-permute-done.9.refs_5_), channel_id=1, source_target_pairs={{0,16},{16,32},{32,48},{48,64},{64,80},{80,96},{96,112},{112,128},... | collective-permute-start | bytes 1572872 | tf_op jit(solution)/shard_map/ppermute | solution.py:270
  127.2 1.0 copy-start.3

commit v5 on v4

--- a/solution.py
+++ b/solution.py
@@ -7,7 +7,7 @@
 from jax.experimental.pallas import tpu as pltpu
 from jax.sharding import PartitionSpec as P
 
-W, B, G, UNROLL = 512, 128, 8, 4
+W, B, G, UNROLL, COPIES = 512, 128, 8, 4, 4
 HI = lax.Precision.HIGHEST
 
 
@@ -170,26 +170,32 @@
 
 def tiles_kernel(reach, targets_ref, left_hbm, tiles_hbm, *refs):
     pieces, (out_hbm, left, far, tiles, out, right, in_sem, far_sem, out_sem) = refs[:len(reach)], refs[len(reach):]
-    blocks, size = left.shape[0], far.shape[2]
+    blocks, size = left.shape[0], far.shape[1]
     count = out.shape[0]
     col, row = lax.axis_index("col"), lax.axis_index("row")
     n_cols = lax.axis_size("col")
     side = lax.div(row, n_cols)
-    far_copies = [pltpu.make_async_copy(piece, far.at[i], far_sem.at[i]) for i, piece in enumerate(pieces)]
+    starts = [0]
+    for piece in pieces:
+        starts.append(starts[-1] + piece.shape[0])
+    far_copies = [
+        pltpu.make_async_copy(piece, far.at[pl.ds(starts[i], piece.shape[0])], far_sem.at[i])
+        for i, piece in enumerate(pieces)
+    ]
     left_copy = pltpu.make_async_copy(left_hbm, left, in_sem.at[0])
     tiles_copy = pltpu.make_async_copy(tiles_hbm, tiles, in_sem.at[1])
     for copy in far_copies:
         copy.start()
     left_copy.start()
     tiles_copy.start()
-    for i, away in enumerate(reach):
+    for i, (away, parts) in enumerate(reach):
         far_copies[i].wait()
-        for part in range(far.shape[1]):
-            twin, slot = part % 2, part // 2
-            apart = lax.rem(row + away - col - twin * (n_cols // 2) + 4 * n_cols, n_cols)
+        for place, part in enumerate(parts):
+            copied, slot = part % COPIES, part // COPIES
+            apart = lax.rem(row + away - col - copied * (n_cols // COPIES) + 4 * n_cols, n_cols)
             k = jnp.where(apart < n_cols // 2, 2 * apart, 2 * n_cols - 1 - 2 * apart)
             to = pl.ds(pl.multiple_of(k * size, size), size)
-            high, low = halves(far[i, part])
+            high, low = halves(far[starts[i] + place])
             for block in range(blocks):
                 right[slot * blocks + block, to, :B] = high[:, block * B:(block + 1) * B]
                 right[slot * blocks + block, to, B:] = low[:, block * B:(block + 1) * B]
@@ -233,7 +239,6 @@
     size, rows = panel.shape[1], panel.shape[0]
     blocks, count = rows // B, tiles.shape[0]
     mine = panel.T
-    half = n_cols // 2
     together = lax.optimization_barrier
 
     def at(r, c):
@@ -246,54 +251,56 @@
         return c // 2 if c % 2 == 0 else n_cols - 1 - c // 2
 
     everyone = [(r, c) for r in range(n_rows) for c in range(n_cols)]
-    turn = [(at(r, c), at(moved(r, spread(c)), r % n_cols)) for r, c in everyone]
-    twin = [(at(r, c), at(moved(r, spread(c) + half), r % n_cols)) for r, c in everyone]
     lift = [(at(r, c), at(r + n_cols, c)) for r, c in everyone if r < n_cols]
     up = [(r, moved(r, 1)) for r in range(n_rows)]
     down = [(r, moved(r, -1)) for r in range(n_rows)]
     flips = [[(c, c ^ flip) for c in range(n_cols)] for flip in (n_cols // 4, n_cols // 8, n_cols // 2, 1)]
 
-    first = lax.ppermute(mine, ("row", "col"), turn)
-    second = lax.ppermute(mine, ("row", "col"), twin)
+    near = []
+    for copied in range(COPIES):
+        apart = copied * (n_cols // COPIES)
+        pairs = [(at(r, c), at(moved(r, spread(c) + apart), r % n_cols)) for r, c in everyone]
+        near.append(lax.ppermute(mine, ("row", "col"), pairs))
+    own = mine
+    received = lax.ppermute(own, "col", flips[0])
     work = factor_step(0, diag_block)
-    first, second, work, own = together((first, second, work, mine))
-
-    near = jnp.stack([first, second])
+    received, work = together((received, work))
+    own = jnp.concatenate([own, received])
+    received = lax.ppermute(own, "col", flips[1])
+    work = factor_step(1, work)
+    near, work = together((near, work))
+
+    near = jnp.stack(near)
     other = lax.ppermute(near, ("row", "col"), lift)
-    received = lax.ppermute(own, "col", flips[0])
-    near, other, work = together((near, other, work))
+    work = factor_step(2, work)
+    near, other, work, received = together((near, other, work, received))
 
     base = jnp.concatenate([near, other])
-    upward, downward, pieces, reach = base, base, [base], [0]
-    for step in range(1, half // 2 + 1):
-        both = step < half // 2
-        upward = lax.ppermute(upward, "row", up)
-        if both:
-            downward = lax.ppermute(downward, "row", down)
-        if step < W // B:
-            work = factor_step(step, work)
-            received, work = together((received, work))
-            own = jnp.concatenate([own, received])
-            received = lax.ppermute(own, "col", flips[step])
-            if step + 1 == W // B:
-                left, panel_slice = own_rows(work, own, received, size, blocks)
-            upward, downward, work = together((upward, downward, work))
-        else:
-            upward, left, panel_slice = together((upward, left, panel_slice))
-        pieces.append(upward)
-        reach.append(-step)
-        if both:
-            pieces.append(downward)
-            reach.append(step)
+    own = jnp.concatenate([own, received])
+    upward = lax.ppermute(base, "row", up)
+    downward = lax.ppermute(base, "row", down)
+    received = lax.ppermute(own, "col", flips[2])
+    work = factor_step(3, work)
+    received, work = together((received, work))
+    own = jnp.concatenate([own, received])
+    received = lax.ppermute(own, "col", flips[3])
+    left, panel_slice = own_rows(work, own, received, size, blocks)
+    upward, downward, left, panel_slice = together((upward, downward, left, panel_slice))
+
+    last_up = lax.ppermute(upward[:COPIES], "row", up)
+    last_down = lax.ppermute(downward[COPIES:], "row", down)
+    whole = tuple(range(2 * COPIES))
+    pieces = [base, upward, downward, last_up, last_down]
+    reach = ((0, whole), (-1, whole), (1, whole), (-2, whole[:COPIES]), (2, whole[COPIES:]))
     any_space = pl.BlockSpec(memory_space=pl.ANY)
     schur = pl.pallas_call(
-        functools.partial(tiles_kernel, tuple(reach)),
+        functools.partial(tiles_kernel, reach),
         out_shape=jax.ShapeDtypeStruct(tiles.shape, F32),
         in_specs=[pl.BlockSpec(memory_space=pltpu.SMEM), *[any_space] * (2 + len(pieces))],
         out_specs=any_space,
         scratch_shapes=[
             pltpu.VMEM(left.shape, BF),
-            pltpu.VMEM((len(pieces), *base.shape), F32),
+            pltpu.VMEM((sum(piece.shape[0] for piece in pieces), size, rows), F32),
             pltpu.VMEM(tiles.shape, F32),
             pltpu.VMEM(tiles.shape, F32),
             pltpu.VMEM((2 * blocks, W, 2 * B), BF),

time: 151 us -> 149 us (0.987)
  starting transfers between devices: 66.4 us -> 57.7 us
  waiting for transfers between devices: 32 us -> 38.9 us
    ppermute x12 -> x11, waiting for transfers between devices: 26.6 us -> 38.6 us  [the longest x1 15.7 us: on_device(): downward = lax.ppermute(base, 'row', down)]
    ppermute x12 -> x11, starting transfers between devices: 58.5 us -> 49.3 us  [the longest x4 31.6 us: on_device(): near.append(lax.ppermute(mine, ('row', 'col'), pairs))]
    ppermute x1, waiting for transfers between devices: 5.42 us -> 0.22 us  [on_device(): other = lax.ppermute(near, ('row', 'col'), lift)]
  transfers between devices with their start and end apart: 14 -> 13, of which waited for: 6 -> 7; matrix products, arithmetic and copies ran while one was open for 1% -> 1% of each run, Pallas kernels for 26% -> 26%
where the time goes in v5:
time: 149 us; the launch traced here: 147 us
  starting transfers between devices  57.7 us (39%)
  Pallas kernels  46.7 us (31%)
  waiting for transfers between devices  38.9 us (26%)
  local copies, waits for them, and re-layouts  2.59 us (2%)
    pallas_call x4, Pallas kernels, factor_step(): pl.pallas_call(functools.partial(factor_step_kernel, b), out_shape=jax.Sh...  32.3 us
    ppermute x4, starting transfers between devices, on_device(): near.append(lax.ppermute(mine, ('row', 'col'), pairs))  31.6 us
    ppermute x1, waiting for transfers between devices, on_device(): downward = lax.ppermute(base, 'row', down)  15.7 us
    ppermute x1, waiting for transfers between devices, on_device(): last_down = lax.ppermute(downward[COPIES:], 'row', down)  9.32 us
    pallas_call x1, Pallas kernels, on_device(): pl.pallas_call(functools.partial(tiles_kernel, reach), out_shape=jax.Shap...  8.24 us
    pallas_call x1, Pallas kernels, own_rows(): pl.pallas_call(own_kernel, out_shape=(jax.ShapeDtypeStruct((blocks, 2 * B...  6.13 us
    ppermute x1, starting transfers between devices, on_device(): other = lax.ppermute(near, ('row', 'col'), lift)  5.1 us
    ppermute x1, waiting for transfers between devices, on_device(): received = lax.ppermute(own, 'col', flips[2])  4.32 us
  transfers between devices with their start and end apart: 13, of which 7 were waited for; matrix products, arithmetic and copies ran while one was open for 1% of the time, Pallas kernels for 26%

profile of v5, /device:TPU:6, one launch (start us, length us, event | category | flops | bytes accessed | tf_op | source)
XLA Modules:
  0.0 147.0 jit_solution(2724361759570207082)
XLA Ops:
  0.6 3.3 %collective-permute-start.4 = (f32[32,1024]{1,0:T(8,128)}, f32[32,1024]{1,0:T(8,128)S(1)}, u32[]{:S(2)}, u32[]{:S(2)}) collective-permute-start(f32[32,1024]{1,0:T(8,128)} %bitcast.7), channel_id=1, source_target_pairs={{0,4},{1,5},{2,6},{3,7},{4,0},{5,1},{6,2},{7,3},{8,12},{9,13},{10,... | collective-permute-start | bytes 393224 | tf_op jit(solution)/shard_map/ppermute | solution.py:265
  4.0 12.9 %collective-permute-start.3 = (f32[32,1024]{1,0:T(8,128)}, f32[32,1024]{1,0:T(8,128)S(1)}, u32[]{:S(2)}, u32[]{:S(2)}) collective-permute-start(f32[32,1024]{1,0:T(8,128)} %bitcast.8), channel_id=1, source_target_pairs={{0,192},{1,176},{2,208},{3,160},{4,224},{5,144},{6,240},{7,128},{8... | collective-permute-start | bytes 393224 | tf_op jit(solution)/shard_map/ppermute | solution.py:263
  16.9 6.5 %collective-permute-start.2 = (f32[32,1024]{1,0:T(8,128)}, f32[32,1024]{1,0:T(8,128)S(1)}, u32[]{:S(2)}, u32[]{:S(2)}) collective-permute-start(f32[32,1024]{1,0:T(8,128)} %bitcast.9), channel_id=1, source_target_pairs={{0,128},{1,112},{2,144},{3,96},{4,160},{5,80},{6,176},{7,64},{8,19... | collective-permute-start | bytes 393224 | tf_op jit(solution)/shard_map/ppermute | solution.py:263
  23.4 10.2 %collective-permute-start.1 = (f32[32,1024]{1,0:T(8,128)}, f32[32,1024]{1,0:T(8,128)S(1)}, u32[]{:S(2)}, u32[]{:S(2)}) collective-permute-start(f32[32,1024]{1,0:T(8,128)} %bitcast.10), channel_id=1, source_target_pairs={{0,64},{1,48},{2,80},{3,32},{4,96},{5,16},{6,112},{7,0},{8,128},{9... | collective-permute-start | bytes 393224 | tf_op jit(solution)/shard_map/ppermute | solution.py:263
  33.7 1.9 %collective-permute-start = (f32[32,1024]{1,0:T(8,128)}, f32[32,1024]{1,0:T(8,128)S(1)}, u32[]{:S(2)}, u32[]{:S(2)}) collective-permute-start(f32[32,1024]{1,0:T(8,128)} %bitcast.11), channel_id=1, source_target_pairs={{0,0},{1,240},{2,16},{3,224},{4,32},{5,208},{6,48},{7,192},{8,64},... | collective-permute-start | bytes 393224 | tf_op jit(solution)/shard_map/ppermute | solution.py:263
  35.6 8.6 %factor_step.4.a_ref = f32[512,512]{1,0:T(8,128)} custom-call(f32[512,512]{1,0:T(8,128)} %a_ref.1), custom_call_target="tpu_custom_call" | custom-call | tf_op jit(solution)/shard_map/factor_step/pallas_call | solution.py:104
  44.2 8.3 %factor_step.5.a_ref = f32[512,512]{1,0:T(8,128)} custom-call(f32[512,512]{1,0:T(8,128)} %factor_step.4.a_ref), custom_call_target="tpu_custom_call" | custom-call | tf_op jit(solution)/shard_map/factor_step/pallas_call | solution.py:104
  52.5 0.0 collective-permute-done.2
  52.5 2.5 %collective-permute-done = f32[32,1024]{1,0:T(8,128)S(1)} collective-permute-done((f32[32,1024]{1,0:T(8,128)}, f32[32,1024]{1,0:T(8,128)S(1)}, u32[]{:S(2)}, u32[]{:S(2)}) %collective-permute-start) | collective-permute-done | bytes 131104 | tf_op jit(solution)/shard_map/ppermute | solution.py:263
  55.1 5.1 %collective-permute-start.5 = (f32[4,32,1024]{2,1,0:T(8,128)S(1)}, f32[4,32,1024]{2,1,0:T(8,128)S(1)}, u32[]{:S(2)}, u32[]{:S(2)}) collective-permute-start(f32[4,32,1024]{2,1,0:T(8,128)S(1)} %pad_maximum_fusion.1), channel_id=1, source_target_pairs={{0,256},{1,257},{2,258},{3,259},{4,260},{5,261},{6,262},{7,263},{8... | collective-permute-start | bytes 1572872 | tf_op jit(solution)/shard_map/ppermute | solution.py:274
  60.2 2.1 %collective-permute-start.6 = (f32[64,1024]{1,0:T(8,128)S(1)}, f32[64,1024]{1,0:T(8,128)S(1)}, u32[]{:S(2)}, u32[]{:S(2)}) collective-permute-start(f32[64,1024]{1,0:T(8,128)S(1)} %pad_maximum_fusion.3), channel_id=1, source_target_pairs={{0,2},{1,3},{2,0},{3,1},{4,6},{5,7},{6,4},{7,5},{8,10},{9,11},{10,... | collective-permute-start | bytes 786440 | tf_op jit(solution)/shard_map/ppermute | solution.py:269
  62.3 8.1 %factor_step.6.a_ref = f32[512,512]{1,0:T(8,128)} custom-call(f32[512,512]{1,0:T(8,128)} %factor_step.5.a_ref), custom_call_target="tpu_custom_call" | custom-call | tf_op jit(solution)/shard_map/factor_step/pallas_call | solution.py:104
  70.4 0.2 collective-permute-done.5
  70.7 1.9 %collective-permute-start.9 = (f32[128,1024]{1,0:T(8,128)S(1)}, f32[128,1024]{1,0:T(8,128)S(1)}, u32[]{:S(2)}, u32[]{:S(2)}) collective-permute-start(f32[128,1024]{1,0:T(8,128)S(1)} %pad_maximum_fusion.2), channel_id=1, source_target_pairs={{0,8},{1,9},{2,10},{3,11},{4,12},{5,13},{6,14},{7,15},{8,0},{9,1},... | collective-permute-start | bytes 1572872 | tf_op jit(solution)/shard_map/ppermute | solution.py:282
  72.6 7.3 %factor_step.7.inverse_ref = f32[512,512]{1,0:T(8,128)} custom-call(f32[512,512]{1,0:T(8,128)} %factor_step.6.a_ref), custom_call_target="tpu_custom_call" | custom-call | tf_op jit(solution)/shard_map/factor_step/pallas_call | solution.py:104
  80.0 0.8 constant_dynamic-update-slice_fusion.1
  80.8 4.3 %collective-permute-done.9 = f32[128,1024]{1,0:T(8,128)S(1)} collective-permute-done((f32[128,1024]{1,0:T(8,128)S(1)}, f32[128,1024]{1,0:T(8,128)S(1)}, u32[]{:S(2)}, u32[]{:S(2)}) %collective-permute-start.9) | collective-permute-done | bytes 524320 | tf_op jit(solution)/shard_map/ppermute | solution.py:282
  85.1 0.1 pad_maximum_fusion.panel_ref
  85.2 0.0 copy-start
  85.3 1.9 %collective-permute-start.10 = (f32[256,1024]{1,0:T(8,128)S(1)}, f32[256,1024]{1,0:T(8,128)}, u32[]{:S(2)}, u32[]{:S(2)}) collective-permute-start(f32[256,1024]{1,0:T(8,128)S(1)} %pad_maximum_fusion.panel_ref), channel_id=1, source_target_pairs={{0,1},{1,0},{2,3},{3,2},{4,5},{5,4},{6,7},{7,6},{8,9},{9,8},{10,11... | collective-permute-start | bytes 3145736 | tf_op jit(solution)/shard_map/ppermute | solution.py:286
  87.2 0.8 constant_dynamic-update-slice_fusion.refs_0_
  88.0 2.1 %collective-permute-start.8 = (f32[8,32,1024]{2,1,0:T(8,128)}, f32[8,32,1024]{2,1,0:T(8,128)S(1)}, u32[]{:S(2)}, u32[]{:S(2)}) collective-permute-start(f32[8,32,1024]{2,1,0:T(8,128)} %constant_dynamic-update-slice_fusion.refs_0_), channel_id=1, source_target_pairs={{0,240},{16,0},{32,16},{48,32},{64,48},{80,64},{96,80},{112,96},{1... | collective-permute-start | bytes 3145736 | tf_op jit(solution)/shard_map/ppermute | solution.py:281
  90.1 3.7 %collective-permute-start.7 = (f32[8,32,1024]{2,1,0:T(8,128)}, f32[8,32,1024]{2,1,0:T(8,128)S(1)}, u32[]{:S(2)}, u32[]{:S(2)}) collective-permute-start(f32[8,32,1024]{2,1,0:T(8,128)} %constant_dynamic-update-slice_fusion.refs_0_), channel_id=1, source_target_pairs={{0,16},{16,32},{32,48},{48,64},{64,80},{80,96},{96,112},{112,128},... | collective-permute-start | bytes 3145736 | tf_op jit(solution)/shard_map/ppermute | solution.py:280
  93.9 6.1 %own_rows.1 = (bf16[8,256,512]{2,1,0:T(8,128)(2,1)}, f32[32,1024]{1,0:T(8,128)}) custom-call(f32[512,512]{1,0:T(8,128)} %factor_step.7.inverse_ref, f32[256,1024]{1,0:T(8,128)} %copy-done, f32[256,1024]{1,0:T(8,128)} %collective-permute-done.10.partner_ref), custom_call_target="tpu_custom_call" | custom-call | tf_op jit(solution)/shard_map/own_rows/pallas_call | solution.py:318
  100.0 15.7 %collective-permute-done.8.refs_2_ = f32[8,32,1024]{2,1,0:T(8,128)S(1)} collective-permute-done((f32[8,32,1024]{2,1,0:T(8,128)}, f32[8,32,1024]{2,1,0:T(8,128)S(1)}, u32[]{:S(2)}, u32[]{:S(2)}) %collective-permute-start.8) | collective-permute-done | bytes 1048608 | tf_op jit(solution)/shard_map/ppermute | solution.py:281
  115.7 3.1 %collective-permute-done.7.refs_1_ = f32[8,32,1024]{2,1,0:T(8,128)S(1)} collective-permute-done((f32[8,32,1024]{2,1,0:T(8,128)}, f32[8,32,1024]{2,1,0:T(8,128)S(1)}, u32[]{:S(2)}, u32[]{:S(2)}) %collective-permute-start.7) | collective-permute-done | bytes 1048608 | tf_op jit(solution)/shard_map/ppermute | solution.py:280
  118.9 2.8 %collective-permute-start.12 = (f32[4,32,1024]{2,1,0:T(8,128)S(1)}, f32[4,32,1024]{2,1,0:T(8,128)S(1)}, u32[]{:S(2)}, u32[]{:S(2)}) collective-permute-start(f32[4,32,1024]{2,1,0:T(8,128)S(1)} %slice.7), channel_id=1, source_target_pairs={{0,240},{16,0},{32,16},{48,32},{64,48},{80,64},{96,80},{112,96},{1... | collective-permute-start | bytes 1572872 | tf_op jit(solution)/shard_map/ppermute | solution.py:291
  121.8 3.0 %collective-permute-start.11 = (f32[4,32,1024]{2,1,0:T(8,128)S(1)}, f32[4,32,1024]{2,1,0:T(8,128)S(1)}, u32[]{:S(2)}, u32[]{:S(2)}) collective-permute-start(f32[4,32,1024]{2,1,0:T(8,128)S(1)} %slice.6), channel_id=1, source_target_pairs={{0,16},{16,32},{32,48},{48,64},{64,80},{80,96},{96,112},{112,128},... | collective-permute-start | bytes 1572872 | tf_op jit(solution)/shard_map/ppermute | solution.py:290
  124.8 9.3 %collective-permute-done.12.refs_4_ = f32[4,32,1024]{2,1,0:T(8,128)S(1)} collective-permute-done((f32[4,32,1024]{2,1,0:T(8,128)S(1)}, f32[4,32,1024]{2,1,0:T(8,128)S(1)}, u32[]{:S(2)}, u32[]{:S(2)}) %collective-permute-start.12) | collective-permute-done | bytes 524320 | tf_op jit(solution)/shard_map/ppermute | solution.py:291
  134.1 3.7 %collective-permute-done.11.refs_3_ = f32[4,32,1024]{2,1,0:T(8,128)S(1)} collective-permute-done((f32[4,32,1024]{2,1,0:T(8,128)S(1)}, f32[4,32,1024]{2,1,0:T(8,128)S(1)}, u32[]{:S(2)}, u32[]{:S(2)}) %collective-permute-start.11) | collective-permute-done | bytes 524320 | tf_op jit(solution)/shard_map/ppermute | solution.py:290
  137.8 0.8 copy-done.5
  138.6 8.2 %schur_tiles.1 = f32[28,128,128]{2,1,0:T(8,128)} custom-call(s32[2,28]{1,0:T(2,128)} %bitcast.19, bf16[8,256,512]{2,1,0:T(8,128)(2,1)} %get-tuple-element.37.left_hbm, f32[28,128,128]{2,1,0:T(8,128)} %tiles_hbm.1, f32[8,32,1024]{2,1,0:T(8,128)} %constant_dynamic-update-slice_fusion.refs_0_, f32[8,32,1024]{2,1,0:T(8,128)} %copy-done.2, ...), custom_call_target="tpu_custom_call" | custom-call | tf_op jit(solution)/shard_map/schur_tiles/pallas_call | solution.py:296
  (20 shorter events, 0.2 us)
Async XLA Ops:
  0.6 43.6 %collective-permute-start.4 = (f32[32,1024]{1,0:T(8,128)}, f32[32,1024]{1,0:T(8,128)S(1)}, u32[]{:S(2)}, u32[]{:S(2)}) collective-permute-start(f32[32,1024]{1,0:T(8,128)} %bitcast.7), channel_id=1, source_target_pairs={{0,4},{1,5},{2,6},{3,7},{4,0},{5,1},{6,2},{7,3},{8,12},{9,13},{10,... | collective-permute-start | bytes 393224 | tf_op jit(solution)/shard_map/ppermute | solution.py:265
  4.0 48.5 %collective-permute-start.3 = (f32[32,1024]{1,0:T(8,128)}, f32[32,1024]{1,0:T(8,128)S(1)}, u32[]{:S(2)}, u32[]{:S(2)}) collective-permute-start(f32[32,1024]{1,0:T(8,128)} %bitcast.8), channel_id=1, source_target_pairs={{0,192},{1,176},{2,208},{3,160},{4,224},{5,144},{6,240},{7,128},{8... | collective-permute-start | bytes 393224 | tf_op jit(solution)/shard_map/ppermute | solution.py:263
  16.9 35.6 %collective-permute-start.2 = (f32[32,1024]{1,0:T(8,128)}, f32[32,1024]{1,0:T(8,128)S(1)}, u32[]{:S(2)}, u32[]{:S(2)}) collective-permute-start(f32[32,1024]{1,0:T(8,128)} %bitcast.9), channel_id=1, source_target_pairs={{0,128},{1,112},{2,144},{3,96},{4,160},{5,80},{6,176},{7,64},{8,19... | collective-permute-start | bytes 393224 | tf_op jit(solution)/shard_map/ppermute | solution.py:263
  23.4 29.1 %collective-permute-start.1 = (f32[32,1024]{1,0:T(8,128)}, f32[32,1024]{1,0:T(8,128)S(1)}, u32[]{:S(2)}, u32[]{:S(2)}) collective-permute-start(f32[32,1024]{1,0:T(8,128)} %bitcast.10), channel_id=1, source_target_pairs={{0,64},{1,48},{2,80},{3,32},{4,96},{5,16},{6,112},{7,0},{8,128},{9... | collective-permute-start | bytes 393224 | tf_op jit(solution)/shard_map/ppermute | solution.py:263
  33.7 21.3 %collective-permute-start = (f32[32,1024]{1,0:T(8,128)}, f32[32,1024]{1,0:T(8,128)S(1)}, u32[]{:S(2)}, u32[]{:S(2)}) collective-permute-start(f32[32,1024]{1,0:T(8,128)} %bitcast.11), channel_id=1, source_target_pairs={{0,0},{1,240},{2,16},{3,224},{4,32},{5,208},{6,48},{7,192},{8,64},... | collective-permute-start | bytes 393224 | tf_op jit(solution)/shard_map/ppermute | solution.py:263
  44.2 16.0 %copy-start.3 = (f32[1024,32]{0,1:T(8,128)S(1)}, f32[1024,32]{0,1:T(8,128)}, u32[]{:S(2)}) copy-start(f32[1024,32]{0,1:T(8,128)} %param.5) | copy-start | bytes 393220
  55.1 15.6 %collective-permute-start.5 = (f32[4,32,1024]{2,1,0:T(8,128)S(1)}, f32[4,32,1024]{2,1,0:T(8,128)S(1)}, u32[]{:S(2)}, u32[]{:S(2)}) collective-permute-start(f32[4,32,1024]{2,1,0:T(8,128)S(1)} %pad_maximum_fusion.1), channel_id=1, source_target_pairs={{0,256},{1,257},{2,258},{3,259},{4,260},{5,261},{6,262},{7,263},{8... | collective-permute-start | bytes 1572872 | tf_op jit(solution)/shard_map/ppermute | solution.py:274
  60.2 10.2 %collective-permute-start.6 = (f32[64,1024]{1,0:T(8,128)S(1)}, f32[64,1024]{1,0:T(8,128)S(1)}, u32[]{:S(2)}, u32[]{:S(2)}) collective-permute-start(f32[64,1024]{1,0:T(8,128)S(1)} %pad_maximum_fusion.3), channel_id=1, source_target_pairs={{0,2},{1,3},{2,0},{3,1},{4,6},{5,7},{6,4},{7,5},{8,10},{9,11},{10,... | collective-permute-start | bytes 786440 | tf_op jit(solution)/shard_map/ppermute | solution.py:269
  70.7 14.4 %collective-permute-start.9 = (f32[128,1024]{1,0:T(8,128)S(1)}, f32[128,1024]{1,0:T(8,128)S(1)}, u32[]{:S(2)}, u32[]{:S(2)}) collective-permute-start(f32[128,1024]{1,0:T(8,128)S(1)} %pad_maximum_fusion.2), channel_id=1, source_target_pairs={{0,8},{1,9},{2,10},{3,11},{4,12},{5,13},{6,14},{7,15},{8,0},{9,1},... | collective-permute-start | bytes 1572872 | tf_op jit(solution)/shard_map/ppermute | solution.py:282
  85.2 8.6 %copy-start = (f32[256,1024]{1,0:T(8,128)}, f32[256,1024]{1,0:T(8,128)S(1)}, u32[]{:S(2)}) copy-start(f32[256,1024]{1,0:T(8,128)S(1)} %pad_maximum_fusion.panel_ref) | copy-start | bytes 3145732
  85.3 8.6 %collective-permute-start.10 = (f32[256,1024]{1,0:T(8,128)S(1)}, f32[256,1024]{1,0:T(8,128)}, u32[]{:S(2)}, u32[]{:S(2)}) collective-permute-start(f32[256,1024]{1,0:T(8,128)S(1)} %pad_maximum_fusion.panel_ref), channel_id=1, source_target_pairs={{0,1},{1,0},{2,3},{3,2},{4,5},{5,4},{6,7},{7,6},{8,9},{9,8},{10,11... | collective-permute-start | bytes 3145736 | tf_op jit(solution)/shard_map/ppermute | solution.py:286
  88.0 27.7 %collective-permute-start.8 = (f32[8,32,1024]{2,1,0:T(8,128)}, f32[8,32,1024]{2,1,0:T(8,128)S(1)}, u32[]{:S(2)}, u32[]{:S(2)}) collective-permute-start(f32[8,32,1024]{2,1,0:T(8,128)} %constant_dynamic-update-slice_fusion.refs_0_), channel_id=1, source_target_pairs={{0,240},{16,0},{32,16},{48,32},{64,48},{80,64},{96,80},{112,96},{1... | collective-permute-start | bytes 3145736 | tf_op jit(solution)/shard_map/ppermute | solution.py:281
  90.1 28.7 %collective-permute-start.7 = (f32[8,32,1024]{2,1,0:T(8,128)}, f32[8,32,1024]{2,1,0:T(8,128)S(1)}, u32[]{:S(2)}, u32[]{:S(2)}) collective-permute-start(f32[8,32,1024]{2,1,0:T(8,128)} %constant_dynamic-update-slice_fusion.refs_0_), channel_id=1, source_target_pairs={{0,16},{16,32},{32,48},{48,64},{64,80},{80,96},{96,112},{112,128},... | collective-permute-start | bytes 3145736 | tf_op jit(solution)/shard_map/ppermute | solution.py:280
  115.7 22.1 %copy-start.1 = (f32[8,32,1024]{2,1,0:T(8,128)}, f32[8,32,1024]{2,1,0:T(8,128)S(1)}, u32[]{:S(2)}) copy-start(f32[8,32,1024]{2,1,0:T(8,128)S(1)} %collective-permute-done.8.refs_2_) | copy-start | bytes 3145732
  118.8 19.0 %copy-start.2 = (f32[8,32,1024]{2,1,0:T(8,128)}, f32[8,32,1024]{2,1,0:T(8,128)S(1)}, u32[]{:S(2)}) copy-start(f32[8,32,1024]{2,1,0:T(8,128)S(1)} %collective-permute-done.7.refs_1_) | copy-start | bytes 3145732
  118.9 15.2 %collective-permute-start.12 = (f32[4,32,1024]{2,1,0:T(8,128)S(1)}, f32[4,32,1024]{2,1,0:T(8,128)S(1)}, u32[]{:S(2)}, u32[]{:S(2)}) collective-permute-start(f32[4,32,1024]{2,1,0:T(8,128)S(1)} %slice.7), channel_id=1, source_target_pairs={{0,240},{16,0},{32,16},{48,32},{64,48},{80,64},{96,80},{112,96},{1... | collective-permute-start | bytes 1572872 | tf_op jit(solution)/shard_map/ppermute | solution.py:291
  121.8 16.0 %collective-permute-start.11 = (f32[4,32,1024]{2,1,0:T(8,128)S(1)}, f32[4,32,1024]{2,1,0:T(8,128)S(1)}, u32[]{:S(2)}, u32[]{:S(2)}) collective-permute-start(f32[4,32,1024]{2,1,0:T(8,128)S(1)} %slice.6), channel_id=1, source_target_pairs={{0,16},{16,32},{32,48},{48,64},{64,80},{80,96},{96,112},{112,128},... | collective-permute-start | bytes 1572872 | tf_op jit(solution)/shard_map/ppermute | solution.py:290
  134.1 3.7 %copy-start.4 = (f32[4,32,1024]{2,1,0:T(8,128)}, f32[4,32,1024]{2,1,0:T(8,128)S(1)}, u32[]{:S(2)}) copy-start(f32[4,32,1024]{2,1,0:T(8,128)S(1)} %collective-permute-done.12.refs_4_) | copy-start | bytes 1572868
  137.8 0.8 copy-start.5

commit v6 on v4

--- a/solution.py
+++ b/solution.py
@@ -7,7 +7,7 @@
 from jax.experimental.pallas import tpu as pltpu
 from jax.sharding import PartitionSpec as P
 
-W, B, G, UNROLL = 512, 128, 8, 4
+W, B, G, UNROLL, COPIES = 512, 128, 8, 4, 2
 HI = lax.Precision.HIGHEST
 
 
@@ -170,26 +170,32 @@
 
 def tiles_kernel(reach, targets_ref, left_hbm, tiles_hbm, *refs):
     pieces, (out_hbm, left, far, tiles, out, right, in_sem, far_sem, out_sem) = refs[:len(reach)], refs[len(reach):]
-    blocks, size = left.shape[0], far.shape[2]
+    blocks, size = left.shape[0], far.shape[1]
     count = out.shape[0]
     col, row = lax.axis_index("col"), lax.axis_index("row")
     n_cols = lax.axis_size("col")
     side = lax.div(row, n_cols)
-    far_copies = [pltpu.make_async_copy(piece, far.at[i], far_sem.at[i]) for i, piece in enumerate(pieces)]
+    starts = [0]
+    for piece in pieces:
+        starts.append(starts[-1] + piece.shape[0])
+    far_copies = [
+        pltpu.make_async_copy(piece, far.at[pl.ds(starts[i], piece.shape[0])], far_sem.at[i])
+        for i, piece in enumerate(pieces)
+    ]
     left_copy = pltpu.make_async_copy(left_hbm, left, in_sem.at[0])
     tiles_copy = pltpu.make_async_copy(tiles_hbm, tiles, in_sem.at[1])
     for copy in far_copies:
         copy.start()
     left_copy.start()
     tiles_copy.start()
-    for i, away in enumerate(reach):
+    for i, (away, parts) in enumerate(reach):
         far_copies[i].wait()
-        for part in range(far.shape[1]):
-            twin, slot = part % 2, part // 2
-            apart = lax.rem(row + away - col - twin * (n_cols // 2) + 4 * n_cols, n_cols)
+        for place, part in enumerate(parts):
+            copied, slot = part % COPIES, part // COPIES
+            apart = lax.rem(row + away - col - copied * (n_cols // COPIES) + 4 * n_cols, n_cols)
             k = jnp.where(apart < n_cols // 2, 2 * apart, 2 * n_cols - 1 - 2 * apart)
             to = pl.ds(pl.multiple_of(k * size, size), size)
-            high, low = halves(far[i, part])
+            high, low = halves(far[starts[i] + place])
             for block in range(blocks):
                 right[slot * blocks + block, to, :B] = high[:, block * B:(block + 1) * B]
                 right[slot * blocks + block, to, B:] = low[:, block * B:(block + 1) * B]
@@ -253,38 +259,40 @@
     down = [(r, moved(r, -1)) for r in range(n_rows)]
     flips = [[(c, c ^ flip) for c in range(n_cols)] for flip in (n_cols // 4, n_cols // 8, n_cols // 2, 1)]
 
+    received = lax.ppermute(mine, "col", flips[0])
     first = lax.ppermute(mine, ("row", "col"), turn)
     second = lax.ppermute(mine, ("row", "col"), twin)
     work = factor_step(0, diag_block)
-    first, second, work, own = together((first, second, work, mine))
+    first, second, work, received = together((first, second, work, received))
 
     near = jnp.stack([first, second])
     other = lax.ppermute(near, ("row", "col"), lift)
-    received = lax.ppermute(own, "col", flips[0])
+    own = jnp.concatenate([mine, received])
+    received = lax.ppermute(own, "col", flips[1])
     near, other, work = together((near, other, work))
 
     base = jnp.concatenate([near, other])
-    upward, downward, pieces, reach = base, base, [base], [0]
+    whole = tuple(range(2 * COPIES))
+    upward, downward, pieces, reach = base, base, [base], [(0, whole)]
     for step in range(1, half // 2 + 1):
         both = step < half // 2
+        if not both:
+            upward, downward = upward[:COPIES], downward[COPIES:]
         upward = lax.ppermute(upward, "row", up)
-        if both:
-            downward = lax.ppermute(downward, "row", down)
+        downward = lax.ppermute(downward, "row", down)
         if step < W // B:
             work = factor_step(step, work)
             received, work = together((received, work))
-            own = jnp.concatenate([own, received])
-            received = lax.ppermute(own, "col", flips[step])
-            if step + 1 == W // B:
+            if step + 1 < W // B:
+                own = jnp.concatenate([own, received])
+                received = lax.ppermute(own, "col", flips[step + 1])
+            else:
                 left, panel_slice = own_rows(work, own, received, size, blocks)
             upward, downward, work = together((upward, downward, work))
         else:
-            upward, left, panel_slice = together((upward, left, panel_slice))
-        pieces.append(upward)
-        reach.append(-step)
-        if both:
-            pieces.append(downward)
-            reach.append(step)
+            upward, downward, left, panel_slice = together((upward, downward, left, panel_slice))
+        pieces += [upward, downward]
+        reach += [(-step, whole if both else whole[:COPIES]), (step, whole if both else whole[COPIES:])]
     any_space = pl.BlockSpec(memory_space=pl.ANY)
     schur = pl.pallas_call(
         functools.partial(tiles_kernel, tuple(reach)),
@@ -293,7 +301,7 @@
         out_specs=any_space,
         scratch_shapes=[
             pltpu.VMEM(left.shape, BF),
-            pltpu.VMEM((len(pieces), *base.shape), F32),
+            pltpu.VMEM((sum(piece.shape[0] for piece in pieces), size, rows), F32),
             pltpu.VMEM(tiles.shape, F32),
             pltpu.VMEM(tiles.shape, F32),
             pltpu.VMEM((2 * blocks, W, 2 * B), BF),

time: 151 us -> 142 us (0.940)
  waiting for transfers between devices: 32 us -> 18 us
  starting transfers between devices: 66.4 us -> 72.4 us
    ppermute x4, waiting for transfers between devices: 18.5 us -> 8.97 us  [on_device(): upward = lax.ppermute(upward, 'row', up)]
    ppermute x3 -> x4, waiting for transfers between devices: 8 us -> 3.01 us  [on_device(): downward = lax.ppermute(downward, 'row', down)]
    ppermute x4, waiting for transfers between devices: 0.01 us -> 4.33 us  [the longest x2 4.33 us: on_device(): received = lax.ppermute(own, 'col', flips[step + 1])]
    ppermute x1, waiting for transfers between devices: 5.42 us -> 1.65 us  [on_device(): other = lax.ppermute(near, ('row', 'col'), lift)]
    ppermute x3 -> x4, starting transfers between devices: 23.3 us -> 26.8 us  [on_device(): downward = lax.ppermute(downward, 'row', down)]
    ppermute x4, starting transfers between devices: 9.58 us -> 12.2 us  [on_device(): upward = lax.ppermute(upward, 'row', up)]
    slice x0 -> x2, local copies, waits for them, and re-layouts: none -> 1.51 us  [on_device(): upward, downward = (upward[:COPIES], downward[COPIES:])]
  transfers between devices with their start and end apart: 14 -> 15, of which waited for: 6 -> 7; matrix products, arithmetic and copies ran while one was open for 1% -> 1% of each run, Pallas kernels for 26% -> 27%
where the time goes in v6:
time: 142 us; the launch traced here: 141 us
  starting transfers between devices  72.4 us (51%)
  Pallas kernels  46.7 us (33%)
  waiting for transfers between devices  18 us (13%)
  local copies, waits for them, and re-layouts  2.26 us (2%)
    pallas_call x4, Pallas kernels, factor_step(): pl.pallas_call(functools.partial(factor_step_kernel, b), out_shape=jax.Sh...  32.3 us
    ppermute x4, starting transfers between devices, on_device(): downward = lax.ppermute(downward, 'row', down)  26.8 us
    ppermute x4, starting transfers between devices, on_device(): upward = lax.ppermute(upward, 'row', up)  12.2 us
    ppermute x1, starting transfers between devices, on_device(): second = lax.ppermute(mine, ('row', 'col'), twin)  11.7 us
    ppermute x4, waiting for transfers between devices, on_device(): upward = lax.ppermute(upward, 'row', up)  8.97 us
    pallas_call x1, Pallas kernels, on_device(): pl.pallas_call(functools.partial(tiles_kernel, tuple(reach)), out_shape=j...  8.28 us
    ppermute x1, starting transfers between devices, on_device(): first = lax.ppermute(mine, ('row', 'col'), turn)  6.58 us
    pallas_call x1, Pallas kernels, own_rows(): pl.pallas_call(own_kernel, out_shape=(jax.ShapeDtypeStruct((blocks, 2 * B...  6.11 us
  transfers between devices with their start and end apart: 15, of which 7 were waited for; matrix products, arithmetic and copies ran while one was open for 1% of the time, Pallas kernels for 27%

profile of v6, /device:TPU:6, one launch (start us, length us, event | category | flops | bytes accessed | tf_op | source)
XLA Modules:
  0.0 140.6 jit_solution(7181412126340237697)
XLA Ops:
  0.6 6.6 %collective-permute-start = (f32[32,1024]{1,0:T(8,128)}, f32[32,1024]{1,0:T(8,128)S(1)}, u32[]{:S(2)}, u32[]{:S(2)}) collective-permute-start(f32[32,1024]{1,0:T(8,128)} %bitcast.5), channel_id=1, source_target_pairs={{0,0},{1,240},{2,16},{3,224},{4,32},{5,208},{6,48},{7,192},{8,64},... | collective-permute-start | bytes 393224 | tf_op jit(solution)/shard_map/ppermute | solution.py:263
  7.2 11.7 %collective-permute-start.1 = (f32[32,1024]{1,0:T(8,128)}, f32[32,1024]{1,0:T(8,128)S(1)}, u32[]{:S(2)}, u32[]{:S(2)}) collective-permute-start(f32[32,1024]{1,0:T(8,128)} %bitcast.6), channel_id=1, source_target_pairs={{0,128},{1,112},{2,144},{3,96},{4,160},{5,80},{6,176},{7,64},{8,19... | collective-permute-start | bytes 393224 | tf_op jit(solution)/shard_map/ppermute | solution.py:264
  18.9 3.3 %collective-permute-start.2 = (f32[32,1024]{1,0:T(8,128)}, f32[32,1024]{1,0:T(8,128)S(1)}, u32[]{:S(2)}, u32[]{:S(2)}) collective-permute-start(f32[32,1024]{1,0:T(8,128)} %bitcast.7), channel_id=1, source_target_pairs={{0,4},{1,5},{2,6},{3,7},{4,0},{5,1},{6,2},{7,3},{8,12},{9,13},{10,... | collective-permute-start | bytes 393224 | tf_op jit(solution)/shard_map/ppermute | solution.py:262
  22.3 8.6 %factor_step.4.a_ref = f32[512,512]{1,0:T(8,128)} custom-call(f32[512,512]{1,0:T(8,128)} %a_ref.1), custom_call_target="tpu_custom_call" | custom-call | tf_op jit(solution)/shard_map/factor_step/pallas_call | solution.py:104
  30.9 4.8 %collective-permute-start.3 = (f32[2,32,1024]{2,1,0:T(8,128)S(1)}, f32[2,32,1024]{2,1,0:T(8,128)S(1)}, u32[]{:S(2)}, u32[]{:S(2)}) collective-permute-start(f32[2,32,1024]{2,1,0:T(8,128)S(1)} %pad_maximum_fusion.2), channel_id=1, source_target_pairs={{0,256},{1,257},{2,258},{3,259},{4,260},{5,261},{6,262},{7,263},{8... | collective-permute-start | bytes 786440 | tf_op jit(solution)/shard_map/ppermute | solution.py:269
  35.8 2.9 %collective-permute-start.6 = (f32[64,1024]{1,0:T(8,128)S(1)}, f32[64,1024]{1,0:T(8,128)S(1)}, u32[]{:S(2)}, u32[]{:S(2)}) collective-permute-start(f32[64,1024]{1,0:T(8,128)S(1)} %pad_maximum_fusion.3), channel_id=1, source_target_pairs={{0,2},{1,3},{2,0},{3,1},{4,6},{5,7},{6,4},{7,5},{8,10},{9,11},{10,... | collective-permute-start | bytes 786440 | tf_op jit(solution)/shard_map/ppermute | solution.py:271
  38.6 1.7 %collective-permute-done.3 = f32[2,32,1024]{2,1,0:T(8,128)S(1)} collective-permute-done((f32[2,32,1024]{2,1,0:T(8,128)S(1)}, f32[2,32,1024]{2,1,0:T(8,128)S(1)}, u32[]{:S(2)}, u32[]{:S(2)}) %collective-permute-start.3) | collective-permute-done | bytes 262176 | tf_op jit(solution)/shard_map/ppermute | solution.py:269
  40.3 3.9 %collective-permute-start.4 = (f32[4,32,1024]{2,1,0:T(8,128)S(1)}, f32[4,32,1024]{2,1,0:T(8,128)}, u32[]{:S(2)}, u32[]{:S(2)}) collective-permute-start(f32[4,32,1024]{2,1,0:T(8,128)S(1)} %constant_dynamic-update-slice_fusion.refs_0_), channel_id=1, source_target_pairs={{0,16},{16,32},{32,48},{48,64},{64,80},{80,96},{96,112},{112,128},... | collective-permute-start | bytes 1572872 | tf_op jit(solution)/shard_map/ppermute | solution.py:281
  44.2 5.7 %collective-permute-start.5 = (f32[4,32,1024]{2,1,0:T(8,128)S(1)}, f32[4,32,1024]{2,1,0:T(8,128)}, u32[]{:S(2)}, u32[]{:S(2)}) collective-permute-start(f32[4,32,1024]{2,1,0:T(8,128)S(1)} %constant_dynamic-update-slice_fusion.refs_0_), channel_id=1, source_target_pairs={{0,240},{16,0},{32,16},{48,32},{64,48},{80,64},{96,80},{112,96},{1... | collective-permute-start | bytes 1572872 | tf_op jit(solution)/shard_map/ppermute | solution.py:282
  49.9 8.3 %factor_step.5.a_ref = f32[512,512]{1,0:T(8,128)} custom-call(f32[512,512]{1,0:T(8,128)} %factor_step.4.a_ref), custom_call_target="tpu_custom_call" | custom-call | tf_op jit(solution)/shard_map/factor_step/pallas_call | solution.py:104
  58.3 2.1 %collective-permute-start.9 = (f32[128,1024]{1,0:T(8,128)S(1)}, f32[128,1024]{1,0:T(8,128)S(1)}, u32[]{:S(2)}, u32[]{:S(2)}) collective-permute-start(f32[128,1024]{1,0:T(8,128)S(1)} %pad_maximum_fusion.1), channel_id=1, source_target_pairs={{0,8},{1,9},{2,10},{3,11},{4,12},{5,13},{6,14},{7,15},{8,0},{9,1},... | collective-permute-start | bytes 1572872 | tf_op jit(solution)/shard_map/ppermute | solution.py:288
  60.4 0.5 collective-permute-done.5.refs_2_
  60.9 8.1 %factor_step.6.a_ref = f32[512,512]{1,0:T(8,128)} custom-call(f32[512,512]{1,0:T(8,128)} %factor_step.5.a_ref), custom_call_target="tpu_custom_call" | custom-call | tf_op jit(solution)/shard_map/factor_step/pallas_call | solution.py:104
  69.0 4.3 %collective-permute-done.9 = f32[128,1024]{1,0:T(8,128)S(1)} collective-permute-done((f32[128,1024]{1,0:T(8,128)S(1)}, f32[128,1024]{1,0:T(8,128)S(1)}, u32[]{:S(2)}, u32[]{:S(2)}) %collective-permute-start.9) | collective-permute-done | bytes 524320 | tf_op jit(solution)/shard_map/ppermute | solution.py:288
  73.4 1.9 %collective-permute-start.7 = (f32[4,32,1024]{2,1,0:T(8,128)}, f32[4,32,1024]{2,1,0:T(8,128)}, u32[]{:S(2)}, u32[]{:S(2)}) collective-permute-start(f32[4,32,1024]{2,1,0:T(8,128)} %collective-permute-done.4.refs_1_), channel_id=1, source_target_pairs={{0,16},{16,32},{32,48},{48,64},{64,80},{80,96},{96,112},{112,128},... | collective-permute-start | bytes 1572872 | tf_op jit(solution)/shard_map/ppermute | solution.py:281
  75.3 12.4 %collective-permute-start.8 = (f32[4,32,1024]{2,1,0:T(8,128)}, f32[4,32,1024]{2,1,0:T(8,128)}, u32[]{:S(2)}, u32[]{:S(2)}) collective-permute-start(f32[4,32,1024]{2,1,0:T(8,128)} %collective-permute-done.5.refs_2_), channel_id=1, source_target_pairs={{0,240},{16,0},{32,16},{48,32},{64,48},{80,64},{96,80},{112,96},{1... | collective-permute-start | bytes 1572872 | tf_op jit(solution)/shard_map/ppermute | solution.py:282
  87.7 0.1 pad_maximum_fusion.panel_ref
  87.8 1.9 %collective-permute-start.12 = (f32[256,1024]{1,0:T(8,128)S(1)}, f32[256,1024]{1,0:T(8,128)S(1)}, u32[]{:S(2)}, u32[]{:S(2)}) collective-permute-start(f32[256,1024]{1,0:T(8,128)S(1)} %pad_maximum_fusion.panel_ref), channel_id=1, source_target_pairs={{0,1},{1,0},{2,3},{3,2},{4,5},{5,4},{6,7},{7,6},{8,9},{9,8},{10,11... | collective-permute-start | bytes 3145736 | tf_op jit(solution)/shard_map/ppermute | solution.py:288
  89.8 7.6 %collective-permute-done.7.refs_3_ = f32[4,32,1024]{2,1,0:T(8,128)} collective-permute-done((f32[4,32,1024]{2,1,0:T(8,128)}, f32[4,32,1024]{2,1,0:T(8,128)}, u32[]{:S(2)}, u32[]{:S(2)}) %collective-permute-start.7) | collective-permute-done | bytes 524320 | tf_op jit(solution)/shard_map/ppermute | solution.py:281
  97.4 1.2 collective-permute-done.8.refs_4_
  98.6 1.9 %collective-permute-start.10 = (f32[4,32,1024]{2,1,0:T(8,128)}, f32[4,32,1024]{2,1,0:T(8,128)S(1)}, u32[]{:S(2)}, u32[]{:S(2)}) collective-permute-start(f32[4,32,1024]{2,1,0:T(8,128)} %collective-permute-done.7.refs_3_), channel_id=1, source_target_pairs={{0,16},{16,32},{32,48},{48,64},{64,80},{80,96},{96,112},{112,128},... | collective-permute-start | bytes 1572872 | tf_op jit(solution)/shard_map/ppermute | solution.py:281
  100.5 5.6 %collective-permute-start.11 = (f32[4,32,1024]{2,1,0:T(8,128)}, f32[4,32,1024]{2,1,0:T(8,128)S(1)}, u32[]{:S(2)}, u32[]{:S(2)}) collective-permute-start(f32[4,32,1024]{2,1,0:T(8,128)} %collective-permute-done.8.refs_4_), channel_id=1, source_target_pairs={{0,240},{16,0},{32,16},{48,32},{64,48},{80,64},{96,80},{112,96},{1... | collective-permute-start | bytes 1572872 | tf_op jit(solution)/shard_map/ppermute | solution.py:282
  106.1 7.4 %factor_step.7.inverse_ref = f32[512,512]{1,0:T(8,128)} custom-call(f32[512,512]{1,0:T(8,128)} %factor_step.6.a_ref), custom_call_target="tpu_custom_call" | custom-call | tf_op jit(solution)/shard_map/factor_step/pallas_call | solution.py:104
  113.5 1.3 collective-permute-done.10.refs_5_
  114.8 1.3 collective-permute-done.11.refs_6_
  116.1 0.8 slice.6
  116.9 4.5 %collective-permute-start.13 = (f32[2,32,1024]{2,1,0:T(8,128)}, f32[2,32,1024]{2,1,0:T(8,128)S(1)}, u32[]{:S(2)}, u32[]{:S(2)}) collective-permute-start(f32[2,32,1024]{2,1,0:T(8,128)} %slice.6), channel_id=1, source_target_pairs={{0,16},{16,32},{32,48},{48,64},{64,80},{80,96},{96,112},{112,128},... | collective-permute-start | bytes 786440 | tf_op jit(solution)/shard_map/ppermute | solution.py:281
  121.4 0.7 slice.7
  122.2 3.1 %collective-permute-start.14 = (f32[2,32,1024]{2,1,0:T(8,128)}, f32[2,32,1024]{2,1,0:T(8,128)}, u32[]{:S(2)}, u32[]{:S(2)}) collective-permute-start(f32[2,32,1024]{2,1,0:T(8,128)} %slice.7), channel_id=1, source_target_pairs={{0,240},{16,0},{32,16},{48,32},{64,48},{80,64},{96,80},{112,96},{1... | collective-permute-start | bytes 786440 | tf_op jit(solution)/shard_map/ppermute | solution.py:282
  125.3 6.1 %own_rows.1 = (bf16[8,256,512]{2,1,0:T(8,128)(2,1)}, f32[32,1024]{1,0:T(8,128)}) custom-call(f32[512,512]{1,0:T(8,128)} %factor_step.7.inverse_ref, f32[256,1024]{1,0:T(8,128)} %copy-done, f32[256,1024]{1,0:T(8,128)} %copy-done.5), custom_call_target="tpu_custom_call" | custom-call | tf_op jit(solution)/shard_map/own_rows/pallas_call | solution.py:319
  131.4 0.7 copy-done.6
  132.1 8.3 %schur_tiles.1 = f32[28,128,128]{2,1,0:T(8,128)} custom-call(s32[2,28]{1,0:T(2,128)} %bitcast.13, bf16[8,256,512]{2,1,0:T(8,128)(2,1)} %get-tuple-element.53.left_hbm, f32[28,128,128]{2,1,0:T(8,128)} %tiles_hbm.1, f32[4,32,1024]{2,1,0:T(8,128)} %copy-done.3, f32[4,32,1024]{2,1,0:T(8,128)} %collective-permute-done.4.refs_1_, ...), custom_call_target="tpu_custom_call" | custom-call | tf_op jit(solution)/shard_map/schur_tiles/pallas_call | solution.py:297
  (26 shorter events, 0.2 us)
Async XLA Ops:
  0.6 35.1 %copy-start.4 = (f32[1024,32]{0,1:T(8,128)S(1)}, f32[1024,32]{0,1:T(8,128)}, u32[]{:S(2)}) copy-start(f32[1024,32]{0,1:T(8,128)} %param.5) | copy-start | bytes 393220
  0.6 30.2 %collective-permute-start = (f32[32,1024]{1,0:T(8,128)}, f32[32,1024]{1,0:T(8,128)S(1)}, u32[]{:S(2)}, u32[]{:S(2)}) collective-permute-start(f32[32,1024]{1,0:T(8,128)} %bitcast.5), channel_id=1, source_target_pairs={{0,0},{1,240},{2,16},{3,224},{4,32},{5,208},{6,48},{7,192},{8,64},... | collective-permute-start | bytes 393224 | tf_op jit(solution)/shard_map/ppermute | solution.py:263
  7.2 23.6 %collective-permute-start.1 = (f32[32,1024]{1,0:T(8,128)}, f32[32,1024]{1,0:T(8,128)S(1)}, u32[]{:S(2)}, u32[]{:S(2)}) collective-permute-start(f32[32,1024]{1,0:T(8,128)} %bitcast.6), channel_id=1, source_target_pairs={{0,128},{1,112},{2,144},{3,96},{4,160},{5,80},{6,176},{7,64},{8,19... | collective-permute-start | bytes 393224 | tf_op jit(solution)/shard_map/ppermute | solution.py:264
  18.9 11.9 %collective-permute-start.2 = (f32[32,1024]{1,0:T(8,128)}, f32[32,1024]{1,0:T(8,128)S(1)}, u32[]{:S(2)}, u32[]{:S(2)}) collective-permute-start(f32[32,1024]{1,0:T(8,128)} %bitcast.7), channel_id=1, source_target_pairs={{0,4},{1,5},{2,6},{3,7},{4,0},{5,1},{6,2},{7,3},{8,12},{9,13},{10,... | collective-permute-start | bytes 393224 | tf_op jit(solution)/shard_map/ppermute | solution.py:262
  30.9 9.4 %collective-permute-start.3 = (f32[2,32,1024]{2,1,0:T(8,128)S(1)}, f32[2,32,1024]{2,1,0:T(8,128)S(1)}, u32[]{:S(2)}, u32[]{:S(2)}) collective-permute-start(f32[2,32,1024]{2,1,0:T(8,128)S(1)} %pad_maximum_fusion.2), channel_id=1, source_target_pairs={{0,256},{1,257},{2,258},{3,259},{4,260},{5,261},{6,262},{7,263},{8... | collective-permute-start | bytes 786440 | tf_op jit(solution)/shard_map/ppermute | solution.py:269
  35.8 22.5 %collective-permute-start.6 = (f32[64,1024]{1,0:T(8,128)S(1)}, f32[64,1024]{1,0:T(8,128)S(1)}, u32[]{:S(2)}, u32[]{:S(2)}) collective-permute-start(f32[64,1024]{1,0:T(8,128)S(1)} %pad_maximum_fusion.3), channel_id=1, source_target_pairs={{0,2},{1,3},{2,0},{3,1},{4,6},{5,7},{6,4},{7,5},{8,10},{9,11},{10,... | collective-permute-start | bytes 786440 | tf_op jit(solution)/shard_map/ppermute | solution.py:271
  40.3 28.7 %copy-start.3 = (f32[4,32,1024]{2,1,0:T(8,128)}, f32[4,32,1024]{2,1,0:T(8,128)S(1)}, u32[]{:S(2)}) copy-start(f32[4,32,1024]{2,1,0:T(8,128)S(1)} %constant_dynamic-update-slice_fusion.refs_0_) | copy-start | bytes 1572868
  40.3 20.0 %collective-permute-start.4 = (f32[4,32,1024]{2,1,0:T(8,128)S(1)}, f32[4,32,1024]{2,1,0:T(8,128)}, u32[]{:S(2)}, u32[]{:S(2)}) collective-permute-start(f32[4,32,1024]{2,1,0:T(8,128)S(1)} %constant_dynamic-update-slice_fusion.refs_0_), channel_id=1, source_target_pairs={{0,16},{16,32},{32,48},{48,64},{64,80},{80,96},{96,112},{112,128},... | collective-permute-start | bytes 1572872 | tf_op jit(solution)/shard_map/ppermute | solution.py:281
  44.2 16.7 %collective-permute-start.5 = (f32[4,32,1024]{2,1,0:T(8,128)S(1)}, f32[4,32,1024]{2,1,0:T(8,128)}, u32[]{:S(2)}, u32[]{:S(2)}) collective-permute-start(f32[4,32,1024]{2,1,0:T(8,128)S(1)} %constant_dynamic-update-slice_fusion.refs_0_), channel_id=1, source_target_pairs={{0,240},{16,0},{32,16},{48,32},{64,48},{80,64},{96,80},{112,96},{1... | collective-permute-start | bytes 1572872 | tf_op jit(solution)/shard_map/ppermute | solution.py:282
  58.3 15.1 %collective-permute-start.9 = (f32[128,1024]{1,0:T(8,128)S(1)}, f32[128,1024]{1,0:T(8,128)S(1)}, u32[]{:S(2)}, u32[]{:S(2)}) collective-permute-start(f32[128,1024]{1,0:T(8,128)S(1)} %pad_maximum_fusion.1), channel_id=1, source_target_pairs={{0,8},{1,9},{2,10},{3,11},{4,12},{5,13},{6,14},{7,15},{8,0},{9,1},... | collective-permute-start | bytes 1572872 | tf_op jit(solution)/shard_map/ppermute | solution.py:288
  73.4 24.0 %collective-permute-start.7 = (f32[4,32,1024]{2,1,0:T(8,128)}, f32[4,32,1024]{2,1,0:T(8,128)}, u32[]{:S(2)}, u32[]{:S(2)}) collective-permute-start(f32[4,32,1024]{2,1,0:T(8,128)} %collective-permute-done.4.refs_1_), channel_id=1, source_target_pairs={{0,16},{16,32},{32,48},{48,64},{64,80},{80,96},{96,112},{112,128},... | collective-permute-start | bytes 1572872 | tf_op jit(solution)/shard_map/ppermute | solution.py:281
  75.3 23.3 %collective-permute-start.8 = (f32[4,32,1024]{2,1,0:T(8,128)}, f32[4,32,1024]{2,1,0:T(8,128)}, u32[]{:S(2)}, u32[]{:S(2)}) collective-permute-start(f32[4,32,1024]{2,1,0:T(8,128)} %collective-permute-done.5.refs_2_), channel_id=1, source_target_pairs={{0,240},{16,0},{32,16},{48,32},{64,48},{80,64},{96,80},{112,96},{1... | collective-permute-start | bytes 1572872 | tf_op jit(solution)/shard_map/ppermute | solution.py:282
  87.8 37.4 %copy-start = (f32[256,1024]{1,0:T(8,128)}, f32[256,1024]{1,0:T(8,128)S(1)}, u32[]{:S(2)}) copy-start(f32[256,1024]{1,0:T(8,128)S(1)} %pad_maximum_fusion.panel_ref) | copy-start | bytes 3145732
  87.8 25.6 %collective-permute-start.12 = (f32[256,1024]{1,0:T(8,128)S(1)}, f32[256,1024]{1,0:T(8,128)S(1)}, u32[]{:S(2)}, u32[]{:S(2)}) collective-permute-start(f32[256,1024]{1,0:T(8,128)S(1)} %pad_maximum_fusion.panel_ref), channel_id=1, source_target_pairs={{0,1},{1,0},{2,3},{3,2},{4,5},{5,4},{6,7},{7,6},{8,9},{9,8},{10,11... | collective-permute-start | bytes 3145736 | tf_op jit(solution)/shard_map/ppermute | solution.py:288
  98.6 16.2 %collective-permute-start.10 = (f32[4,32,1024]{2,1,0:T(8,128)}, f32[4,32,1024]{2,1,0:T(8,128)S(1)}, u32[]{:S(2)}, u32[]{:S(2)}) collective-permute-start(f32[4,32,1024]{2,1,0:T(8,128)} %collective-permute-done.7.refs_3_), channel_id=1, source_target_pairs={{0,16},{16,32},{32,48},{48,64},{64,80},{80,96},{96,112},{112,128},... | collective-permute-start | bytes 1572872 | tf_op jit(solution)/shard_map/ppermute | solution.py:281
  100.5 15.6 %collective-permute-start.11 = (f32[4,32,1024]{2,1,0:T(8,128)}, f32[4,32,1024]{2,1,0:T(8,128)S(1)}, u32[]{:S(2)}, u32[]{:S(2)}) collective-permute-start(f32[4,32,1024]{2,1,0:T(8,128)} %collective-permute-done.8.refs_4_), channel_id=1, source_target_pairs={{0,240},{16,0},{32,16},{48,32},{64,48},{80,64},{96,80},{112,96},{1... | collective-permute-start | bytes 1572872 | tf_op jit(solution)/shard_map/ppermute | solution.py:282
  113.5 11.8 %copy-start.5 = (f32[256,1024]{1,0:T(8,128)}, f32[256,1024]{1,0:T(8,128)S(1)}, u32[]{:S(2)}) copy-start(f32[256,1024]{1,0:T(8,128)S(1)} %collective-permute-done.12.partner_ref) | copy-start | bytes 3145732
  114.8 16.6 %copy-start.1 = (f32[4,32,1024]{2,1,0:T(8,128)}, f32[4,32,1024]{2,1,0:T(8,128)S(1)}, u32[]{:S(2)}) copy-start(f32[4,32,1024]{2,1,0:T(8,128)S(1)} %collective-permute-done.10.refs_5_) | copy-start | bytes 1572868
  116.1 15.3 %copy-start.2 = (f32[4,32,1024]{2,1,0:T(8,128)}, f32[4,32,1024]{2,1,0:T(8,128)S(1)}, u32[]{:S(2)}) copy-start(f32[4,32,1024]{2,1,0:T(8,128)S(1)} %collective-permute-done.11.refs_6_) | copy-start | bytes 1572868
  116.9 14.5 %collective-permute-start.13 = (f32[2,32,1024]{2,1,0:T(8,128)}, f32[2,32,1024]{2,1,0:T(8,128)S(1)}, u32[]{:S(2)}, u32[]{:S(2)}) collective-permute-start(f32[2,32,1024]{2,1,0:T(8,128)} %slice.6), channel_id=1, source_target_pairs={{0,16},{16,32},{32,48},{48,64},{64,80},{80,96},{96,112},{112,128},... | collective-permute-start | bytes 786440 | tf_op jit(solution)/shard_map/ppermute | solution.py:281
  122.2 9.2 %collective-permute-start.14 = (f32[2,32,1024]{2,1,0:T(8,128)}, f32[2,32,1024]{2,1,0:T(8,128)}, u32[]{:S(2)}, u32[]{:S(2)}) collective-permute-start(f32[2,32,1024]{2,1,0:T(8,128)} %slice.7), channel_id=1, source_target_pairs={{0,240},{16,0},{32,16},{48,32},{64,48},{80,64},{96,80},{112,96},{1... | collective-permute-start | bytes 786440 | tf_op jit(solution)/shard_map/ppermute | solution.py:282
  131.4 0.7 copy-start.6

commit v7 on v6

--- a/solution.py
+++ b/solution.py
@@ -103,12 +103,13 @@
 def factor_step(b, a):
     return pl.pallas_call(
         functools.partial(factor_step_kernel, b),
-        out_shape=jax.ShapeDtypeStruct((W, W), jnp.float32),
+        out_shape=pltpu.VMEM((W, W), jnp.float32),
         in_specs=[pl.BlockSpec(memory_space=pltpu.VMEM)],
         out_specs=pl.BlockSpec(memory_space=pltpu.VMEM),
         scratch_shapes=[pltpu.VMEM((B, B), jnp.float32)],
+        compiler_params=pltpu.CompilerParams(vmem_limit_bytes=24 << 20),
         name="factor_step",
-    )(a)
+    )(pltpu.with_memory_space_constraint(a, pltpu.VMEM))
 
 
 BF, F32 = jnp.bfloat16, jnp.float32
@@ -168,38 +169,25 @@
                 left_ref[first // B + part, B:, across] = low[part * B:(part + 1) * B]
 
 
-def tiles_kernel(reach, targets_ref, left_hbm, tiles_hbm, *refs):
-    pieces, (out_hbm, left, far, tiles, out, right, in_sem, far_sem, out_sem) = refs[:len(reach)], refs[len(reach):]
-    blocks, size = left.shape[0], far.shape[1]
+def tiles_kernel(reach, targets_ref, tiles_hbm, left, *refs):
+    pieces, (out_hbm, tiles, out, right, in_sem, out_sem) = refs[:len(reach)], refs[len(reach):]
+    blocks, size = left.shape[0], pieces[0].shape[1]
     count = out.shape[0]
     col, row = lax.axis_index("col"), lax.axis_index("row")
     n_cols = lax.axis_size("col")
     side = lax.div(row, n_cols)
-    starts = [0]
-    for piece in pieces:
-        starts.append(starts[-1] + piece.shape[0])
-    far_copies = [
-        pltpu.make_async_copy(piece, far.at[pl.ds(starts[i], piece.shape[0])], far_sem.at[i])
-        for i, piece in enumerate(pieces)
-    ]
-    left_copy = pltpu.make_async_copy(left_hbm, left, in_sem.at[0])
-    tiles_copy = pltpu.make_async_copy(tiles_hbm, tiles, in_sem.at[1])
-    for copy in far_copies:
-        copy.start()
-    left_copy.start()
+    tiles_copy = pltpu.make_async_copy(tiles_hbm, tiles, in_sem)
     tiles_copy.start()
     for i, (away, parts) in enumerate(reach):
-        far_copies[i].wait()
         for place, part in enumerate(parts):
             copied, slot = part % COPIES, part // COPIES
             apart = lax.rem(row + away - col - copied * (n_cols // COPIES) + 4 * n_cols, n_cols)
             k = jnp.where(apart < n_cols // 2, 2 * apart, 2 * n_cols - 1 - 2 * apart)
             to = pl.ds(pl.multiple_of(k * size, size), size)
-            high, low = halves(far[starts[i] + place])
+            high, low = halves(pieces[i][place])
             for block in range(blocks):
                 right[slot * blocks + block, to, :B] = high[:, block * B:(block + 1) * B]
                 right[slot * blocks + block, to, B:] = low[:, block * B:(block + 1) * B]
-    left_copy.wait()
     tiles_copy.wait()
 
     def one(slot, carry):
@@ -234,6 +222,10 @@
     return order
 
 
+def near_core(value):
+    return pltpu.with_memory_space_constraint(value, pltpu.VMEM)
+
+
 def on_device(diag_block, panel, tiles, targets):
     n_rows, n_cols = lax.axis_size("row"), lax.axis_size("col")
     size, rows = panel.shape[1], panel.shape[0]
@@ -259,9 +251,9 @@
     down = [(r, moved(r, -1)) for r in range(n_rows)]
     flips = [[(c, c ^ flip) for c in range(n_cols)] for flip in (n_cols // 4, n_cols // 8, n_cols // 2, 1)]
 
-    received = lax.ppermute(mine, "col", flips[0])
     first = lax.ppermute(mine, ("row", "col"), turn)
     second = lax.ppermute(mine, ("row", "col"), twin)
+    received = lax.ppermute(mine, "col", flips[0])
     work = factor_step(0, diag_block)
     first, second, work, received = together((first, second, work, received))
 
@@ -297,20 +289,18 @@
     schur = pl.pallas_call(
         functools.partial(tiles_kernel, tuple(reach)),
         out_shape=jax.ShapeDtypeStruct(tiles.shape, F32),
-        in_specs=[pl.BlockSpec(memory_space=pltpu.SMEM), *[any_space] * (2 + len(pieces))],
+        in_specs=[pl.BlockSpec(memory_space=pltpu.SMEM), any_space, *vmem(1 + len(pieces))],
         out_specs=any_space,
         scratch_shapes=[
-            pltpu.VMEM(left.shape, BF),
-            pltpu.VMEM((sum(piece.shape[0] for piece in pieces), size, rows), F32),
             pltpu.VMEM(tiles.shape, F32),
             pltpu.VMEM(tiles.shape, F32),
             pltpu.VMEM((2 * blocks, W, 2 * B), BF),
-            pltpu.SemaphoreType.DMA((2,)),
-            pltpu.SemaphoreType.DMA((len(pieces),)),
+            pltpu.SemaphoreType.DMA,
             pltpu.SemaphoreType.DMA((count,)),
         ],
+        compiler_params=pltpu.CompilerParams(vmem_limit_bytes=24 << 20),
         name="schur_tiles",
-    )(targets.T, left, tiles, *pieces)
+    )(targets.T, tiles, *[near_core(value) for value in (left, *pieces)])
     return panel_slice.T, schur
 
 
@@ -319,7 +309,7 @@
     return pl.pallas_call(
         own_kernel,
         out_shape=(
-            jax.ShapeDtypeStruct((blocks, 2 * B, W), BF),
+            pltpu.VMEM((blocks, 2 * B, W), BF),
             jax.ShapeDtypeStruct((size, rows), F32),
         ),
         in_specs=vmem(3),
@@ -330,8 +320,9 @@
             *[pltpu.VMEM((rows, W), BF)] * 2,
             pltpu.VMEM((W, rows), F32),
         ],
+        compiler_params=pltpu.CompilerParams(vmem_limit_bytes=24 << 20),
         name="own_rows",
-    )(inverse, own, received)
+    )(near_core(inverse), near_core(own), near_core(received))
 
 
 def solution(mesh):

time: 142 us -> 134 us (0.944)
  Pallas kernels: 46.7 us -> 32.1 us
  waiting for transfers between devices: 18 us -> 24.3 us
    pallas_call x5, Pallas kernels: 38.4 us -> 26.5 us  [the longest x4 23.6 us: factor_step(): pl.pallas_call(functools.partial(factor_step_kernel, b), out_shape=pltpu....]
    ppermute x4, waiting for transfers between devices: 8.97 us -> 12.2 us  [on_device(): upward = lax.ppermute(upward, 'row', up)]
    pallas_call x1, Pallas kernels: 8.28 us -> 5.51 us  [on_device(): pl.pallas_call(functools.partial(tiles_kernel, tuple(reach)), out_shape=j...]
    ppermute x4, waiting for transfers between devices: 3.01 us -> 5.73 us  [on_device(): downward = lax.ppermute(downward, 'row', down)]
    slice x2, local copies, waits for them, and re-layouts: 1.51 us -> 0.04 us  [on_device(): upward, downward = (upward[:COPIES], downward[COPIES:])]
  transfers between devices with their start and end apart: 15 -> 15, of which waited for: 7 -> 9; matrix products, arithmetic and copies ran while one was open for 1% -> 0% of each run, Pallas kernels for 27% -> 20%
where the time goes in v7:
time: 134 us; the launch traced here: 132 us
  starting transfers between devices  72.9 us (54%)
  Pallas kernels  32.1 us (24%)
  waiting for transfers between devices  24.3 us (18%)
    ppermute x4, starting transfers between devices, on_device(): downward = lax.ppermute(downward, 'row', down)  27.8 us
    pallas_call x4, Pallas kernels, factor_step(): pl.pallas_call(functools.partial(factor_step_kernel, b), out_shape=pltpu....  23.6 us
    ppermute x4, waiting for transfers between devices, on_device(): upward = lax.ppermute(upward, 'row', up)  12.2 us
    ppermute x1, starting transfers between devices, on_device(): second = lax.ppermute(mine, ('row', 'col'), twin)  11.7 us
    ppermute x4, starting transfers between devices, on_device(): upward = lax.ppermute(upward, 'row', up)  11.5 us
    ppermute x1, starting transfers between devices, on_device(): first = lax.ppermute(mine, ('row', 'col'), turn)  6.45 us
    ppermute x4, waiting for transfers between devices, on_device(): downward = lax.ppermute(downward, 'row', down)  5.73 us
    pallas_call x1, Pallas kernels, on_device(): pl.pallas_call(functools.partial(tiles_kernel, tuple(reach)), out_shape=j...  5.51 us
  transfers between devices with their start and end apart: 15, of which 9 were waited for; matrix products, arithmetic and copies ran while one was open for 0% of the time, Pallas kernels for 20%

profile of v7, /device:TPU:6, one launch (start us, length us, event | category | flops | bytes accessed | tf_op | source)
XLA Modules:
  0.0 131.9 jit_solution(4448500356390790976)
XLA Ops:
  0.6 6.4 %collective-permute-start = (f32[32,1024]{1,0:T(8,128)}, f32[32,1024]{1,0:T(8,128)S(1)}, u32[]{:S(2)}, u32[]{:S(2)}) collective-permute-start(f32[32,1024]{1,0:T(8,128)} %bitcast.6), channel_id=1, source_target_pairs={{0,0},{1,240},{2,16},{3,224},{4,32},{5,208},{6,48},{7,192},{8,64},... | collective-permute-start | bytes 393224 | tf_op jit(solution)/shard_map/ppermute | solution.py:254
  7.1 11.7 %collective-permute-start.1 = (f32[32,1024]{1,0:T(8,128)}, f32[32,1024]{1,0:T(8,128)S(1)}, u32[]{:S(2)}, u32[]{:S(2)}) collective-permute-start(f32[32,1024]{1,0:T(8,128)} %bitcast.7), channel_id=1, source_target_pairs={{0,128},{1,112},{2,144},{3,96},{4,160},{5,80},{6,176},{7,64},{8,19... | collective-permute-start | bytes 393224 | tf_op jit(solution)/shard_map/ppermute | solution.py:255
  18.8 3.3 %collective-permute-start.2 = (f32[32,1024]{1,0:T(8,128)}, f32[32,1024]{1,0:T(8,128)S(1)}, u32[]{:S(2)}, u32[]{:S(2)}) collective-permute-start(f32[32,1024]{1,0:T(8,128)} %bitcast.8), channel_id=1, source_target_pairs={{0,4},{1,5},{2,6},{3,7},{4,0},{5,1},{6,2},{7,3},{8,12},{9,13},{10,... | collective-permute-start | bytes 393224 | tf_op jit(solution)/shard_map/ppermute | solution.py:256
  22.1 1.2 copy-done.1
  23.4 6.4 %factor_step.4.a_ref = f32[512,512]{1,0:T(8,128)S(1)} custom-call(f32[512,512]{1,0:T(8,128)S(1)} %copy-done.1), custom_call_target="tpu_custom_call" | custom-call | tf_op jit(solution)/shard_map/factor_step/pallas_call | solution.py:104
  29.8 4.8 %collective-permute-start.3 = (f32[2,32,1024]{2,1,0:T(8,128)S(1)}, f32[2,32,1024]{2,1,0:T(8,128)S(1)}, u32[]{:S(2)}, u32[]{:S(2)}) collective-permute-start(f32[2,32,1024]{2,1,0:T(8,128)S(1)} %pad_maximum_fusion.2), channel_id=1, source_target_pairs={{0,256},{1,257},{2,258},{3,259},{4,260},{5,261},{6,262},{7,263},{8... | collective-permute-start | bytes 786440 | tf_op jit(solution)/shard_map/ppermute | solution.py:261
  34.7 3.3 %collective-permute-start.6 = (f32[64,1024]{1,0:T(8,128)S(1)}, f32[64,1024]{1,0:T(8,128)S(1)}, u32[]{:S(2)}, u32[]{:S(2)}) collective-permute-start(f32[64,1024]{1,0:T(8,128)S(1)} %pad_maximum_fusion.3), channel_id=1, source_target_pairs={{0,2},{1,3},{2,0},{3,1},{4,6},{5,7},{6,4},{7,5},{8,10},{9,11},{10,... | collective-permute-start | bytes 786440 | tf_op jit(solution)/shard_map/ppermute | solution.py:263
  38.0 2.2 %collective-permute-done.3 = f32[2,32,1024]{2,1,0:T(8,128)S(1)} collective-permute-done((f32[2,32,1024]{2,1,0:T(8,128)S(1)}, f32[2,32,1024]{2,1,0:T(8,128)S(1)}, u32[]{:S(2)}, u32[]{:S(2)}) %collective-permute-start.3) | collective-permute-done | bytes 262176 | tf_op jit(solution)/shard_map/ppermute | solution.py:261
  40.2 2.9 %collective-permute-start.4 = (f32[4,32,1024]{2,1,0:T(8,128)S(1)}, f32[4,32,1024]{2,1,0:T(8,128)S(1)}, u32[]{:S(2)}, u32[]{:S(2)}) collective-permute-start(f32[4,32,1024]{2,1,0:T(8,128)S(1)} %constant_dynamic-update-slice_fusion.refs_0_), channel_id=1, source_target_pairs={{0,16},{16,32},{32,48},{48,64},{64,80},{80,96},{96,112},{112,128},... | collective-permute-start | bytes 1572872 | tf_op jit(solution)/shard_map/ppermute | solution.py:273
  43.1 5.7 %collective-permute-start.5 = (f32[4,32,1024]{2,1,0:T(8,128)S(1)}, f32[4,32,1024]{2,1,0:T(8,128)S(1)}, u32[]{:S(2)}, u32[]{:S(2)}) collective-permute-start(f32[4,32,1024]{2,1,0:T(8,128)S(1)} %constant_dynamic-update-slice_fusion.refs_0_), channel_id=1, source_target_pairs={{0,240},{16,0},{32,16},{48,32},{64,48},{80,64},{96,80},{112,96},{1... | collective-permute-start | bytes 1572872 | tf_op jit(solution)/shard_map/ppermute | solution.py:274
  48.9 6.1 %factor_step.5.a_ref = f32[512,512]{1,0:T(8,128)S(1)} custom-call(f32[512,512]{1,0:T(8,128)S(1)} %factor_step.4.a_ref), custom_call_target="tpu_custom_call" | custom-call | tf_op jit(solution)/shard_map/factor_step/pallas_call | solution.py:104
  55.0 2.1 %collective-permute-start.9 = (f32[128,1024]{1,0:T(8,128)S(1)}, f32[128,1024]{1,0:T(8,128)S(1)}, u32[]{:S(2)}, u32[]{:S(2)}) collective-permute-start(f32[128,1024]{1,0:T(8,128)S(1)} %pad_maximum_fusion.1), channel_id=1, source_target_pairs={{0,8},{1,9},{2,10},{3,11},{4,12},{5,13},{6,14},{7,15},{8,0},{9,1},... | collective-permute-start | bytes 1572872 | tf_op jit(solution)/shard_map/ppermute | solution.py:280
  57.1 1.6 %collective-permute-done.4.refs_1_ = f32[4,32,1024]{2,1,0:T(8,128)S(1)} collective-permute-done((f32[4,32,1024]{2,1,0:T(8,128)S(1)}, f32[4,32,1024]{2,1,0:T(8,128)S(1)}, u32[]{:S(2)}, u32[]{:S(2)}) %collective-permute-start.4) | collective-permute-done | bytes 524320 | tf_op jit(solution)/shard_map/ppermute | solution.py:273
  58.7 1.2 collective-permute-done.5.refs_2_
  59.8 6.0 %factor_step.6.a_ref = f32[512,512]{1,0:T(8,128)S(1)} custom-call(f32[512,512]{1,0:T(8,128)S(1)} %factor_step.5.a_ref), custom_call_target="tpu_custom_call" | custom-call | tf_op jit(solution)/shard_map/factor_step/pallas_call | solution.py:104
  65.8 4.3 %collective-permute-done.9 = f32[128,1024]{1,0:T(8,128)S(1)} collective-permute-done((f32[128,1024]{1,0:T(8,128)S(1)}, f32[128,1024]{1,0:T(8,128)S(1)}, u32[]{:S(2)}, u32[]{:S(2)}) %collective-permute-start.9) | collective-permute-done | bytes 524320 | tf_op jit(solution)/shard_map/ppermute | solution.py:280
  70.1 1.9 %collective-permute-start.7 = (f32[4,32,1024]{2,1,0:T(8,128)S(1)}, f32[4,32,1024]{2,1,0:T(8,128)S(1)}, u32[]{:S(2)}, u32[]{:S(2)}) collective-permute-start(f32[4,32,1024]{2,1,0:T(8,128)S(1)} %collective-permute-done.4.refs_1_), channel_id=1, source_target_pairs={{0,16},{16,32},{32,48},{48,64},{64,80},{80,96},{96,112},{112,128},... | collective-permute-start | bytes 1572872 | tf_op jit(solution)/shard_map/ppermute | solution.py:273
  72.0 13.3 %collective-permute-start.8 = (f32[4,32,1024]{2,1,0:T(8,128)S(1)}, f32[4,32,1024]{2,1,0:T(8,128)S(1)}, u32[]{:S(2)}, u32[]{:S(2)}) collective-permute-start(f32[4,32,1024]{2,1,0:T(8,128)S(1)} %collective-permute-done.5.refs_2_), channel_id=1, source_target_pairs={{0,240},{16,0},{32,16},{48,32},{64,48},{80,64},{96,80},{112,96},{1... | collective-permute-start | bytes 1572872 | tf_op jit(solution)/shard_map/ppermute | solution.py:274
  85.4 0.1 pad_maximum_fusion.panel_ref
  85.5 1.9 %collective-permute-start.12 = (f32[256,1024]{1,0:T(8,128)S(1)}, f32[256,1024]{1,0:T(8,128)S(1)}, u32[]{:S(2)}, u32[]{:S(2)}) collective-permute-start(f32[256,1024]{1,0:T(8,128)S(1)} %pad_maximum_fusion.panel_ref), channel_id=1, source_target_pairs={{0,1},{1,0},{2,3},{3,2},{4,5},{5,4},{6,7},{7,6},{8,9},{9,8},{10,11... | collective-permute-start | bytes 3145736 | tf_op jit(solution)/shard_map/ppermute | solution.py:280
  87.4 7.3 %collective-permute-done.7.refs_3_ = f32[4,32,1024]{2,1,0:T(8,128)S(1)} collective-permute-done((f32[4,32,1024]{2,1,0:T(8,128)S(1)}, f32[4,32,1024]{2,1,0:T(8,128)S(1)}, u32[]{:S(2)}, u32[]{:S(2)}) %collective-permute-start.7) | collective-permute-done | bytes 524320 | tf_op jit(solution)/shard_map/ppermute | solution.py:273
  94.7 1.2 collective-permute-done.8.refs_4_
  95.9 1.9 %collective-permute-start.10 = (f32[4,32,1024]{2,1,0:T(8,128)S(1)}, f32[4,32,1024]{2,1,0:T(8,128)S(1)}, u32[]{:S(2)}, u32[]{:S(2)}) collective-permute-start(f32[4,32,1024]{2,1,0:T(8,128)S(1)} %collective-permute-done.7.refs_3_), channel_id=1, source_target_pairs={{0,16},{16,32},{32,48},{48,64},{64,80},{80,96},{96,112},{112,128},... | collective-permute-start | bytes 1572872 | tf_op jit(solution)/shard_map/ppermute | solution.py:273
  97.8 5.6 %collective-permute-start.11 = (f32[4,32,1024]{2,1,0:T(8,128)S(1)}, f32[4,32,1024]{2,1,0:T(8,128)S(1)}, u32[]{:S(2)}, u32[]{:S(2)}) collective-permute-start(f32[4,32,1024]{2,1,0:T(8,128)S(1)} %collective-permute-done.8.refs_4_), channel_id=1, source_target_pairs={{0,240},{16,0},{32,16},{48,32},{64,48},{80,64},{96,80},{112,96},{1... | collective-permute-start | bytes 1572872 | tf_op jit(solution)/shard_map/ppermute | solution.py:274
  103.4 5.2 %factor_step.7.inverse_ref = f32[512,512]{1,0:T(8,128)S(1)} custom-call(f32[512,512]{1,0:T(8,128)S(1)} %factor_step.6.a_ref), custom_call_target="tpu_custom_call" | custom-call | tf_op jit(solution)/shard_map/factor_step/pallas_call | solution.py:104
  108.6 3.3 %collective-permute-done.10.refs_5_ = f32[4,32,1024]{2,1,0:T(8,128)S(1)} collective-permute-done((f32[4,32,1024]{2,1,0:T(8,128)S(1)}, f32[4,32,1024]{2,1,0:T(8,128)S(1)}, u32[]{:S(2)}, u32[]{:S(2)}) %collective-permute-start.10) | collective-permute-done | bytes 524320 | tf_op jit(solution)/shard_map/ppermute | solution.py:273
  111.9 1.2 collective-permute-done.11.refs_6_
  113.1 4.8 %collective-permute-start.13 = (f32[2,32,1024]{2,1,0:T(8,128)S(1)}, f32[2,32,1024]{2,1,0:T(8,128)S(1)}, u32[]{:S(2)}, u32[]{:S(2)}) collective-permute-start(f32[2,32,1024]{2,1,0:T(8,128)S(1)} %slice.6), channel_id=1, source_target_pairs={{0,16},{16,32},{32,48},{48,64},{64,80},{80,96},{96,112},{112,128},... | collective-permute-start | bytes 786440 | tf_op jit(solution)/shard_map/ppermute | solution.py:273
  117.9 3.1 %collective-permute-start.14 = (f32[2,32,1024]{2,1,0:T(8,128)S(1)}, f32[2,32,1024]{2,1,0:T(8,128)S(1)}, u32[]{:S(2)}, u32[]{:S(2)}) collective-permute-start(f32[2,32,1024]{2,1,0:T(8,128)S(1)} %slice.7), channel_id=1, source_target_pairs={{0,240},{16,0},{32,16},{48,32},{64,48},{80,64},{96,80},{112,96},{1... | collective-permute-start | bytes 786440 | tf_op jit(solution)/shard_map/ppermute | solution.py:274
  121.0 2.9 %own_rows.1 = (bf16[8,256,512]{2,1,0:T(8,128)(2,1)S(1)}, f32[32,1024]{1,0:T(8,128)}) custom-call(f32[512,512]{1,0:T(8,128)S(1)} %factor_step.7.inverse_ref, f32[256,1024]{1,0:T(8,128)S(1)} %pad_maximum_fusion.panel_ref, f32[256,1024]{1,0:T(8,128)S(1)} %collective-permute-done.12.partner_ref), custom_call_target="tpu_custom_call" | custom-call | tf_op jit(solution)/shard_map/own_rows/pallas_call | solution.py:309
  124.0 2.2 %collective-permute-done.14.refs_8_ = f32[2,32,1024]{2,1,0:T(8,128)S(1)} collective-permute-done((f32[2,32,1024]{2,1,0:T(8,128)S(1)}, f32[2,32,1024]{2,1,0:T(8,128)S(1)}, u32[]{:S(2)}, u32[]{:S(2)}) %collective-permute-start.14) | collective-permute-done | bytes 262176 | tf_op jit(solution)/shard_map/ppermute | solution.py:274
  126.2 5.5 %schur_tiles.1 = f32[28,128,128]{2,1,0:T(8,128)} custom-call(s32[2,28]{1,0:T(2,128)S(1)} %bitcast.5, f32[28,128,128]{2,1,0:T(8,128)S(1)} %copy-done, bf16[8,256,512]{2,1,0:T(8,128)(2,1)S(1)} %get-tuple-element.53.left, f32[4,32,1024]{2,1,0:T(8,128)S(1)} %constant_dynamic-update-slice_fusion.refs_0_, f32[4,32,1024]{2,1,0:T(8,128)S(1)} %collective-permute-done.4.refs_1_, ...), custom_call_target="tpu_custom_call" | custom-call | tf_op jit(solution)/shard_map/schur_tiles/pallas_call | solution.py:289
  (20 shorter events, 0.2 us)
Async XLA Ops:
  0.6 29.1 %collective-permute-start = (f32[32,1024]{1,0:T(8,128)}, f32[32,1024]{1,0:T(8,128)S(1)}, u32[]{:S(2)}, u32[]{:S(2)}) collective-permute-start(f32[32,1024]{1,0:T(8,128)} %bitcast.6), channel_id=1, source_target_pairs={{0,0},{1,240},{2,16},{3,224},{4,32},{5,208},{6,48},{7,192},{8,64},... | collective-permute-start | bytes 393224 | tf_op jit(solution)/shard_map/ppermute | solution.py:254
  7.1 22.7 %collective-permute-start.1 = (f32[32,1024]{1,0:T(8,128)}, f32[32,1024]{1,0:T(8,128)S(1)}, u32[]{:S(2)}, u32[]{:S(2)}) collective-permute-start(f32[32,1024]{1,0:T(8,128)} %bitcast.7), channel_id=1, source_target_pairs={{0,128},{1,112},{2,144},{3,96},{4,160},{5,80},{6,176},{7,64},{8,19... | collective-permute-start | bytes 393224 | tf_op jit(solution)/shard_map/ppermute | solution.py:255
  18.8 11.0 %collective-permute-start.2 = (f32[32,1024]{1,0:T(8,128)}, f32[32,1024]{1,0:T(8,128)S(1)}, u32[]{:S(2)}, u32[]{:S(2)}) collective-permute-start(f32[32,1024]{1,0:T(8,128)} %bitcast.8), channel_id=1, source_target_pairs={{0,4},{1,5},{2,6},{3,7},{4,0},{5,1},{6,2},{7,3},{8,12},{9,13},{10,... | collective-permute-start | bytes 393224 | tf_op jit(solution)/shard_map/ppermute | solution.py:256
  22.1 1.2 copy-start.1
  23.4 11.3 %copy-start.3 = (f32[1024,32]{0,1:T(8,128)S(1)}, f32[1024,32]{0,1:T(8,128)}, u32[]{:S(2)}) copy-start(f32[1024,32]{0,1:T(8,128)} %param.5) | copy-start | bytes 393220
  29.8 10.3 %collective-permute-start.3 = (f32[2,32,1024]{2,1,0:T(8,128)S(1)}, f32[2,32,1024]{2,1,0:T(8,128)S(1)}, u32[]{:S(2)}, u32[]{:S(2)}) collective-permute-start(f32[2,32,1024]{2,1,0:T(8,128)S(1)} %pad_maximum_fusion.2), channel_id=1, source_target_pairs={{0,256},{1,257},{2,258},{3,259},{4,260},{5,261},{6,262},{7,263},{8... | collective-permute-start | bytes 786440 | tf_op jit(solution)/shard_map/ppermute | solution.py:261
  34.7 20.2 %collective-permute-start.6 = (f32[64,1024]{1,0:T(8,128)S(1)}, f32[64,1024]{1,0:T(8,128)S(1)}, u32[]{:S(2)}, u32[]{:S(2)}) collective-permute-start(f32[64,1024]{1,0:T(8,128)S(1)} %pad_maximum_fusion.3), channel_id=1, source_target_pairs={{0,2},{1,3},{2,0},{3,1},{4,6},{5,7},{6,4},{7,5},{8,10},{9,11},{10,... | collective-permute-start | bytes 786440 | tf_op jit(solution)/shard_map/ppermute | solution.py:263
  40.2 18.5 %collective-permute-start.4 = (f32[4,32,1024]{2,1,0:T(8,128)S(1)}, f32[4,32,1024]{2,1,0:T(8,128)S(1)}, u32[]{:S(2)}, u32[]{:S(2)}) collective-permute-start(f32[4,32,1024]{2,1,0:T(8,128)S(1)} %constant_dynamic-update-slice_fusion.refs_0_), channel_id=1, source_target_pairs={{0,16},{16,32},{32,48},{48,64},{64,80},{80,96},{96,112},{112,128},... | collective-permute-start | bytes 1572872 | tf_op jit(solution)/shard_map/ppermute | solution.py:273
  43.1 16.7 %collective-permute-start.5 = (f32[4,32,1024]{2,1,0:T(8,128)S(1)}, f32[4,32,1024]{2,1,0:T(8,128)S(1)}, u32[]{:S(2)}, u32[]{:S(2)}) collective-permute-start(f32[4,32,1024]{2,1,0:T(8,128)S(1)} %constant_dynamic-update-slice_fusion.refs_0_), channel_id=1, source_target_pairs={{0,240},{16,0},{32,16},{48,32},{64,48},{80,64},{96,80},{112,96},{1... | collective-permute-start | bytes 1572872 | tf_op jit(solution)/shard_map/ppermute | solution.py:274
  55.0 15.1 %collective-permute-start.9 = (f32[128,1024]{1,0:T(8,128)S(1)}, f32[128,1024]{1,0:T(8,128)S(1)}, u32[]{:S(2)}, u32[]{:S(2)}) collective-permute-start(f32[128,1024]{1,0:T(8,128)S(1)} %pad_maximum_fusion.1), channel_id=1, source_target_pairs={{0,8},{1,9},{2,10},{3,11},{4,12},{5,13},{6,14},{7,15},{8,0},{9,1},... | collective-permute-start | bytes 1572872 | tf_op jit(solution)/shard_map/ppermute | solution.py:280
  70.1 24.6 %collective-permute-start.7 = (f32[4,32,1024]{2,1,0:T(8,128)S(1)}, f32[4,32,1024]{2,1,0:T(8,128)S(1)}, u32[]{:S(2)}, u32[]{:S(2)}) collective-permute-start(f32[4,32,1024]{2,1,0:T(8,128)S(1)} %collective-permute-done.4.refs_1_), channel_id=1, source_target_pairs={{0,16},{16,32},{32,48},{48,64},{64,80},{80,96},{96,112},{112,128},... | collective-permute-start | bytes 1572872 | tf_op jit(solution)/shard_map/ppermute | solution.py:273
  72.0 23.9 %collective-permute-start.8 = (f32[4,32,1024]{2,1,0:T(8,128)S(1)}, f32[4,32,1024]{2,1,0:T(8,128)S(1)}, u32[]{:S(2)}, u32[]{:S(2)}) collective-permute-start(f32[4,32,1024]{2,1,0:T(8,128)S(1)} %collective-permute-done.5.refs_2_), channel_id=1, source_target_pairs={{0,240},{16,0},{32,16},{48,32},{64,48},{80,64},{96,80},{112,96},{1... | collective-permute-start | bytes 1572872 | tf_op jit(solution)/shard_map/ppermute | solution.py:274
  85.5 23.2 %collective-permute-start.12 = (f32[256,1024]{1,0:T(8,128)S(1)}, f32[256,1024]{1,0:T(8,128)S(1)}, u32[]{:S(2)}, u32[]{:S(2)}) collective-permute-start(f32[256,1024]{1,0:T(8,128)S(1)} %pad_maximum_fusion.panel_ref), channel_id=1, source_target_pairs={{0,1},{1,0},{2,3},{3,2},{4,5},{5,4},{6,7},{7,6},{8,9},{9,8},{10,11... | collective-permute-start | bytes 3145736 | tf_op jit(solution)/shard_map/ppermute | solution.py:280
  95.9 16.0 %collective-permute-start.10 = (f32[4,32,1024]{2,1,0:T(8,128)S(1)}, f32[4,32,1024]{2,1,0:T(8,128)S(1)}, u32[]{:S(2)}, u32[]{:S(2)}) collective-permute-start(f32[4,32,1024]{2,1,0:T(8,128)S(1)} %collective-permute-done.7.refs_3_), channel_id=1, source_target_pairs={{0,16},{16,32},{32,48},{48,64},{64,80},{80,96},{96,112},{112,128},... | collective-permute-start | bytes 1572872 | tf_op jit(solution)/shard_map/ppermute | solution.py:273
  97.8 15.3 %collective-permute-start.11 = (f32[4,32,1024]{2,1,0:T(8,128)S(1)}, f32[4,32,1024]{2,1,0:T(8,128)S(1)}, u32[]{:S(2)}, u32[]{:S(2)}) collective-permute-start(f32[4,32,1024]{2,1,0:T(8,128)S(1)} %collective-permute-done.8.refs_4_), channel_id=1, source_target_pairs={{0,240},{16,0},{32,16},{48,32},{64,48},{80,64},{96,80},{112,96},{1... | collective-permute-start | bytes 1572872 | tf_op jit(solution)/shard_map/ppermute | solution.py:274
  113.1 13.1 %copy-start = (f32[28,128,128]{2,1,0:T(8,128)S(1)}, f32[28,128,128]{2,1,0:T(8,128)}, u32[]{:S(2)}) copy-start(f32[28,128,128]{2,1,0:T(8,128)} %tiles_hbm.1) | copy-start | bytes 5505028
  113.1 13.1 %copy-start.2 = (s32[28,2]{0,1:T(2,128)S(1)}, s32[28,2]{0,1:T(2,128)}, u32[]{:S(2)}) copy-start(s32[28,2]{0,1:T(2,128)} %param.7) | copy-start | bytes 676
  113.1 10.9 %collective-permute-start.13 = (f32[2,32,1024]{2,1,0:T(8,128)S(1)}, f32[2,32,1024]{2,1,0:T(8,128)S(1)}, u32[]{:S(2)}, u32[]{:S(2)}) collective-permute-start(f32[2,32,1024]{2,1,0:T(8,128)S(1)} %slice.6), channel_id=1, source_target_pairs={{0,16},{16,32},{32,48},{48,64},{64,80},{80,96},{96,112},{112,128},... | collective-permute-start | bytes 786440 | tf_op jit(solution)/shard_map/ppermute | solution.py:273
  117.9 8.3 %collective-permute-start.14 = (f32[2,32,1024]{2,1,0:T(8,128)S(1)}, f32[2,32,1024]{2,1,0:T(8,128)S(1)}, u32[]{:S(2)}, u32[]{:S(2)}) collective-permute-start(f32[2,32,1024]{2,1,0:T(8,128)S(1)} %slice.7), channel_id=1, source_target_pairs={{0,240},{16,0},{32,16},{48,32},{64,48},{80,64},{96,80},{112,96},{1... | collective-permute-start | bytes 786440 | tf_op jit(solution)/shard_map/ppermute | solution.py:274
